TPU v7x, 32 devices: a whole 2x2x4 slice. The times are simulated.
32 devices in a mesh: ctx: 4 (over z), rec: 8 (over y, x, core).
Axes of the slice: x: 2, y: 2, z: 4, core: 2. Of those that a mesh axis runs over, the one named last changes fastest.
Arguments:
- queries: bfloat16 [8, 1024, 1280], P('rec', 'ctx'), may hold values from -24 to 24
- video_keys: bfloat16 [8, 512, 1280], P('rec', 'ctx'), may hold values from -24 to 24
- video_values: bfloat16 [8, 512, 1280], P('rec', 'ctx'), may hold values from -6 to 6
- out_weight: bfloat16 [1280, 1280], replicated, may hold values from -0.15625 to 0.15625
- gate_logit: float32 [1], replicated, may hold values from 0.3 to 1.2
- row_grads: bfloat16 [16384, 1280], P(('ctx', 'rec')), may hold values from -6 to 6
- dest_device: int32 [16384], P(('ctx', 'rec')), may hold values from 0 to 31, as said below
- dest_row: int32 [16384], P(('ctx', 'rec')), may hold values from 0 to 255, as said below
- live_count: int32 [32], P(('ctx', 'rec')), may hold values from 0 to 512, as said below
Outputs:
- query_grads: bfloat16 [16384, 1280], P(('ctx', 'rec'))
- key_grads: bfloat16 [8, 512, 1280], P('rec', 'ctx')
- value_grads: bfloat16 [8, 512, 1280], P('rec', 'ctx')
- weight_grads: float32 [1280, 1280], P(('ctx', 'rec'))
- gate_grad: float32 [1], replicated
Inputs may be any that keep to these rules, and one draw needn't show every extreme that they name: `dest_device`: for the live slots of all devices together, each pair of owner device and audio row appears exactly once; the live slots of one device name one owner at most 16 times, and some device names each owner exactly 16 times. Slots that are not live hold 0. `dest_row`: slots that are not live hold 0. `live_count`: the live slots of a device are its first ones; the counts sum to 8192, and the largest is exactly 512.
All inputs are finite; a program needn't handle non-finite values.
Results may differ from a plain program's by a relative error of at most 0.012.
The roundings to bfloat16 on the way count: a program that leaves them out, or rounds other values in their place, can miss the bound.
Values may be sent and summed in bfloat16 or wider, within the bound.
No kernel may reach another device: no remote copies, remote signals or barrier semaphores. Data moves between devices by JAX's collectives and lax.ppermute only.
A program may use at most 192 MiB of HBM per device.

v0:
```python
import math

import jax
import jax.numpy as jnp
from jax import lax
from jax.sharding import PartitionSpec as P

HEADS = 20
HEAD_DIM = 64


def head_blocks(query_rows, keys_all, values_all, grad_attn):
    rows_q = query_rows.shape[0]
    rows_k = keys_all.shape[0]
    model_width = query_rows.shape[1]
    per_block = math.gcd(HEADS, 4)
    col_span = per_block * HEAD_DIM
    inv_root = HEAD_DIM ** (-0.5)
    attn_parts = []
    query_parts = []
    key_parts = []
    value_parts = []
    for block_idx in range(model_width // col_span):
        first_col = block_idx * col_span
        query_heads = query_rows[:, first_col : first_col + col_span].reshape(
            rows_q, per_block, HEAD_DIM
        )
        key_heads = keys_all[:, first_col : first_col + col_span].reshape(
            rows_k, per_block, HEAD_DIM
        )
        value_heads = values_all[:, first_col : first_col + col_span].reshape(
            rows_k, per_block, HEAD_DIM
        )
        grad_heads = grad_attn[:, first_col : first_col + col_span].reshape(
            rows_q, per_block, HEAD_DIM
        )
        scores = (
            jnp.einsum("ahd,vhd->hav", query_heads, key_heads, preferred_element_type=jnp.float32)
            * inv_root
        )
        row_peak = jnp.max(scores, axis=-1, keepdims=True)
        shifted = jnp.exp(scores - row_peak)
        softmax_w = shifted / jnp.sum(shifted, axis=-1, keepdims=True)
        probs_low = softmax_w.astype(jnp.bfloat16)
        attn_low = jnp.einsum(
            "hav,vhd->ahd", probs_low, value_heads, preferred_element_type=jnp.float32
        ).astype(jnp.bfloat16)
        row_delta = jnp.einsum(
            "ahd,ahd->ha", grad_heads, attn_low, preferred_element_type=jnp.float32
        )
        dprob = jnp.einsum(
            "ahd,vhd->hav", grad_heads, value_heads, preferred_element_type=jnp.float32
        )
        dscore = (softmax_w * (dprob - row_delta[:, :, None])).astype(jnp.bfloat16)
        query_part = (
            jnp.einsum("hav,vhd->ahd", dscore, key_heads, preferred_element_type=jnp.float32)
            * inv_root
        )
        key_part = (
            jnp.einsum("hav,ahd->vhd", dscore, query_heads, preferred_element_type=jnp.float32)
            * inv_root
        )
        value_part = jnp.einsum(
            "hav,ahd->vhd", probs_low, grad_heads, preferred_element_type=jnp.float32
        )
        attn_parts.append(attn_low.reshape(rows_q, col_span))
        query_parts.append(query_part.reshape(rows_q, col_span))
        key_parts.append(key_part.reshape(rows_k, col_span).astype(jnp.bfloat16))
        value_parts.append(value_part.reshape(rows_k, col_span).astype(jnp.bfloat16))
    return (
        jnp.concatenate(attn_parts, axis=1),
        jnp.concatenate(query_parts, axis=1),
        jnp.concatenate(key_parts, axis=1),
        jnp.concatenate(value_parts, axis=1),
    )


def local(
    queries,
    video_keys,
    video_values,
    out_weight,
    gate_logit,
    row_grads,
    dest_device,
    dest_row,
    live_count,
):
    ctx_count = lax.axis_size("ctx")
    rec_count = lax.axis_size("rec")
    all_count = ctx_count * rec_count
    slot_count = row_grads.shape[0]
    pair_cap = slot_count // all_count
    audio_rows = queries.shape[1]
    model_width = out_weight.shape[0]
    slot_ids = jnp.arange(slot_count, dtype=jnp.int32)
    is_live = slot_ids < live_count[0]
    owner_ids = jnp.arange(all_count, dtype=jnp.int32)
    owner_hot = jnp.logical_and(
        dest_device[:, None] == owner_ids[None, :], is_live[:, None]
    ).astype(jnp.bfloat16)
    earlier = (slot_ids[None, :] < slot_ids[:, None]).astype(jnp.bfloat16)
    before = jnp.dot(earlier, owner_hot, preferred_element_type=jnp.float32)
    bucket_rank = jnp.sum(before * owner_hot.astype(jnp.float32), axis=1).astype(jnp.int32)
    slot_target = jnp.where(is_live, dest_device * pair_cap + bucket_rank, slot_count)
    send_grads = (
        jnp.zeros((slot_count, model_width), jnp.bfloat16)
        .at[slot_target]
        .set(row_grads, mode="drop")
    )
    send_index = (
        jnp.full((slot_count,), audio_rows, jnp.int32).at[slot_target].set(dest_row, mode="drop")
    )
    recv_grads, recv_index = (
        lax.all_to_all(
            send_grads.reshape(all_count, pair_cap, model_width),
            ("ctx", "rec"),
            split_axis=0,
            concat_axis=0,
            tiled=True,
        ),
        lax.all_to_all(
            send_index.reshape(all_count, pair_cap),
            ("ctx", "rec"),
            split_axis=0,
            concat_axis=0,
            tiled=True,
        ),
    )
    recv_grads = recv_grads.reshape(slot_count, model_width)
    recv_index = recv_index.reshape(slot_count)
    grad_rows = (
        jnp.zeros((audio_rows + 1, model_width), jnp.bfloat16)
        .at[recv_index]
        .set(recv_grads)[:audio_rows]
    )
    keys_all, values_all = (
        lax.all_gather(video_keys, "ctx", axis=1, tiled=True),
        lax.all_gather(video_values, "ctx", axis=1, tiled=True),
    )
    gate_value = jnp.tanh(gate_logit[0])
    upstream = lax.dot_general(
        grad_rows, out_weight, (((1,), (1,)), ((), ())), preferred_element_type=jnp.float32
    )
    grad_attn = (gate_value * upstream).astype(jnp.bfloat16)
    attn_low, query_grad, key_term, value_term = head_blocks(
        queries[0], keys_all[0], values_all[0], grad_attn
    )
    key_sum, value_sum = (
        lax.psum_scatter(key_term[None], "ctx", scatter_dimension=1, tiled=True).astype(
            jnp.float32
        ),
        lax.psum_scatter(value_term[None], "ctx", scatter_dimension=1, tiled=True).astype(
            jnp.float32
        ),
    )
    weight_grad = lax.psum_scatter(
        gate_value
        * lax.dot_general(
            grad_rows, attn_low, (((0,), (0,)), ((), ())), preferred_element_type=jnp.float32
        ),
        ("ctx", "rec"),
        scatter_dimension=0,
        tiled=True,
    )
    shrink = 1.0 - gate_value * gate_value
    gate_total = lax.psum(jnp.sum(upstream * attn_low.astype(jnp.float32)), ("ctx", "rec"))
    gate_grad = shrink * gate_total
    padded_grad = jnp.concatenate(
        [query_grad.astype(jnp.bfloat16), jnp.zeros((1, model_width), jnp.bfloat16)], axis=0
    )
    back_rows = padded_grad[recv_index]
    returned = lax.all_to_all(
        back_rows.reshape(all_count, pair_cap, model_width),
        ("ctx", "rec"),
        split_axis=0,
        concat_axis=0,
        tiled=True,
    )
    returned = returned.reshape(slot_count, model_width)
    picked = returned[jnp.minimum(slot_target, slot_count - 1)]
    query_grads = jnp.where(is_live[:, None], picked, jnp.zeros((), jnp.bfloat16))
    return (
        query_grads,
        key_sum.astype(jnp.bfloat16),
        value_sum.astype(jnp.bfloat16),
        weight_grad,
        gate_grad.reshape(1),
    )


def solution(mesh):
    in_specs = (
        P("rec", "ctx", None),
        P("rec", "ctx", None),
        P("rec", "ctx", None),
        P(),
        P(),
        P(("ctx", "rec"), None),
        P(("ctx", "rec")),
        P(("ctx", "rec")),
        P(("ctx", "rec")),
    )
    out_specs = (
        P(("ctx", "rec"), None),
        P("rec", "ctx", None),
        P("rec", "ctx", None),
        P(("ctx", "rec"), None),
        P(),
    )
    return jax.shard_map(local, mesh=mesh, in_specs=in_specs, out_specs=out_specs, check_vma=False)
```

profile of v0, /device:TPU:0, one launch (start us, length us, event | category | flops | bytes accessed | tf_op | source)
XLA Modules:
  0.0 445.9 jit_solution(16039810445099604421)
XLA Ops:
  11.6 2.6 scatter_custom_fusion
  14.9 7.3 %all-to-all-start = ((s32[32,1,16]{2,1,0:T(1,128)}), s32[32,1,16]{2,1,0:T(1,128)S(1)}, u32[]{:S(2)}, u32[]{:S(2)}) async-start(s32[32,1,16]{2,1,0:T(1,128)} %bitcast.16), calls=%async_computation | async-start | bytes 32768 | tf_op jit(solution)/shard_map/all_to_all | solution.py:122
  31.3 4.7 %scatter_custom_fusion.1 = bf16[512,1280]{1,0:T(8,128)(2,1)} fusion(s32[512]{0:T(512)} %copy-done.28, bf16[512,1280]{1,0:T(8,128)(2,1)} %param.14, bf16[]{:T(256)} %constant.14.clone.1), kind=kCustom, calls=%fused_computation.82 | custom fusion | bytes 1311232 | tf_op jit(solution)/shard_map/scatter | solution.py:109
  36.0 5.9 %all-to-all-start.1 = ((bf16[32,16,1280]{2,1,0:T(8,128)(2,1)}), bf16[32,16,1280]{2,1,0:T(8,128)(2,1)}, u32[]{:S(2)}, u32[]{:S(2)}) async-start(bf16[32,16,1280]{2,1,0:T(8,128)(2,1)} %bitcast.197), calls=%async_computation.1 | async-start | bytes 2621440 | tf_op jit(solution)/shard_map/all_to_all | solution.py:115
  49.5 45.7 %all-gather.5.cloned.1.call-done = bf16[1,512,1280]{2,1,0:T(8,128)(2,1)} async-done(((bf16[1,128,1280]{2,1,0:T(8,128)(2,1)}), bf16[1,512,1280]{2,1,0:T(8,128)(2,1)}) %all-gather.5.cloned.1.call-update) | async-done | bytes 1310736 | tf_op jit(solution)/shard_map/all_gather | solution.py:139
  95.2 2.4 fusion.66
  112.8 3.2 fusion.69
  120.0 3.1 fusion.70
  127.2 3.2 fusion.71
  135.9 3.8 fusion.72
  145.3 3.8 fusion.73
  162.7 4.3 scatter_custom_fusion.2
  167.0 3.0 multiply_reduce_fusion.5
  250.3 5.1 %convolution_multiply_fusion = f32[1280,1280]{1,0:T(8,128)} fusion(bf16[256,1280]{1,0:T(8,128)(2,1)} %constant_dynamic-update-slice_fusion.15, f32[]{:T(128)} %bitcast.15, bf16[257,1280]{1,0:T(8,128)(2,1)} %scatter_custom_fusion.2), kind=kOutput, calls=%fused_computation.10 | convolution fusion | flops 840499200 | bytes 7864832 | tf_op jit(solution)/shard_map/dot_general | solution.py:159
  256.3 2.3 fusion.19
  260.3 2.5 fusion.18
  264.5 2.4 fusion.17
  268.5 2.4 fusion.16
  280.5 5.1 %gather_fusion = bf16[512,1280]{1,0:T(8,128)(2,1)} fusion(bf16[257,1280]{1,0:T(8,128)(2,1)} %concatenate.17, s32[1024]{0:T(1024)S(1)} %pad_clamp_fusion.1), kind=kCustom, calls=%fused_computation | custom fusion | bytes 2623488 | tf_op jit(solution)/shard_map/gather | solution.py:172
  285.6 3.8 all-to-all-start.2
  289.5 59.1 %psum.7 = f32[]{:T(128)} all-reduce(f32[]{:T(128)} %get-tuple-element.5), channel_id=1, replica_groups=mesh['ctx'=4,'rec'=8] {'ctx','rec'}, use_global_device_ids=true, to_apply=%region_18.19 | all-reduce | flops 1 | bytes 8 | tf_op jit(solution)/shard_map/psum | solution.py:167
  349.2 5.4 %gather_fusion.1 = bf16[512,1280]{1,0:T(8,128)(2,1)} fusion(bf16[512,1280]{1,0:T(8,128)(2,1)} %bitcast.70, s32[1024]{0:T(1024)S(1)} %pad_clamp_fusion), kind=kCustom, calls=%fused_computation.1 | custom fusion | bytes 2623488 | tf_op jit(solution)/shard_map/gather | solution.py:181
  354.7 2.5 broadcast_select_fusion
  357.2 81.1 %reduce-scatter.8.cloned.1.call-done = f32[40,1280]{1,0:T(8,128)} async-done(((f32[1280,1280]{1,0:T(8,128)}), f32[40,1280]{1,0:T(8,128)}) %reduce-scatter.8.cloned.1.call-update) | async-done | bytes 204816 | tf_op jit(solution)/shard_map/reduce_scatter | solution.py:157
  (183 shorter events, 164.1 us)
Async XLA Ops:
  7.2 159.8 %copy-start = (bf16[1280,1280]{1,0:T(8,128)(2,1)S(1)}, bf16[1280,1280]{1,0:T(8,128)(2,1)}, u32[]{:S(2)}) copy-start(bf16[1280,1280]{1,0:T(8,128)(2,1)} %param.12) | copy-start | bytes 9830404
  7.2 38.3 %all-gather.3.cloned.1.call-start = ((), (), s32[]{:S(2)}) async-start(), calls=%async_computation.6 | async-start | bytes 1638400 | tf_op jit(solution)/shard_map/all_gather | solution.py:138
  7.9 87.3 %all-gather.5.cloned.1.call-start = ((), (), s32[]{:S(2)}) async-start(), calls=%async_computation.7 | async-start | bytes 1638400 | tf_op jit(solution)/shard_map/all_gather | solution.py:139
  11.6 10.6 %copy-start.28 = (s32[512]{0:T(512)}, s32[512]{0:T(512)S(1)}, u32[]{:S(2)}) copy-start(s32[512]{0:T(512)S(1)} %get-tuple-element.28) | copy-start | bytes 6148
  14.9 21.1 %all-to-all-start = ((s32[32,1,16]{2,1,0:T(1,128)}), s32[32,1,16]{2,1,0:T(1,128)S(1)}, u32[]{:S(2)}, u32[]{:S(2)}) async-start(s32[32,1,16]{2,1,0:T(1,128)} %bitcast.16), calls=%async_computation | async-start | bytes 32768 | tf_op jit(solution)/shard_map/all_to_all | solution.py:122
  36.0 126.7 %all-to-all-start.1 = ((bf16[32,16,1280]{2,1,0:T(8,128)(2,1)}), bf16[32,16,1280]{2,1,0:T(8,128)(2,1)}, u32[]{:S(2)}, u32[]{:S(2)}) async-start(bf16[32,16,1280]{2,1,0:T(8,128)(2,1)} %bitcast.197), calls=%async_computation.1 | async-start | bytes 2621440 | tf_op jit(solution)/shard_map/all_to_all | solution.py:115
  41.9 315.2 %reduce-scatter.6.cloned.1.call-start = ((), (), s32[]{:S(2)}) async-start(), calls=%async_computation.9 | async-start | bytes 1638400 | tf_op jit(solution)/shard_map/reduce_scatter | solution.py:153
  116.0 2.9 copy-start.16
  116.0 4.1 copy-start.22
  123.1 2.9 copy-start.17
  175.8 3.3 copy-start.26
  188.6 3.4 copy-start.25
  215.5 7.0 %copy-start.13 = (bf16[512,256]{1,0:T(8,128)(2,1)S(1)}, bf16[512,256]{1,0:T(8,128)(2,1)}, u32[]{:S(2)}) copy-start(bf16[512,256]{1,0:T(8,128)(2,1)} %copy.134) | copy-start | bytes 786436
  223.2 134.0 %reduce-scatter.4.cloned.1.call-start = ((), (), s32[]{:S(2)}) async-start(), calls=%async_computation.8 | async-start | bytes 1638400 | tf_op jit(solution)/shard_map/reduce_scatter | solution.py:150
  223.3 3.3 copy-start.24
  230.3 3.4 copy-start.23
  230.3 6.2 %copy-start.11 = (bf16[256,256]{0,1:T(8,128)(2,1)S(1)}, bf16[256,256]{0,1:T(8,128)(2,1)}, u32[]{:S(2)}) copy-start(bf16[256,256]{0,1:T(8,128)(2,1)} %copy.102) | copy-start | bytes 393220
  236.5 3.2 copy-start.21
  239.7 9.7 %copy-start.12 = (bf16[512,256]{1,0:T(8,128)(2,1)S(1)}, bf16[512,256]{1,0:T(8,128)(2,1)}, u32[]{:S(2)}) copy-start(bf16[512,256]{1,0:T(8,128)(2,1)} %copy.129) | copy-start | bytes 786436
  250.2 188.1 %reduce-scatter.8.cloned.1.call-start = ((), (), s32[]{:S(2)}) async-start(), calls=%async_computation.10 | async-start | bytes 6758400 | tf_op jit(solution)/shard_map/reduce_scatter | solution.py:157
  262.8 9.7 %copy-start.15 = (bf16[512,256]{0,1:T(8,128)(2,1)S(1)}, bf16[512,256]{0,1:T(8,128)(2,1)}, u32[]{:S(2)}) copy-start(bf16[512,256]{0,1:T(8,128)(2,1)} %copy.100) | copy-start | bytes 786436
  285.6 3.9 copy-start.27
  285.6 63.6 %all-to-all-start.2 = ((bf16[32,16,1280]{2,1,0:T(8,128)(2,1)}), bf16[32,16,1280]{2,1,0:T(8,128)(2,1)}, u32[]{:S(2)}, u32[]{:S(2)}) async-start(bf16[32,16,1280]{2,1,0:T(8,128)(2,1)} %bitcast.196), calls=%async_computation.2 | async-start | bytes 2621440 | tf_op jit(solution)/shard_map/all_to_all | solution.py:173
  349.2 5.4 %copy-start.30 = (pred[512]{0:T(512)(128)(4,1)S(1)}, pred[512]{0:T(512)(128)(4,1)}, u32[]{:S(2)}) copy-start(pred[512]{0:T(512)(128)(4,1)} %copy-done.29) | copy-start | bytes 1540
  (15 other events, 21.8 us)
Sparse Core Ops, SparseCore 0:
  9.6 35.8 all-gather.2
  47.0 48.1 all-gather.4
  223.3 30.4 reduce-scatter.5
  256.5 29.9 reduce-scatter.3
  289.3 148.9 reduce-scatter.7
where the time goes:
time: 449 us; the launch traced here: 446 us
  local copies, waits for them, and re-layouts  134 us (30%)
  waiting for transfers between devices  130 us (29%)
  matrix products  70 us (16%)
  blocking collectives  59.1 us (13%)
  other arithmetic  18.4 us (4%)
  starting transfers between devices  17.5 us (4%)
  between operations  17.3 us (4%)
    reduce_scatter x1, waiting for transfers between devices, local(): lax.psum_scatter(gate_value * lax.dot_general(grad_rows, attn_low, (((0,)...  81.1 us
    psum x1, blocking collectives, local(): lax.psum(jnp.sum(upstream * attn_low.astype(jnp.float32)), ('ctx', 'rec'))  59.1 us
    all_gather x1, waiting for transfers between devices, local(): lax.all_gather(video_values, 'ctx', axis=1, tiled=True)  45.7 us
    unnamed x78, local copies, waits for them, and re-layouts  33.9 us
    sub x5, matrix products, head_blocks(): shifted = jnp.exp(scores - row_peak)  17 us
    dot_general x5, matrix products, head_blocks(): jnp.einsum('hav,vhd->ahd', dscore, key_heads, preferred_element_type=jnp....  11.9 us
    dot_general x5, matrix products, head_blocks(): jnp.einsum('hav,ahd->vhd', probs_low, grad_heads, preferred_element_type=...  11.5 us
    dot_general x5, matrix products, head_blocks(): jnp.einsum('ahd,vhd->hav', grad_heads, value_heads, preferred_element_typ...  11.4 us
  transfers between devices with their start and end apart: 8, of which 3 were waited for; matrix products, arithmetic and copies ran while one was open for 34% of the time, Pallas kernels for 0%

commit v1 on v0

v1 whole, which is shorter than its diff:
```python
import jax
import jax.numpy as jnp
from jax import lax
from jax.experimental import pallas as pl
from jax.experimental.pallas import tpu as pltpu
from jax.sharding import PartitionSpec as P

HEAD_DIM = 64
LANES = 128
VMEM_LIMIT = 48 * 1024 * 1024
NT = (((1,), (1,)), ((), ()))
NN = (((1,), (0,)), ((), ()))


def mm(left, right, dims=NN):
    return lax.dot_general(left, right, dims, preferred_element_type=jnp.float32)


def iota(shape, dim):
    return lax.broadcasted_iota(jnp.int32, shape, dim)


def params():
    return pltpu.CompilerParams(vmem_limit_bytes=VMEM_LIMIT)


def as_column(row_vector):
    wide = jnp.broadcast_to(row_vector, (LANES, row_vector.shape[1]))
    return jnp.transpose(wide)[:, :1]


def as_row(column_block):
    return jnp.transpose(column_block.astype(jnp.float32))[:1, :]


def prep_kernel(pair_cap, owners, live_ref, dest_ref, row_ref, grads_ref, send_ref, target_ref):
    slots, width = grads_ref.shape
    slot = iota((1, slots), 1)
    is_live = slot < live_ref[0]
    dest = dest_ref[...]
    hot = jnp.logical_and(iota((owners, slots), 0) == dest, is_live)
    hot_f = jnp.where(hot, 1.0, 0.0)
    earlier = jnp.where(iota((slots, slots), 0) < iota((slots, slots), 1), 1.0, 0.0)
    before = mm(hot_f.astype(jnp.bfloat16), earlier.astype(jnp.bfloat16))
    rank = jnp.sum(hot_f * before, axis=0, keepdims=True).astype(jnp.int32)
    target = jnp.where(is_live, dest * pair_cap + rank, slots)
    target_ref[...] = target
    chosen = iota((slots, slots), 0) == target
    place = jnp.where(chosen, 1.0, 0.0).astype(jnp.bfloat16)
    send_ref[:, :width] = mm(place, grads_ref[...]).astype(jnp.bfloat16)
    row_no = (row_ref[...] + 1).astype(jnp.float32)
    index = jnp.sum(jnp.where(chosen, row_no, 0.0), axis=1, keepdims=True)
    send_ref[:, width:] = jnp.broadcast_to(index, (slots, LANES)).astype(jnp.bfloat16)


def route_prep(live_count, dest_device, dest_row, row_grads, owners):
    slots, width = row_grads.shape
    kernel = lambda *refs: prep_kernel(slots // owners, owners, *refs)
    vmem = pl.BlockSpec(memory_space=pltpu.VMEM)
    return pl.pallas_call(
        kernel,
        out_shape=(
            jax.ShapeDtypeStruct((slots, width + LANES), jnp.bfloat16),
            jax.ShapeDtypeStruct((1, slots), jnp.int32),
        ),
        in_specs=[pl.BlockSpec(memory_space=pltpu.SMEM), vmem, vmem, vmem],
        out_specs=(vmem, vmem),
        compiler_params=params(),
        name="route_prep",
        cost_estimate=pl.CostEstimate(
            flops=2 * slots * slots * width,
            bytes_accessed=4 * slots * width,
            transcendentals=0,
        ),
    )(live_count, dest_device.reshape(1, slots), dest_row.reshape(1, slots), row_grads)


def head_masks(shape, dim):
    first = iota(shape, dim) < HEAD_DIM
    return first, jnp.logical_not(first)


def keep(mask, value):
    return jnp.where(mask, value, jnp.zeros((), value.dtype))


def forward_kernel(query_ref, key_ref, value_ref, attn_ref, stat_ref):
    rows = query_ref.shape[0]
    query = query_ref[...] * jnp.asarray(HEAD_DIM ** -0.5, jnp.bfloat16)
    keys = key_ref[...]
    values_tr = jnp.transpose(value_ref[...])
    for head, mask in enumerate(head_masks((rows, LANES), 1)):
        scores = mm(keys, keep(mask, query), NT)
        peak = jnp.max(scores, axis=0, keepdims=True)
        shifted = jnp.exp(scores - peak)
        inverse = 1.0 / jnp.sum(shifted, axis=0, keepdims=True)
        probs_low = (shifted * inverse).astype(jnp.bfloat16)
        span = slice(head * HEAD_DIM, (head + 1) * HEAD_DIM)
        attn_ref[span, :] = mm(values_tr[span, :], probs_low).astype(jnp.bfloat16)
        stat_ref[0, head : head + 1, :] = peak
        stat_ref[0, head + 2 : head + 3, :] = inverse


def attention_forward(queries, keys, values):
    rows, width = queries.shape
    tokens = keys.shape[0]
    pairs = width // LANES
    columns = lambda i: (0, i)
    return pl.pallas_call(
        forward_kernel,
        grid=(pairs,),
        out_shape=(
            jax.ShapeDtypeStruct((width, rows), jnp.bfloat16),
            jax.ShapeDtypeStruct((pairs, 8, rows), jnp.float32),
        ),
        in_specs=[
            pl.BlockSpec((rows, LANES), columns),
            pl.BlockSpec((tokens, LANES), columns),
            pl.BlockSpec((tokens, LANES), columns),
        ],
        out_specs=(
            pl.BlockSpec((LANES, rows), lambda i: (i, 0)),
            pl.BlockSpec((1, 8, rows), lambda i: (i, 0, 0)),
        ),
        compiler_params=params(),
        name="attention_forward",
        cost_estimate=pl.CostEstimate(
            flops=16 * rows * tokens * width,
            bytes_accessed=4 * tokens * width + 4 * rows * width,
            transcendentals=rows * tokens * width // HEAD_DIM,
        ),
    )(queries, keys, values)


def grads_kernel(
    gate_ref, recv_ref, weight_ref, attn_blk_ref, attn_ref,
    grad_t_ref, grad_ref, gate_out_ref, weight_out_ref, rows_ref, rows_t_ref,
):
    step = pl.program_id(0)
    slots = recv_ref.shape[0]
    rows, width = rows_ref.shape

    @pl.when(step == 0)
    def _():
        index = as_row(recv_ref[:, width:])
        place = index == (iota((rows, slots), 0) + 1).astype(jnp.float32)
        place = jnp.where(place, 1.0, 0.0).astype(jnp.bfloat16)
        owned = mm(place, recv_ref[:, :width]).astype(jnp.bfloat16)
        rows_ref[...] = owned
        rows_t_ref[...] = jnp.transpose(owned)
        gate_out_ref[...] = jnp.zeros_like(gate_out_ref)

    gate = jnp.tanh(jnp.full((1, LANES), gate_ref[0], jnp.float32))[:, :1]
    upstream = mm(weight_ref[...], rows_ref[...], NT)
    grad_t = (gate * upstream).astype(jnp.bfloat16)
    grad_t_ref[...] = grad_t
    grad_ref[...] = jnp.transpose(grad_t)
    product = upstream * attn_blk_ref[...].astype(jnp.float32)
    gate_out_ref[...] += jnp.sum(product, axis=0, keepdims=True)
    first = pl.multiple_of(step * LANES, LANES)
    block = mm(rows_t_ref[pl.ds(first, LANES), :], attn_ref[...], NT)
    weight_out_ref[...] = (gate * block).astype(jnp.bfloat16)


def output_grads(gate_logit, recv, out_weight, attn_t):
    slots = recv.shape[0]
    width, rows = attn_t.shape
    blocks = width // LANES
    whole = lambda i: (0, 0)
    down = lambda i: (i, 0)
    return pl.pallas_call(
        grads_kernel,
        grid=(blocks,),
        out_shape=(
            jax.ShapeDtypeStruct((width, rows), jnp.bfloat16),
            jax.ShapeDtypeStruct((rows, width), jnp.bfloat16),
            jax.ShapeDtypeStruct((1, rows), jnp.float32),
            jax.ShapeDtypeStruct((width, width), jnp.bfloat16),
        ),
        in_specs=[
            pl.BlockSpec(memory_space=pltpu.SMEM),
            pl.BlockSpec((slots, width + LANES), whole),
            pl.BlockSpec((LANES, width), down),
            pl.BlockSpec((LANES, rows), down),
            pl.BlockSpec((width, rows), whole),
        ],
        out_specs=(
            pl.BlockSpec((LANES, rows), down),
            pl.BlockSpec((rows, LANES), lambda i: (0, i)),
            pl.BlockSpec((1, rows), whole),
            pl.BlockSpec((LANES, width), down),
        ),
        scratch_shapes=[
            pltpu.VMEM((rows, width), jnp.bfloat16),
            pltpu.VMEM((width, rows), jnp.bfloat16),
        ],
        compiler_params=params(),
        name="output_grads",
        cost_estimate=pl.CostEstimate(
            flops=4 * rows * width * width + 2 * slots * rows * width,
            bytes_accessed=4 * width * width + 8 * rows * width,
            transcendentals=0,
        ),
    )(gate_logit, recv, out_weight, attn_t, attn_t)


def backward_kernel(
    query_ref, key_ref, value_ref, grad_ref, grad_t_ref, attn_ref, stat_ref, index_ref,
    key_out_ref, value_out_ref, back_ref,
):
    rows = query_ref.shape[0]
    slots = index_ref.shape[0]
    root = jnp.asarray(HEAD_DIM ** -0.5, jnp.bfloat16)
    query = query_ref[...] * root
    keys = key_ref[...]
    values = value_ref[...]
    keys_tr = jnp.transpose(keys)
    grad = grad_ref[...]
    grad_t = grad_t_ref[...]
    lane_masks = head_masks((rows, LANES), 1)
    row_masks = head_masks((LANES, rows), 0)
    key_term = None
    value_term = None
    query_parts = []
    for head in range(2):
        span = slice(head * HEAD_DIM, (head + 1) * HEAD_DIM)
        query_h = keep(lane_masks[head], query)
        grad_h = keep(lane_masks[head], grad)
        scores = mm(keys, query_h, NT)
        peak = stat_ref[0, head : head + 1, :]
        inverse = stat_ref[0, head + 2 : head + 3, :]
        probs = jnp.exp(scores - peak) * inverse
        probs_low = probs.astype(jnp.bfloat16)
        delta = jnp.sum(
            grad_t_ref[span, :].astype(jnp.float32) * attn_ref[span, :].astype(jnp.float32),
            axis=0,
            keepdims=True,
        )
        dprob = mm(values, keep(row_masks[head], grad_t))
        dscore = (probs * (dprob - delta)).astype(jnp.bfloat16)
        value_part = mm(probs_low, grad_h)
        key_part = mm(dscore, query_h)
        value_term = value_part if head == 0 else value_term + value_part
        key_term = key_part if head == 0 else key_term + key_part
        query_parts.append(mm(keys_tr[span, :], dscore) * (HEAD_DIM ** -0.5))
    key_out_ref[...] = key_term.astype(jnp.bfloat16)
    value_out_ref[...] = value_term.astype(jnp.bfloat16)
    query_grad = jnp.transpose(jnp.concatenate(query_parts, axis=0).astype(jnp.bfloat16))
    index = index_ref[...][:, :1].astype(jnp.float32)
    place = index == (iota((slots, rows), 1) + 1).astype(jnp.float32)
    place = jnp.where(place, 1.0, 0.0).astype(jnp.bfloat16)
    back_ref[...] = mm(place, query_grad).astype(jnp.bfloat16)


def attention_backward(queries, keys, values, grad, grad_t, attn_t, stats, recv):
    rows, width = queries.shape
    tokens = keys.shape[0]
    slots = recv.shape[0]
    pairs = width // LANES
    columns = lambda i: (0, i)
    down = lambda i: (i, 0)
    return pl.pallas_call(
        backward_kernel,
        grid=(pairs,),
        out_shape=(
            jax.ShapeDtypeStruct((tokens, width), jnp.bfloat16),
            jax.ShapeDtypeStruct((tokens, width), jnp.bfloat16),
            jax.ShapeDtypeStruct((slots, width), jnp.bfloat16),
        ),
        in_specs=[
            pl.BlockSpec((rows, LANES), columns),
            pl.BlockSpec((tokens, LANES), columns),
            pl.BlockSpec((tokens, LANES), columns),
            pl.BlockSpec((rows, LANES), columns),
            pl.BlockSpec((LANES, rows), down),
            pl.BlockSpec((LANES, rows), down),
            pl.BlockSpec((1, 8, rows), lambda i: (i, 0, 0)),
            pl.BlockSpec((slots, LANES), lambda i: (0, width // LANES)),
        ],
        out_specs=(
            pl.BlockSpec((tokens, LANES), columns),
            pl.BlockSpec((tokens, LANES), columns),
            pl.BlockSpec((slots, LANES), columns),
        ),
        compiler_params=params(),
        name="attention_backward",
        cost_estimate=pl.CostEstimate(
            flops=40 * rows * tokens * width,
            bytes_accessed=8 * tokens * width + 12 * rows * width,
            transcendentals=rows * tokens * width // HEAD_DIM,
        ),
    )(queries, keys, values, grad, grad_t, attn_t, stats, recv)


def pick_kernel(target_ref, returned_ref, out_ref):
    slots = out_ref.shape[0]
    target = as_column(target_ref[...].astype(jnp.float32))
    place = target == iota((slots, slots), 1).astype(jnp.float32)
    place = jnp.where(place, 1.0, 0.0).astype(jnp.bfloat16)
    out_ref[...] = mm(place, returned_ref[...]).astype(jnp.bfloat16)


def pick_rows(target, returned):
    slots, width = returned.shape
    vmem = pl.BlockSpec(memory_space=pltpu.VMEM)
    return pl.pallas_call(
        pick_kernel,
        out_shape=jax.ShapeDtypeStruct((slots, width), jnp.bfloat16),
        in_specs=[vmem, vmem],
        out_specs=vmem,
        compiler_params=params(),
        name="pick_rows",
        cost_estimate=pl.CostEstimate(
            flops=2 * slots * slots * width,
            bytes_accessed=4 * slots * width,
            transcendentals=0,
        ),
    )(target, returned)


def shift(value, step):
    count = lax.axis_size("ctx")
    pairs = [(i, (i + step) % count) for i in range(count)]
    return lax.ppermute(value, "ctx", pairs)


def gather_ring(chunk):
    count = lax.axis_size("ctx")
    parts = [chunk]
    ahead = behind = chunk
    half = chunk.shape[0] // 2
    for step in range(1, count // 2 + 1):
        if 2 * step == count:
            if count == 2:
                parts.append(shift(chunk, 1))
            else:
                parts.append(shift(ahead[:half], 1))
                parts.append(shift(behind[half:], -1))
        else:
            ahead = shift(ahead, 1)
            behind = shift(behind, -1)
            parts.append(ahead)
            parts.append(behind)
    return jnp.concatenate(parts, axis=0)


def add(left, right):
    return (left.astype(jnp.float32) + right.astype(jnp.float32)).astype(jnp.bfloat16)


def scatter_ring(terms):
    count = lax.axis_size("ctx")
    rows = terms.shape[0] // count
    half = rows // 2
    take = lambda part: terms[part * rows : (part + 1) * rows]
    from_ahead = from_behind = None
    for step in range(count // 2, 0, -1):
        if 2 * step == count:
            last = take(count - 1)
            from_ahead = shift(last[:half], -1)
            from_behind = shift(last[half:], 1)
            continue
        back = take(2 * step - 1)
        forth = take(2 * step)
        if 2 * step == count - 2:
            back = jnp.concatenate([add(back[:half], from_ahead), back[half:]], axis=0)
            forth = jnp.concatenate([forth[:half], add(forth[half:], from_behind)], axis=0)
        else:
            back = add(back, from_ahead)
            forth = add(forth, from_behind)
        from_ahead = shift(back, -1)
        from_behind = shift(forth, 1)
    own = take(0).astype(jnp.float32)
    total = own + from_ahead.astype(jnp.float32) + from_behind.astype(jnp.float32)
    return total.astype(jnp.bfloat16)


def scatter_weight(term):
    ctx_count = lax.axis_size("ctx")
    rec_count = lax.axis_size("rec")
    width = term.shape[1]
    rows = term.shape[0] // (ctx_count * rec_count)
    rec = lax.axis_index("rec")
    left = rec_count
    bit = 0
    while left > 1:
        left //= 2
        term = term.reshape(ctx_count, left, 2, rows, width)
        mine = (rec >> bit) & 1
        sent = lax.dynamic_index_in_dim(term, 1 - mine, 2, keepdims=False)
        kept = lax.dynamic_index_in_dim(term, mine, 2, keepdims=False)
        got = lax.ppermute(sent, "rec", [(i, i ^ (1 << bit)) for i in range(rec_count)])
        term = add(kept, got)
        bit += 1
    term = term.reshape(ctx_count, rows, width)
    parts = lax.all_to_all(term, "ctx", split_axis=0, concat_axis=0, tiled=True)
    return jnp.sum(parts.astype(jnp.float32), axis=0)


def exchange(value, count):
    slots, width = value.shape
    moved = lax.all_to_all(
        value.reshape(count, slots // count, width),
        ("ctx", "rec"),
        split_axis=0,
        concat_axis=0,
        tiled=True,
    )
    return moved.reshape(slots, width)


def local(
    queries,
    video_keys,
    video_values,
    out_weight,
    gate_logit,
    row_grads,
    dest_device,
    dest_row,
    live_count,
):
    count = lax.axis_size("ctx") * lax.axis_size("rec")
    keys = gather_ring(video_keys[0])
    values = gather_ring(video_values[0])
    send, target = route_prep(live_count, dest_device, dest_row, row_grads, count)
    recv = exchange(send, count)
    attn_t, stats = attention_forward(queries[0], keys, values)
    grad_t, grad, gate_part, weight_term = output_grads(gate_logit, recv, out_weight, attn_t)
    weight_grad = scatter_weight(weight_term)
    key_term, value_term, back = attention_backward(
        queries[0], keys, values, grad, grad_t, attn_t, stats, recv
    )
    key_sum = scatter_ring(key_term)
    value_sum = scatter_ring(value_term)
    gate_row = jnp.broadcast_to(jnp.sum(gate_part), (count, 1, LANES))
    gate_parts = lax.all_to_all(
        gate_row, ("ctx", "rec"), split_axis=0, concat_axis=0, tiled=True
    )
    gate_total = jnp.sum(gate_parts[:, 0, 0])
    gate_value = jnp.tanh(gate_logit[0])
    gate_grad = (1.0 - gate_value * gate_value) * gate_total
    query_grads = pick_rows(target, exchange(back, count))
    return query_grads, key_sum[None], value_sum[None], weight_grad, gate_grad.reshape(1)


def solution(mesh):
    in_specs = (
        P("rec", "ctx", None),
        P("rec", "ctx", None),
        P("rec", "ctx", None),
        P(),
        P(),
        P(("ctx", "rec"), None),
        P(("ctx", "rec")),
        P(("ctx", "rec")),
        P(("ctx", "rec")),
    )
    out_specs = (
        P(("ctx", "rec"), None),
        P("rec", "ctx", None),
        P("rec", "ctx", None),
        P(("ctx", "rec"), None),
        P(),
    )
    return jax.shard_map(local, mesh=mesh, in_specs=in_specs, out_specs=out_specs, check_vma=False)
```

time: 449 us -> 212 us (0.47)
  local copies, waits for them, and re-layouts: 134 us -> 18.9 us
  matrix products: 70 us -> 0 us
  blocking collectives: 59.1 us -> 0 us
  waiting for transfers between devices: 130 us -> 71.3 us
  starting transfers between devices: 17.5 us -> 61.9 us
  Pallas kernels: 0 us -> 40.4 us
  between operations: 17.3 us -> 3.98 us
    reduce_scatter x3 -> x0, waiting for transfers between devices: 81.1 us -> none  [the longest x1 81.1 us: local(): lax.psum_scatter(gate_value * lax.dot_general(grad_rows, attn_low, (((0,)...]
    ppermute x0 -> x19, waiting for transfers between devices: none -> 59.5 us  [the longest x16 32.3 us: shift(): return lax.ppermute(value, 'ctx', pairs)]
    psum x1 -> x0, blocking collectives: 59.1 us -> none  [local(): lax.psum(jnp.sum(upstream * attn_low.astype(jnp.float32)), ('ctx', 'rec'))]
    dot_general x28 -> x0, matrix products: 53 us -> none  [the longest x5 11.9 us: head_blocks(): jnp.einsum('hav,vhd->ahd', dscore, key_heads, preferred_element_type=jnp....]
    ppermute x0 -> x19, starting transfers between devices: none -> 48.5 us  [the longest x16 45.2 us: shift(): return lax.ppermute(value, 'ctx', pairs)]
    all_gather x2 -> x0, waiting for transfers between devices: 47.7 us -> none  [the longest x1 45.7 us: local(): lax.all_gather(video_values, 'ctx', axis=1, tiled=True)]
    pallas_call x0 -> x5, Pallas kernels: none -> 40.4 us  [the longest x1 13.6 us: attention_backward(): pl.pallas_call(backward_kernel, grid=(pairs,), out_shape=(jax.ShapeDtypeS...]
    slice x24 -> x6, local copies, waits for them, and re-layouts: 39.2 us -> 3.36 us  [the longest x2 1.48 us: scatter_ring(): from_ahead = shift(last[:half], -1)]
  transfers between devices with their start and end apart: 8 -> 23, of which waited for: 3 -> 10; matrix products, arithmetic and copies ran while one was open for 34% -> 11% of each run, Pallas kernels for 0% -> 14%
where the time goes in v1:
time: 212 us; the launch traced here: 211 us
  waiting for transfers between devices  71.3 us (34%)
  starting transfers between devices  61.9 us (29%)
  Pallas kernels  40.4 us (19%)
  local copies, waits for them, and re-layouts  18.9 us (9%)
  other arithmetic  14.6 us (7%)
  between operations  3.98 us (2%)
    ppermute x16, starting transfers between devices, shift(): return lax.ppermute(value, 'ctx', pairs)  45.2 us
    ppermute x16, waiting for transfers between devices, shift(): return lax.ppermute(value, 'ctx', pairs)  32.3 us
    ppermute x3, waiting for transfers between devices, scatter_weight(): lax.ppermute(sent, 'rec', [(i, i ^ 1 << bit) for i in range(rec_count)])  27.2 us
    pallas_call x1, Pallas kernels, attention_backward(): pl.pallas_call(backward_kernel, grid=(pairs,), out_shape=(jax.ShapeDtypeS...  13.6 us
    pallas_call x1, Pallas kernels, attention_forward(): pl.pallas_call(forward_kernel, grid=(pairs,), out_shape=(jax.ShapeDtypeSt...  11.7 us
    unnamed x30, local copies, waits for them, and re-layouts  11.3 us
    pallas_call x1, Pallas kernels, output_grads(): pl.pallas_call(grads_kernel, grid=(blocks,), out_shape=(jax.ShapeDtypeStr...  10.7 us
    all_to_all x1, waiting for transfers between devices, scatter_weight(): parts = lax.all_to_all(term, 'ctx', split_axis=0, concat_axis=0, tiled=True)  9.23 us
  transfers between devices with their start and end apart: 23, of which 10 were waited for; matrix products, arithmetic and copies ran while one was open for 11% of the time, Pallas kernels for 14%

profile of v1, /device:TPU:0, one launch (start us, length us, event | category | flops | bytes accessed | tf_op | source)
XLA Modules:
  0.0 211.0 jit_solution(15934653251489760336)
XLA Ops:
  0.6 3.1 %collective-permute-start = (bf16[128,1280]{1,0:T(8,128)(2,1)}, bf16[128,1280]{1,0:T(8,128)(2,1)S(1)}, u32[]{:S(2)}, u32[]{:S(2)}) collective-permute-start(bf16[128,1280]{1,0:T(8,128)(2,1)} %bitcast.43), channel_id=1, source_target_pairs={{0,8},{8,16},{16,24},{24,0},{1,9},{9,17},{17,25},{25,1},{2,10},{10... | collective-permute-start | bytes 983048 | tf_op jit(solution)/shard_map/ppermute | solution.py:324
  5.8 3.8 %collective-permute-start.5 = (bf16[128,1280]{1,0:T(8,128)(2,1)}, bf16[128,1280]{1,0:T(8,128)(2,1)}, u32[]{:S(2)}, u32[]{:S(2)}) collective-permute-start(bf16[128,1280]{1,0:T(8,128)(2,1)} %bitcast.46), channel_id=1, source_target_pairs={{0,24},{8,0},{16,8},{24,16},{1,25},{9,1},{17,9},{25,17},{2,26},{10... | collective-permute-start | bytes 983048 | tf_op jit(solution)/shard_map/ppermute | solution.py:324
  15.2 3.0 %all-to-all-start = ((bf16[32,16,1408]{2,1,0:T(8,128)(2,1)}), bf16[32,16,1408]{2,1,0:T(8,128)(2,1)S(1)}, u32[]{:S(2)}, u32[]{:S(2)}) async-start(bf16[32,16,1408]{2,1,0:T(8,128)(2,1)} %bitcast.5), calls=%async_computation | async-start | bytes 2883584 | tf_op jit(solution)/shard_map/all_to_all | solution.py:402
  24.9 3.8 %collective-permute-done.4 = bf16[128,1280]{1,0:T(8,128)(2,1)} collective-permute-done((bf16[128,1280]{1,0:T(8,128)(2,1)}, bf16[128,1280]{1,0:T(8,128)(2,1)}, u32[]{:S(2)}, u32[]{:S(2)}) %collective-permute-start.4) | collective-permute-done | bytes 327712 | tf_op jit(solution)/shard_map/ppermute | solution.py:324
  29.7 7.9 %collective-permute-start.6 = (bf16[64,1280]{1,0:T(8,128)(2,1)S(1)}, bf16[64,1280]{1,0:T(8,128)(2,1)S(1)}, u32[]{:S(2)}, u32[]{:S(2)}) collective-permute-start(bf16[64,1280]{1,0:T(8,128)(2,1)S(1)} %slice.96), channel_id=1, source_target_pairs={{0,8},{8,16},{16,24},{24,0},{1,9},{9,17},{17,25},{25,1},{2,10},{10... | collective-permute-start | bytes 491528 | tf_op jit(solution)/shard_map/ppermute | solution.py:324
  38.5 3.3 %collective-permute-start.7 = (bf16[64,1280]{1,0:T(8,128)(2,1)S(1)}, bf16[64,1280]{1,0:T(8,128)(2,1)S(1)}, u32[]{:S(2)}, u32[]{:S(2)}) collective-permute-start(bf16[64,1280]{1,0:T(8,128)(2,1)S(1)} %slice.97), channel_id=1, source_target_pairs={{0,24},{8,0},{16,8},{24,16},{1,25},{9,1},{17,9},{25,17},{2,26},{10... | collective-permute-start | bytes 491528 | tf_op jit(solution)/shard_map/ppermute | solution.py:324
  43.9 18.5 %collective-permute-done.2 = bf16[64,1280]{1,0:T(8,128)(2,1)S(1)} collective-permute-done((bf16[64,1280]{1,0:T(8,128)(2,1)S(1)}, bf16[64,1280]{1,0:T(8,128)(2,1)S(1)}, u32[]{:S(2)}, u32[]{:S(2)}) %collective-permute-start.2) | collective-permute-done | bytes 163872 | tf_op jit(solution)/shard_map/ppermute | solution.py:324
  63.6 5.8 %collective-permute-done.6 = bf16[64,1280]{1,0:T(8,128)(2,1)S(1)} collective-permute-done((bf16[64,1280]{1,0:T(8,128)(2,1)S(1)}, bf16[64,1280]{1,0:T(8,128)(2,1)S(1)}, u32[]{:S(2)}, u32[]{:S(2)}) %collective-permute-start.6) | collective-permute-done | bytes 163872 | tf_op jit(solution)/shard_map/ppermute | solution.py:324
  69.5 11.7 %attention_forward.1 = (bf16[1280,256]{1,0:T(8,128)(2,1)S(1)}, f32[10,8,256]{2,1,0:T(8,128)S(1)}) custom-call(bf16[256,1280]{1,0:T(8,128)(2,1)S(1)} %bitcast.34, bf16[512,1280]{1,0:T(8,128)(2,1)S(1)} %constant_dynamic-update-slice_fusion.key_ref, bf16[512,1280]{1,0:T(8,128)(2,1)S(1)} %constant_dynamic-update-slice_fusion.5.value_ref), custom_call_target="tpu_custom_call" | custom-call | flops 2684354560 | bytes 3932160 | tf_op jit(solution)/shard_map/attention_forward/pallas_call | solution.py:109
  84.7 10.7 %output_grads.1 = (bf16[1280,256]{1,0:T(8,128)(2,1)S(1)}, bf16[256,1280]{1,0:T(8,128)(2,1)S(1)}, f32[1,256]{1,0:T(1,128)S(1)}, bf16[1280,1280]{1,0:T(8,128)(2,1)}) custom-call(f32[1]{0:T(128)S(6)} %copy.24.gate_ref, bf16[512,1408]{1,0:T(8,128)(2,1)S(1)} %bitcast.32, bf16[1280,1280]{1,0:T(8,128)(2,1)} %weight_ref.1, bf16[1280,256]{1,0:T(8,128)(2,1)S(1)} %copy-done.9, ...), custom_call_target="tpu_custom_call" | custom-call | flops 2013265920 | bytes 9175040 | tf_op jit(solution)/shard_map/output_grads/pallas_call | solution.py:171
  95.4 2.8 %dynamic-slice_bitcast_fusion = bf16[4,4,40,1280]{3,2,1,0:T(8,128)(2,1)} fusion(bf16[4,4,2,40,1280]{4,3,2,1,0:T(8,128)(2,1)} %bitcast.40, s32[]{:T(128)S(6)} %select_n.22), kind=kLoop, calls=%fused_computation.4 | loop fusion | bytes 3276804 | tf_op jit(solution)/shard_map/jit(dynamic_index_in_dim)/squeeze | solution.py:390
  98.2 13.6 %attention_backward.1 = (bf16[512,1280]{1,0:T(8,128)(2,1)S(1)}, bf16[512,1280]{1,0:T(8,128)(2,1)S(1)}, bf16[512,1280]{1,0:T(8,128)(2,1)}) custom-call(bf16[256,1280]{1,0:T(8,128)(2,1)S(1)} %bitcast.35, bf16[512,1280]{1,0:T(8,128)(2,1)} %copy-done.2, bf16[512,1280]{1,0:T(8,128)(2,1)} %copy-done.3, bf16[256,1280]{1,0:T(8,128)(2,1)S(1)} %get-tuple-element.19.grad_ref, ...), custom_call_target="tpu_custom_call" | custom-call | flops 6710886400 | bytes 9175040 | tf_op jit(solution)/shard_map/attention_backward/pallas_call | solution.py:262
  113.5 4.3 %collective-permute-start.12 = (bf16[64,1280]{1,0:T(8,128)(2,1)}, bf16[64,1280]{1,0:T(8,128)(2,1)}, u32[]{:S(2)}, u32[]{:S(2)}) collective-permute-start(bf16[64,1280]{1,0:T(8,128)(2,1)} %get-tuple-element.29), channel_id=1, source_target_pairs={{0,24},{8,0},{16,8},{24,16},{1,25},{9,1},{17,9},{25,17},{2,26},{10... | collective-permute-start | bytes 491528 | tf_op jit(solution)/shard_map/ppermute | solution.py:324
  117.8 6.6 %collective-permute-start.14 = (bf16[64,1280]{1,0:T(8,128)(2,1)S(1)}, bf16[64,1280]{1,0:T(8,128)(2,1)}, u32[]{:S(2)}, u32[]{:S(2)}) collective-permute-start(bf16[64,1280]{1,0:T(8,128)(2,1)S(1)} %get-tuple-element.30), channel_id=1, source_target_pairs={{0,8},{8,16},{16,24},{24,0},{1,9},{9,17},{17,25},{25,1},{2,10},{10... | collective-permute-start | bytes 491528 | tf_op jit(solution)/shard_map/ppermute | solution.py:324
  126.2 4.4 %all-to-all-start.3 = ((f32[32,1,128]{2,1,0:T(1,128)}), f32[32,1,128]{2,1,0:T(1,128)S(1)}, u32[]{:S(2)}, u32[]{:S(2)}) async-start(f32[32,1,128]{2,1,0:T(1,128)} %broadcast_in_dim.11), calls=%async_computation.3 | async-start | bytes 32768 | tf_op jit(solution)/shard_map/all_to_all | solution.py:437
  135.2 2.6 %all-to-all-done.3 = f32[32,1,128]{2,1,0:T(1,128)S(1)} async-done(((f32[32,1,128]{2,1,0:T(1,128)}), f32[32,1,128]{2,1,0:T(1,128)S(1)}, u32[]{:S(2)}, u32[]{:S(2)}) %all-to-all-start.3) | async-done | bytes 16416 | tf_op jit(solution)/shard_map/all_to_all | solution.py:437
  137.8 2.7 %all-to-all-start.1 = ((bf16[32,16,1280]{2,1,0:T(8,128)(2,1)}), bf16[32,16,1280]{2,1,0:T(8,128)(2,1)S(1)}, u32[]{:S(2)}, u32[]{:S(2)}) async-start(bf16[32,16,1280]{2,1,0:T(8,128)(2,1)} %bitcast.42), calls=%async_computation.1 | async-start | bytes 2621440 | tf_op jit(solution)/shard_map/all_to_all | solution.py:402
  147.8 3.5 %collective-permute-start.13 = (bf16[128,1280]{1,0:T(8,128)(2,1)}, bf16[128,1280]{1,0:T(8,128)(2,1)S(1)}, u32[]{:S(2)}, u32[]{:S(2)}) collective-permute-start(bf16[128,1280]{1,0:T(8,128)(2,1)} %pad_maximum_fusion.2), channel_id=1, source_target_pairs={{0,24},{8,0},{16,8},{24,16},{1,25},{9,1},{17,9},{25,17},{2,26},{10... | collective-permute-start | bytes 983048 | tf_op jit(solution)/shard_map/ppermute | solution.py:324
  153.1 21.7 %collective-permute-done.17 = bf16[4,2,40,1280]{3,2,1,0:T(8,128)(2,1)S(1)} collective-permute-done((bf16[4,2,40,1280]{3,2,1,0:T(8,128)(2,1)S(1)}, bf16[4,2,40,1280]{3,2,1,0:T(8,128)(2,1)S(1)}, u32[]{:S(2)}, u32[]{:S(2)}) %collective-permute-start.17) | collective-permute-done | bytes 819232 | tf_op jit(solution)/shard_map/ppermute | solution.py:392
  177.3 3.0 %collective-permute-start.9 = (bf16[128,1280]{1,0:T(8,128)(2,1)}, bf16[128,1280]{1,0:T(8,128)(2,1)}, u32[]{:S(2)}, u32[]{:S(2)}) collective-permute-start(bf16[128,1280]{1,0:T(8,128)(2,1)} %pad_maximum_fusion), channel_id=1, source_target_pairs={{0,24},{8,0},{16,8},{24,16},{1,25},{9,1},{17,9},{25,17},{2,26},{10... | collective-permute-start | bytes 983048 | tf_op jit(solution)/shard_map/ppermute | solution.py:324
  181.1 5.6 %collective-permute-done.18 = bf16[4,1,40,1280]{3,2,1,0:T(8,128)(2,1)S(1)} collective-permute-done((bf16[4,1,40,1280]{3,2,1,0:T(8,128)(2,1)S(1)}, bf16[4,1,40,1280]{3,2,1,0:T(8,128)(2,1)S(1)}, u32[]{:S(2)}, u32[]{:S(2)}) %collective-permute-start.18) | collective-permute-done | bytes 409632 | tf_op jit(solution)/shard_map/ppermute | solution.py:392
  187.5 3.5 %all-to-all-start.2 = ((bf16[4,40,1280]{2,1,0:T(8,128)(2,1)}), bf16[4,40,1280]{2,1,0:T(8,128)(2,1)S(1)}, u32[]{:S(2)}, u32[]{:S(2)}) async-start(bf16[4,40,1280]{2,1,0:T(8,128)(2,1)} %fusion.2), calls=%async_computation.2 | async-start | bytes 819200 | tf_op jit(solution)/shard_map/all_to_all | solution.py:396
  192.9 2.9 %collective-permute-done.11 = bf16[128,1280]{1,0:T(8,128)(2,1)} collective-permute-done((bf16[128,1280]{1,0:T(8,128)(2,1)}, bf16[128,1280]{1,0:T(8,128)(2,1)}, u32[]{:S(2)}, u32[]{:S(2)}) %collective-permute-start.11) | collective-permute-done | bytes 327712 | tf_op jit(solution)/shard_map/ppermute | solution.py:324
  199.9 9.2 %all-to-all-done.2 = bf16[4,40,1280]{2,1,0:T(8,128)(2,1)S(1)} async-done(((bf16[4,40,1280]{2,1,0:T(8,128)(2,1)}), bf16[4,40,1280]{2,1,0:T(8,128)(2,1)S(1)}, u32[]{:S(2)}, u32[]{:S(2)}) %all-to-all-start.2) | async-done | bytes 409632 | tf_op jit(solution)/shard_map/all_to_all | solution.py:396
  (83 shorter events, 49.5 us)
Async XLA Ops:
  0.6 20.3 %collective-permute-start = (bf16[128,1280]{1,0:T(8,128)(2,1)}, bf16[128,1280]{1,0:T(8,128)(2,1)S(1)}, u32[]{:S(2)}, u32[]{:S(2)}) collective-permute-start(bf16[128,1280]{1,0:T(8,128)(2,1)} %bitcast.43), channel_id=1, source_target_pairs={{0,8},{8,16},{16,24},{24,0},{1,9},{9,17},{17,25},{25,1},{2,10},{10... | collective-permute-start | bytes 983048 | tf_op jit(solution)/shard_map/ppermute | solution.py:324
  3.7 19.1 %collective-permute-start.1 = (bf16[128,1280]{1,0:T(8,128)(2,1)}, bf16[128,1280]{1,0:T(8,128)(2,1)S(1)}, u32[]{:S(2)}, u32[]{:S(2)}) collective-permute-start(bf16[128,1280]{1,0:T(8,128)(2,1)} %bitcast.44), channel_id=1, source_target_pairs={{0,24},{8,0},{16,8},{24,16},{1,25},{9,1},{17,9},{25,17},{2,26},{10... | collective-permute-start | bytes 983048 | tf_op jit(solution)/shard_map/ppermute | solution.py:324
  5.8 22.9 %collective-permute-start.4 = (bf16[128,1280]{1,0:T(8,128)(2,1)}, bf16[128,1280]{1,0:T(8,128)(2,1)}, u32[]{:S(2)}, u32[]{:S(2)}) collective-permute-start(bf16[128,1280]{1,0:T(8,128)(2,1)} %bitcast.45), channel_id=1, source_target_pairs={{0,8},{8,16},{16,24},{24,0},{1,9},{9,17},{17,25},{25,1},{2,10},{10... | collective-permute-start | bytes 983048 | tf_op jit(solution)/shard_map/ppermute | solution.py:324
  5.8 31.8 %collective-permute-start.5 = (bf16[128,1280]{1,0:T(8,128)(2,1)}, bf16[128,1280]{1,0:T(8,128)(2,1)}, u32[]{:S(2)}, u32[]{:S(2)}) collective-permute-start(bf16[128,1280]{1,0:T(8,128)(2,1)} %bitcast.46), channel_id=1, source_target_pairs={{0,24},{8,0},{16,8},{24,16},{1,25},{9,1},{17,9},{25,17},{2,26},{10... | collective-permute-start | bytes 983048 | tf_op jit(solution)/shard_map/ppermute | solution.py:324
  15.2 67.9 %all-to-all-start = ((bf16[32,16,1408]{2,1,0:T(8,128)(2,1)}), bf16[32,16,1408]{2,1,0:T(8,128)(2,1)S(1)}, u32[]{:S(2)}, u32[]{:S(2)}) async-start(bf16[32,16,1408]{2,1,0:T(8,128)(2,1)} %bitcast.5), calls=%async_computation | async-start | bytes 2883584 | tf_op jit(solution)/shard_map/all_to_all | solution.py:402
  21.0 41.4 %collective-permute-start.2 = (bf16[64,1280]{1,0:T(8,128)(2,1)S(1)}, bf16[64,1280]{1,0:T(8,128)(2,1)S(1)}, u32[]{:S(2)}, u32[]{:S(2)}) collective-permute-start(bf16[64,1280]{1,0:T(8,128)(2,1)S(1)} %slice.94), channel_id=1, source_target_pairs={{0,8},{8,16},{16,24},{24,0},{1,9},{9,17},{17,25},{25,1},{2,10},{10... | collective-permute-start | bytes 491528 | tf_op jit(solution)/shard_map/ppermute | solution.py:324
  22.8 40.8 %collective-permute-start.3 = (bf16[64,1280]{1,0:T(8,128)(2,1)S(1)}, bf16[64,1280]{1,0:T(8,128)(2,1)S(1)}, u32[]{:S(2)}, u32[]{:S(2)}) collective-permute-start(bf16[64,1280]{1,0:T(8,128)(2,1)S(1)} %slice.95), channel_id=1, source_target_pairs={{0,24},{8,0},{16,8},{24,16},{1,25},{9,1},{17,9},{25,17},{2,26},{10... | collective-permute-start | bytes 491528 | tf_op jit(solution)/shard_map/ppermute | solution.py:324
  29.7 39.7 %collective-permute-start.6 = (bf16[64,1280]{1,0:T(8,128)(2,1)S(1)}, bf16[64,1280]{1,0:T(8,128)(2,1)S(1)}, u32[]{:S(2)}, u32[]{:S(2)}) collective-permute-start(bf16[64,1280]{1,0:T(8,128)(2,1)S(1)} %slice.96), channel_id=1, source_target_pairs={{0,8},{8,16},{16,24},{24,0},{1,9},{9,17},{17,25},{25,1},{2,10},{10... | collective-permute-start | bytes 491528 | tf_op jit(solution)/shard_map/ppermute | solution.py:324
  38.5 31.0 %collective-permute-start.7 = (bf16[64,1280]{1,0:T(8,128)(2,1)S(1)}, bf16[64,1280]{1,0:T(8,128)(2,1)S(1)}, u32[]{:S(2)}, u32[]{:S(2)}) collective-permute-start(bf16[64,1280]{1,0:T(8,128)(2,1)S(1)} %slice.97), channel_id=1, source_target_pairs={{0,24},{8,0},{16,8},{24,16},{1,25},{9,1},{17,9},{25,17},{2,26},{10... | collective-permute-start | bytes 491528 | tf_op jit(solution)/shard_map/ppermute | solution.py:324
  41.8 27.7 %copy-start.5 = (bf16[1,256,1280]{2,1,0:T(8,128)(2,1)S(1)}, bf16[1,256,1280]{2,1,0:T(8,128)(2,1)}, u32[]{:S(2)}) copy-start(bf16[1,256,1280]{2,1,0:T(8,128)(2,1)} %param.9) | copy-start | bytes 1966084
  98.1 44.8 %collective-permute-start.16 = (bf16[4,4,40,1280]{3,2,1,0:T(8,128)(2,1)}, bf16[4,4,40,1280]{3,2,1,0:T(8,128)(2,1)}, u32[]{:S(2)}, u32[]{:S(2)}) collective-permute-start(bf16[4,4,40,1280]{3,2,1,0:T(8,128)(2,1)} %dynamic-slice_bitcast_fusion), channel_id=1, source_target_pairs={{0,1},{1,0},{2,3},{3,2},{4,5},{5,4},{6,7},{7,6},{8,9},{9,8},{10,11... | collective-permute-start | bytes 4915208 | tf_op jit(solution)/shard_map/ppermute | solution.py:392
  113.5 28.2 %collective-permute-start.12 = (bf16[64,1280]{1,0:T(8,128)(2,1)}, bf16[64,1280]{1,0:T(8,128)(2,1)}, u32[]{:S(2)}, u32[]{:S(2)}) collective-permute-start(bf16[64,1280]{1,0:T(8,128)(2,1)} %get-tuple-element.29), channel_id=1, source_target_pairs={{0,24},{8,0},{16,8},{24,16},{1,25},{9,1},{17,9},{25,17},{2,26},{10... | collective-permute-start | bytes 491528 | tf_op jit(solution)/shard_map/ppermute | solution.py:324
  117.8 23.9 %collective-permute-start.14 = (bf16[64,1280]{1,0:T(8,128)(2,1)S(1)}, bf16[64,1280]{1,0:T(8,128)(2,1)}, u32[]{:S(2)}, u32[]{:S(2)}) collective-permute-start(bf16[64,1280]{1,0:T(8,128)(2,1)S(1)} %get-tuple-element.30), channel_id=1, source_target_pairs={{0,8},{8,16},{16,24},{24,0},{1,9},{9,17},{17,25},{25,1},{2,10},{10... | collective-permute-start | bytes 491528 | tf_op jit(solution)/shard_map/ppermute | solution.py:324
  126.2 11.5 %all-to-all-start.3 = ((f32[32,1,128]{2,1,0:T(1,128)}), f32[32,1,128]{2,1,0:T(1,128)S(1)}, u32[]{:S(2)}, u32[]{:S(2)}) async-start(f32[32,1,128]{2,1,0:T(1,128)} %broadcast_in_dim.11), calls=%async_computation.3 | async-start | bytes 32768 | tf_op jit(solution)/shard_map/all_to_all | solution.py:437
  131.4 20.7 %collective-permute-start.10 = (bf16[64,1280]{1,0:T(8,128)(2,1)}, bf16[64,1280]{1,0:T(8,128)(2,1)}, u32[]{:S(2)}, u32[]{:S(2)}) collective-permute-start(bf16[64,1280]{1,0:T(8,128)(2,1)} %get-tuple-element.36), channel_id=1, source_target_pairs={{0,8},{8,16},{16,24},{24,0},{1,9},{9,17},{17,25},{25,1},{2,10},{10... | collective-permute-start | bytes 491528 | tf_op jit(solution)/shard_map/ppermute | solution.py:324
  133.1 18.9 %collective-permute-start.8 = (bf16[64,1280]{1,0:T(8,128)(2,1)}, bf16[64,1280]{1,0:T(8,128)(2,1)}, u32[]{:S(2)}, u32[]{:S(2)}) collective-permute-start(bf16[64,1280]{1,0:T(8,128)(2,1)} %get-tuple-element.35), channel_id=1, source_target_pairs={{0,24},{8,0},{16,8},{24,16},{1,25},{9,1},{17,9},{25,17},{2,26},{10... | collective-permute-start | bytes 491528 | tf_op jit(solution)/shard_map/ppermute | solution.py:324
  137.8 49.7 %all-to-all-start.1 = ((bf16[32,16,1280]{2,1,0:T(8,128)(2,1)}), bf16[32,16,1280]{2,1,0:T(8,128)(2,1)S(1)}, u32[]{:S(2)}, u32[]{:S(2)}) async-start(bf16[32,16,1280]{2,1,0:T(8,128)(2,1)} %bitcast.42), calls=%async_computation.1 | async-start | bytes 2621440 | tf_op jit(solution)/shard_map/all_to_all | solution.py:402
  145.4 29.4 %collective-permute-start.17 = (bf16[4,2,40,1280]{3,2,1,0:T(8,128)(2,1)S(1)}, bf16[4,2,40,1280]{3,2,1,0:T(8,128)(2,1)S(1)}, u32[]{:S(2)}, u32[]{:S(2)}) collective-permute-start(bf16[4,2,40,1280]{3,2,1,0:T(8,128)(2,1)S(1)} %dynamic-slice_bitcast_fusion.1), channel_id=1, source_target_pairs={{0,2},{1,3},{2,0},{3,1},{4,6},{5,7},{6,4},{7,5},{8,10},{9,11},{10,... | collective-permute-start | bytes 2457608 | tf_op jit(solution)/shard_map/ppermute | solution.py:392
  147.8 43.2 %collective-permute-start.13 = (bf16[128,1280]{1,0:T(8,128)(2,1)}, bf16[128,1280]{1,0:T(8,128)(2,1)S(1)}, u32[]{:S(2)}, u32[]{:S(2)}) collective-permute-start(bf16[128,1280]{1,0:T(8,128)(2,1)} %pad_maximum_fusion.2), channel_id=1, source_target_pairs={{0,24},{8,0},{16,8},{24,16},{1,25},{9,1},{17,9},{25,17},{2,26},{10... | collective-permute-start | bytes 983048 | tf_op jit(solution)/shard_map/ppermute | solution.py:324
  152.0 39.0 %collective-permute-start.15 = (bf16[128,1280]{1,0:T(8,128)(2,1)}, bf16[128,1280]{1,0:T(8,128)(2,1)}, u32[]{:S(2)}, u32[]{:S(2)}) collective-permute-start(bf16[128,1280]{1,0:T(8,128)(2,1)} %pad_maximum_fusion.3), channel_id=1, source_target_pairs={{0,8},{8,16},{16,24},{24,0},{1,9},{9,17},{17,25},{25,1},{2,10},{10... | collective-permute-start | bytes 983048 | tf_op jit(solution)/shard_map/ppermute | solution.py:324
  175.1 11.6 %collective-permute-start.18 = (bf16[4,1,40,1280]{3,2,1,0:T(8,128)(2,1)S(1)}, bf16[4,1,40,1280]{3,2,1,0:T(8,128)(2,1)S(1)}, u32[]{:S(2)}, u32[]{:S(2)}) collective-permute-start(bf16[4,1,40,1280]{3,2,1,0:T(8,128)(2,1)S(1)} %constant_dynamic-slice_fusion), channel_id=1, source_target_pairs={{0,4},{1,5},{2,6},{3,7},{4,0},{5,1},{6,2},{7,3},{8,12},{9,13},{10,... | collective-permute-start | bytes 1228808 | tf_op jit(solution)/shard_map/ppermute | solution.py:392
  177.3 15.6 %collective-permute-start.9 = (bf16[128,1280]{1,0:T(8,128)(2,1)}, bf16[128,1280]{1,0:T(8,128)(2,1)}, u32[]{:S(2)}, u32[]{:S(2)}) collective-permute-start(bf16[128,1280]{1,0:T(8,128)(2,1)} %pad_maximum_fusion), channel_id=1, source_target_pairs={{0,24},{8,0},{16,8},{24,16},{1,25},{9,1},{17,9},{25,17},{2,26},{10... | collective-permute-start | bytes 983048 | tf_op jit(solution)/shard_map/ppermute | solution.py:324
  181.1 14.8 %collective-permute-start.11 = (bf16[128,1280]{1,0:T(8,128)(2,1)}, bf16[128,1280]{1,0:T(8,128)(2,1)}, u32[]{:S(2)}, u32[]{:S(2)}) collective-permute-start(bf16[128,1280]{1,0:T(8,128)(2,1)} %pad_maximum_fusion.1), channel_id=1, source_target_pairs={{0,8},{8,16},{16,24},{24,0},{1,9},{9,17},{17,25},{25,1},{2,10},{10... | collective-permute-start | bytes 983048 | tf_op jit(solution)/shard_map/ppermute | solution.py:324
  187.5 21.7 %all-to-all-start.2 = ((bf16[4,40,1280]{2,1,0:T(8,128)(2,1)}), bf16[4,40,1280]{2,1,0:T(8,128)(2,1)S(1)}, u32[]{:S(2)}, u32[]{:S(2)}) async-start(bf16[4,40,1280]{2,1,0:T(8,128)(2,1)} %fusion.2), calls=%async_computation.2 | async-start | bytes 819200 | tf_op jit(solution)/shard_map/all_to_all | solution.py:396
  (10 other events, 39.8 us)

commit v2 on v1

v2 whole, which is shorter than its diff:
```python
import jax
import jax.numpy as jnp
from jax import lax
from jax.experimental import pallas as pl
from jax.experimental.pallas import tpu as pltpu
from jax.sharding import PartitionSpec as P

HEAD_DIM = 64
LANES = 128
VMEM_LIMIT = 32 * 1024 * 1024
VMEM_WHOLE = 62 * 1024 * 1024
ATTENTION_COST = 150
FAR_COST = 300000
STEP_COST = 74000
NT = (((1,), (1,)), ((), ()))
NN = (((1,), (0,)), ((), ()))


def mm(left, right, dims=NN):
    return lax.dot_general(left, right, dims, preferred_element_type=jnp.float32)


def iota(shape, dim):
    return lax.broadcasted_iota(jnp.int32, shape, dim)


def params(limit=VMEM_LIMIT):
    return pltpu.CompilerParams(vmem_limit_bytes=limit)


def as_column(row_vector):
    wide = jnp.broadcast_to(row_vector, (LANES, row_vector.shape[1]))
    return jnp.transpose(wide)[:, :1]


def as_row(column_block):
    return jnp.transpose(column_block.astype(jnp.float32))[:1, :]


def prep_kernel(pair_cap, owners, live_ref, dest_ref, row_ref, grads_ref, send_ref, target_ref):
    slots, width = grads_ref.shape
    slot = iota((1, slots), 1)
    is_live = slot < live_ref[0]
    dest = dest_ref[...]
    hot = jnp.logical_and(iota((owners, slots), 0) == dest, is_live)
    hot_f = jnp.where(hot, 1.0, 0.0)
    earlier = jnp.where(iota((slots, slots), 0) < iota((slots, slots), 1), 1.0, 0.0)
    before = mm(hot_f.astype(jnp.bfloat16), earlier.astype(jnp.bfloat16))
    rank = jnp.sum(hot_f * before, axis=0, keepdims=True).astype(jnp.int32)
    target = jnp.where(is_live, dest * pair_cap + rank, slots)
    target_ref[...] = target
    chosen = iota((slots, slots), 0) == target
    place = jnp.where(chosen, 1.0, 0.0).astype(jnp.bfloat16)
    send_ref[:, :width] = mm(place, grads_ref[...]).astype(jnp.bfloat16)
    row_no = (row_ref[...] + 1).astype(jnp.float32)
    index = jnp.sum(jnp.where(chosen, row_no, 0.0), axis=1, keepdims=True)
    send_ref[:, width:] = jnp.broadcast_to(index, (slots, LANES)).astype(jnp.bfloat16)


def route_prep(live_count, dest_device, dest_row, row_grads, owners):
    slots, width = row_grads.shape
    kernel = lambda *refs: prep_kernel(slots // owners, owners, *refs)
    vmem = pl.BlockSpec(memory_space=pltpu.VMEM)
    return pl.pallas_call(
        kernel,
        out_shape=(
            jax.ShapeDtypeStruct((slots, width + LANES), jnp.bfloat16),
            jax.ShapeDtypeStruct((1, slots), jnp.int32),
        ),
        in_specs=[pl.BlockSpec(memory_space=pltpu.SMEM), vmem, vmem, vmem],
        out_specs=(vmem, vmem),
        compiler_params=params(),
        name="route_prep",
        cost_estimate=pl.CostEstimate(
            flops=2 * slots * slots * width,
            bytes_accessed=4 * slots * width,
            transcendentals=0,
        ),
    )(live_count, dest_device.reshape(1, slots), dest_row.reshape(1, slots), row_grads)


def head_masks(shape, dim):
    first = iota(shape, dim) < HEAD_DIM
    return first, jnp.logical_not(first)


def keep(mask, value):
    return jnp.where(mask, value, jnp.zeros((), value.dtype))


def unpack_kernel(recv_ref, rows_ref, rows_t_ref):
    slots = recv_ref.shape[0]
    rows, width = rows_ref.shape
    index = as_row(recv_ref[:, width:])
    place = index == (iota((rows, slots), 0) + 1).astype(jnp.float32)
    place = jnp.where(place, 1.0, 0.0).astype(jnp.bfloat16)
    owned = mm(place, recv_ref[:, :width]).astype(jnp.bfloat16)
    rows_ref[...] = owned
    rows_t_ref[...] = jnp.transpose(owned)


def unpack_rows(recv, rows):
    slots, width = recv.shape
    width -= LANES
    vmem = pl.BlockSpec(memory_space=pltpu.VMEM)
    return pl.pallas_call(
        unpack_kernel,
        out_shape=(
            jax.ShapeDtypeStruct((rows, width), jnp.bfloat16),
            jax.ShapeDtypeStruct((width, rows), jnp.bfloat16),
        ),
        in_specs=[vmem],
        out_specs=(vmem, vmem),
        compiler_params=params(),
        name="unpack_rows",
        cost_estimate=pl.CostEstimate(
            flops=2 * slots * rows * width,
            bytes_accessed=2 * (slots + 2 * rows) * width,
            transcendentals=0,
        ),
    )(recv)


def attend(gate_ref, query_ref, weight_ref, rows_ref, index_ref, keys, values,
           attn_ref, back_ref, gate_out_ref):
    rows = query_ref.shape[0]
    slots = index_ref.shape[0]
    root = HEAD_DIM ** -0.5
    query = query_ref[...] * jnp.asarray(root, jnp.bfloat16)
    keys_tr = jnp.transpose(keys)
    values_tr = jnp.transpose(values)
    gate = jnp.tanh(jnp.full((1, LANES), gate_ref[0], jnp.float32))[:, :1]
    upstream = mm(weight_ref[...], rows_ref[...], NT)
    grad_t = (gate * upstream).astype(jnp.bfloat16)
    grad = jnp.transpose(grad_t)
    lane_masks = head_masks((rows, LANES), 1)
    row_masks = head_masks((LANES, rows), 0)
    key_term = None
    value_term = None
    query_parts = []
    gate_sum = None
    for head in range(2):
        span = slice(head * HEAD_DIM, (head + 1) * HEAD_DIM)
        query_h = keep(lane_masks[head], query)
        grad_h = keep(lane_masks[head], grad)
        scores = mm(keys, query_h, NT)
        peak = jnp.max(scores, axis=0, keepdims=True)
        shifted = jnp.exp(scores - peak)
        inverse = 1.0 / jnp.sum(shifted, axis=0, keepdims=True)
        probs = shifted * inverse
        probs_low = probs.astype(jnp.bfloat16)
        attn_h = mm(values_tr[span, :], probs_low).astype(jnp.bfloat16)
        attn_ref[span, :] = attn_h
        attn_wide = attn_h.astype(jnp.float32)
        delta = jnp.sum(grad_t[span, :].astype(jnp.float32) * attn_wide, axis=0, keepdims=True)
        gate_h = jnp.sum(upstream[span, :] * attn_wide, axis=0, keepdims=True)
        dprob = mm(values, keep(row_masks[head], grad_t))
        dscore = (probs * (dprob - delta)).astype(jnp.bfloat16)
        value_part = mm(probs_low, grad_h)
        key_part = mm(dscore, query_h)
        value_term = value_part if head == 0 else value_term + value_part
        key_term = key_part if head == 0 else key_term + key_part
        gate_sum = gate_h if head == 0 else gate_sum + gate_h
        query_parts.append(mm(keys_tr[span, :], dscore) * root)
    gate_out_ref[...] += gate_sum
    query_grad = jnp.transpose(jnp.concatenate(query_parts, axis=0).astype(jnp.bfloat16))
    index = index_ref[...][:, :1].astype(jnp.float32)
    place = index == (iota((slots, rows), 1) + 1).astype(jnp.float32)
    place = jnp.where(place, 1.0, 0.0).astype(jnp.bfloat16)
    back_ref[...] = mm(place, query_grad).astype(jnp.bfloat16)
    return key_term.astype(jnp.bfloat16), value_term.astype(jnp.bfloat16)


def gate_lanes(total, shape):
    high = total.astype(jnp.bfloat16).astype(jnp.float32)
    middle = (total - high).astype(jnp.bfloat16).astype(jnp.float32)
    low = total - high - middle
    lane = iota(shape, 1)
    terms = jnp.where(lane == 0, high, jnp.where(lane == 1, middle, low))
    return jnp.where(lane < 3, terms, 0.0).astype(jnp.bfloat16)


def attention_kernel(blocks, pairs, gate_ref, before_ref, query_ref, weight_ref, rows_ref,
                     index_ref, *refs):
    parts, outs = refs[: blocks + 1], refs[blocks + 1 : 2 * blocks + 2]
    attn_ref, back_ref, gate_out_ref = refs[2 * blocks + 2 :]
    step = pl.program_id(0)

    @pl.when(step == 0)
    def _():
        gate_out_ref[...] = before_ref[...]

    @pl.when(step < pairs)
    def _():
        chunk = parts[-1].shape[0]
        keys = jnp.concatenate([part[:chunk] for part in parts[:-1]], axis=0)
        values = jnp.concatenate(
            [part[chunk:] for part in parts[:-2]] + [parts[-1][...]], axis=0
        )
        key_term, value_term = attend(
            gate_ref, query_ref, weight_ref, rows_ref, index_ref, keys, values,
            attn_ref, back_ref, gate_out_ref,
        )
        for number, out in enumerate(outs[:-2]):
            span = slice(number * chunk, (number + 1) * chunk)
            out[:chunk] = key_term[span]
            out[chunk:] = value_term[span]
        outs[-2][...] = key_term[-chunk:]
        outs[-1][...] = value_term[-chunk:]

    @pl.when(step == pairs)
    def _():
        total = jnp.sum(gate_out_ref[...], axis=1, keepdims=True)
        back_ref[...] = gate_lanes(total, back_ref.shape)


def attention(gate_logit, before, queries, out_weight, grad_rows, recv, parts, first_pair, extra):
    rows, width = queries.shape
    slots = recv.shape[0]
    span = parts[0].shape[1]
    pairs = span // LANES
    tokens = (len(parts) - 1) * parts[-1].shape[0]
    at = lambda i: jnp.minimum(i, pairs - 1)
    columns = lambda i: (0, at(i))
    part_specs = [pl.BlockSpec((part.shape[0], LANES), columns) for part in parts]
    whole = lambda i: (0, 0)
    outs = pl.pallas_call(
        lambda *refs: attention_kernel(len(parts) - 1, pairs, *refs),
        grid=(pairs + extra,),
        out_shape=(
            *[jax.ShapeDtypeStruct(part.shape, jnp.bfloat16) for part in parts],
            jax.ShapeDtypeStruct((span, rows), jnp.bfloat16),
            jax.ShapeDtypeStruct((slots, span + extra * LANES), jnp.bfloat16),
            jax.ShapeDtypeStruct((1, rows), jnp.float32),
        ),
        in_specs=[
            pl.BlockSpec(memory_space=pltpu.SMEM),
            pl.BlockSpec((1, rows), whole),
            pl.BlockSpec((rows, LANES), lambda i: (0, at(i) + first_pair)),
            pl.BlockSpec((LANES, width), lambda i: (at(i) + first_pair, 0)),
            pl.BlockSpec((rows, width), whole),
            pl.BlockSpec((slots, LANES), lambda i: (0, width // LANES)),
            *part_specs,
        ],
        out_specs=(
            *part_specs,
            pl.BlockSpec((LANES, rows), lambda i: (at(i), 0)),
            pl.BlockSpec((slots, LANES), lambda i: (0, i)),
            pl.BlockSpec((1, rows), whole),
        ),
        compiler_params=params(VMEM_WHOLE),
        name="attention",
        cost_estimate=pl.CostEstimate(
            flops=ATTENTION_COST * rows * tokens * span,
            bytes_accessed=8 * tokens * span + 12 * rows * span,
            transcendentals=rows * tokens * span // HEAD_DIM,
        ),
    )(gate_logit, before, queries, out_weight, grad_rows, recv, *parts)
    return outs[: len(parts)], *outs[len(parts) :]


def weight_kernel(gate_ref, rows_t_ref, first_ref, second_ref, out_ref):
    gate = jnp.tanh(jnp.full((1, LANES), gate_ref[0], jnp.float32))[:, :1]
    half = first_ref.shape[0]
    for number, attn_ref in enumerate((first_ref, second_ref)):
        block = mm(rows_t_ref[...], attn_ref[...], NT)
        out_ref[:, number * half : (number + 1) * half] = (gate * block).astype(jnp.bfloat16)


def weight_term(gate_logit, rows_t, first_attn, second_attn):
    width, rows = rows_t.shape
    steps = 5
    return pl.pallas_call(
        weight_kernel,
        grid=(steps,),
        out_shape=jax.ShapeDtypeStruct((width, width), jnp.bfloat16),
        in_specs=[
            pl.BlockSpec(memory_space=pltpu.SMEM),
            pl.BlockSpec((width // steps, rows), lambda i: (i, 0)),
            pl.BlockSpec((width // 2, rows), lambda i: (0, 0)),
            pl.BlockSpec((width // 2, rows), lambda i: (0, 0)),
        ],
        out_specs=pl.BlockSpec((width // steps, width), lambda i: (i, 0)),
        compiler_params=params(),
        name="weight_term",
        cost_estimate=pl.CostEstimate(
            flops=2 * rows * width * width,
            bytes_accessed=2 * width * width + 4 * rows * width,
            transcendentals=0,
        ),
    )(gate_logit, rows_t, first_attn, second_attn)


def pick_kernel(pair_cap, target_ref, first_ref, second_ref, out_ref, gate_ref):
    slots, half = first_ref.shape
    target = as_column(target_ref[...].astype(jnp.float32))
    place = target == iota((slots, slots), 1).astype(jnp.float32)
    place = jnp.where(place, 1.0, 0.0).astype(jnp.bfloat16)
    out_ref[:, :half] = mm(place, first_ref[...]).astype(jnp.bfloat16)
    out_ref[:, half:] = mm(place, second_ref[:, :half]).astype(jnp.bfloat16)
    shares = second_ref[:, half:].astype(jnp.float32)
    shares = jnp.where(iota(shares.shape, 0) % pair_cap == 0, shares, 0.0)
    gate_ref[...] = jnp.sum(jnp.sum(shares, axis=0, keepdims=True), axis=1, keepdims=True)


def pick_rows(target, first, second, pair_cap):
    slots, half = first.shape
    vmem = pl.BlockSpec(memory_space=pltpu.VMEM)
    return pl.pallas_call(
        lambda *refs: pick_kernel(pair_cap, *refs),
        out_shape=(
            jax.ShapeDtypeStruct((slots, 2 * half), jnp.bfloat16),
            jax.ShapeDtypeStruct((1, 1), jnp.float32),
        ),
        in_specs=[vmem, vmem, vmem],
        out_specs=(vmem, vmem),
        compiler_params=params(),
        name="pick_rows",
        cost_estimate=pl.CostEstimate(
            flops=4 * slots * slots * half,
            bytes_accessed=8 * slots * half,
            transcendentals=0,
        ),
    )(target, first, second)


def shift(value, step):
    count = lax.axis_size("ctx")
    pairs = [(i, (i + step) % count) for i in range(count)]
    return lax.ppermute(value, "ctx", pairs)


def gather_near(chunk):
    parts = [chunk]
    ahead = behind = chunk
    for _ in range(1, lax.axis_size("ctx") // 2):
        ahead = shift(ahead, 1)
        behind = shift(behind, -1)
        parts += [ahead, behind]
    return parts


def halves_kernel(ahead_ref, behind_ref, keys_ref, values_ref):
    half = keys_ref.shape[0]
    keys_ref[...] = ahead_ref[:half]
    values_ref[...] = behind_ref[half:]


def farthest(ahead, behind, cost):
    half = ahead.shape[0] // 2
    vmem = pl.BlockSpec(memory_space=pltpu.VMEM)
    return pl.pallas_call(
        halves_kernel,
        out_shape=(jax.ShapeDtypeStruct((half, ahead.shape[1]), ahead.dtype),) * 2,
        in_specs=[vmem, vmem],
        out_specs=(vmem, vmem),
        compiler_params=params(),
        name="farthest",
        cost_estimate=pl.CostEstimate(
            flops=cost * ahead.size, bytes_accessed=4 * ahead.size, transcendentals=0
        ),
    )(ahead, behind)


def gather_far(parts, cost):
    keys, values = farthest(parts[-2], parts[-1], cost)
    return [*parts, shift(keys, 1), shift(values, -1)]


def add(left, right):
    return (left.astype(jnp.float32) + right.astype(jnp.float32)).astype(jnp.bfloat16)


def start_sums(parts):
    return shift(parts[-2], -1), shift(parts[-1], 1)


def step_kernel(back_ref, forth_ref, far_keys_ref, far_values_ref, back_out_ref, forth_out_ref):
    half = far_keys_ref.shape[0]
    back_out_ref[:half] = add(back_ref[:half], far_keys_ref[...])
    back_out_ref[half:] = back_ref[half:]
    forth_out_ref[:half] = forth_ref[:half]
    forth_out_ref[half:] = add(forth_ref[half:], far_values_ref[...])


def step_sums(back, forth, far_keys, far_values):
    vmem = pl.BlockSpec(memory_space=pltpu.VMEM)
    return pl.pallas_call(
        step_kernel,
        out_shape=(jax.ShapeDtypeStruct(back.shape, back.dtype),) * 2,
        in_specs=[vmem] * 4,
        out_specs=(vmem, vmem),
        compiler_params=params(),
        name="step_sums",
        cost_estimate=pl.CostEstimate(
            flops=STEP_COST * back.size,
            bytes_accessed=8 * back.size,
            transcendentals=0,
        ),
    )(back, forth, far_keys, far_values)


def finish_sums(parts, far_keys, far_values):
    half = far_keys.shape[0]
    steps = lax.axis_size("ctx") // 2 - 1
    back, forth = step_sums(parts[2 * steps - 1], parts[2 * steps], far_keys, far_values)
    for step in range(steps, 0, -1):
        if step < steps:
            back = add(parts[2 * step - 1], back)
            forth = add(parts[2 * step], forth)
        back = shift(back, -1)
        forth = shift(forth, 1)
    own = parts[0].astype(jnp.float32)
    total = own + back.astype(jnp.float32) + forth.astype(jnp.float32)
    total = total.astype(jnp.bfloat16)
    return total[:half], total[half:]


def halve(term, bit):
    rec_count = lax.axis_size("rec")
    ctx_count, left, rows, width = term.shape
    term = term.reshape(ctx_count, left // 2, 2, rows, width)
    mine = (lax.axis_index("rec") >> bit) & 1
    sent = lax.dynamic_index_in_dim(term, 1 - mine, 2, keepdims=False)
    kept = lax.dynamic_index_in_dim(term, mine, 2, keepdims=False)
    return add(kept, lax.ppermute(sent, "rec", [(i, i ^ (1 << bit)) for i in range(rec_count)]))


def sum_blocks(term):
    ctx_count = lax.axis_size("ctx")
    block = lax.axis_index("ctx")
    total = lax.dynamic_index_in_dim(term, block, 0, keepdims=False).astype(jnp.float32)
    for step in range(1, ctx_count):
        sent = lax.dynamic_index_in_dim(term, block ^ step, 0, keepdims=False)
        pairs = [(i, i ^ step) for i in range(ctx_count)]
        total = total + lax.ppermute(sent, "ctx", pairs).astype(jnp.float32)
    return total


def exchange(value, count):
    slots, width = value.shape
    moved = lax.all_to_all(
        value.reshape(count, slots // count, width),
        ("ctx", "rec"),
        split_axis=0,
        concat_axis=0,
        tiled=True,
    )
    return moved.reshape(slots, width)


def local(
    queries,
    video_keys,
    video_values,
    out_weight,
    gate_logit,
    row_grads,
    dest_device,
    dest_row,
    live_count,
):
    count = lax.axis_size("ctx") * lax.axis_size("rec")
    rows, width = queries.shape[1:]
    half = width // 2
    tie = lax.optimization_barrier
    first, second = (
        jnp.concatenate([video_keys[0][:, part], video_values[0][:, part]], axis=0)
        for part in (slice(0, half), slice(half, width))
    )
    first_parts = gather_far(gather_near(first), FAR_COST)
    send, target = route_prep(live_count, dest_device, dest_row, row_grads, count)
    recv = exchange(send, count)
    recv, second = tie((recv, second))
    second_parts = gather_near(second)
    grad_rows, rows_t = unpack_rows(recv, rows)
    common = (queries[0], out_weight, grad_rows, recv)
    first_terms, first_attn, first_back, gate_part = attention(
        gate_logit, jnp.zeros((1, rows), jnp.float32), *common, first_parts, 0, 0
    )
    first_far = start_sums(first_terms)
    first_returned = exchange(first_back, count)
    second_parts, gate_part = tie((second_parts, gate_part))
    second_parts = gather_far(second_parts, 1)
    second_terms, second_attn, second_back, _ = attention(
        gate_logit, gate_part, *common, second_parts, half // LANES, 1
    )
    second_far = start_sums(second_terms)
    first_far, second_attn = tie((first_far, second_attn))
    product = weight_term(gate_logit, rows_t, first_attn, second_attn)
    first_returned, product = tie((first_returned, product))
    blocks, devices = lax.axis_size("ctx"), lax.axis_size("rec")
    product = halve(product.reshape(blocks, devices, width // count, width), 0)
    second_returned = exchange(second_back, count)
    first_sum = finish_sums(first_terms, *first_far)
    bit = 1
    while product.shape[1] > 1:
        product = halve(product, bit)
        bit += 1
    second_far, weight_chips = tie((second_far, product[:, 0]))
    second_sum = finish_sums(second_terms, *second_far)
    weight_grad = sum_blocks(weight_chips)
    query_grads, gate_total = pick_rows(
        target, first_returned, second_returned, row_grads.shape[0] // count
    )
    gate_value = jnp.tanh(gate_logit[0])
    gate_grad = (1.0 - gate_value * gate_value) * gate_total[0, 0]
    key_sum, value_sum = (jnp.concatenate(pair, axis=1) for pair in zip(first_sum, second_sum))
    return query_grads, key_sum[None], value_sum[None], weight_grad, gate_grad.reshape(1)


def solution(mesh):
    in_specs = (
        P("rec", "ctx", None),
        P("rec", "ctx", None),
        P("rec", "ctx", None),
        P(),
        P(),
        P(("ctx", "rec"), None),
        P(("ctx", "rec")),
        P(("ctx", "rec")),
        P(("ctx", "rec")),
    )
    out_specs = (
        P(("ctx", "rec"), None),
        P("rec", "ctx", None),
        P("rec", "ctx", None),
        P(("ctx", "rec"), None),
        P(),
    )
    return jax.shard_map(local, mesh=mesh, in_specs=in_specs, out_specs=out_specs, check_vma=False)
```

time: 212 us -> 192 us (0.906)
  waiting for transfers between devices: 71.3 us -> 81.6 us
  other arithmetic: 14.6 us -> 5.39 us
  starting transfers between devices: 61.9 us -> 53.8 us
  local copies, waits for them, and re-layouts: 18.9 us -> 11.5 us
  Pallas kernels: 40.4 us -> 35.3 us
    all_to_all x2 -> x3, waiting for transfers between devices: 0.01 us -> 27.5 us  [exchange(): lax.all_to_all(value.reshape(count, slots // count, width), ('ctx', 'rec'...]
    ppermute x16, starting transfers between devices: 45.2 us -> 29.9 us  [shift(): return lax.ppermute(value, 'ctx', pairs)]
    all_to_all x2 -> x0, waiting for transfers between devices: 11.8 us -> none  [the longest x1 9.23 us: scatter_weight(): parts = lax.all_to_all(term, 'ctx', split_axis=0, concat_axis=0, tiled=True)]
    all_to_all x2 -> x3, starting transfers between devices: 5.63 us -> 15.8 us  [exchange(): lax.all_to_all(value.reshape(count, slots // count, width), ('ctx', 'rec'...]
    all_to_all x2 -> x0, starting transfers between devices: 7.84 us -> none  [the longest x1 4.37 us: local(): lax.all_to_all(gate_row, ('ctx', 'rec'), split_axis=0, concat_axis=0, til...]
    pallas_call x4 -> x9, Pallas kernels: 38.1 us -> 33 us  [the longest x2 24.2 us: attention(): pl.pallas_call(lambda *refs: attention_kernel(len(parts) - 1, pairs, *ref...]
    ppermute x3 -> x6, starting transfers between devices: 3.22 us -> 8.15 us  [the longest x3 5.29 us: sum_blocks(): total = total + lax.ppermute(sent, 'ctx', pairs).astype(jnp.float32)]
    ppermute x3 -> x6, waiting for transfers between devices: 27.2 us -> 24 us  [the longest x3 18.6 us: halve(): lax.ppermute(sent, 'rec', [(i, i ^ 1 << bit) for i in range(rec_count)])]
  transfers between devices with their start and end apart: 23 -> 25, of which waited for: 10 -> 8; matrix products, arithmetic and copies ran while one was open for 11% -> 2% of each run, Pallas kernels for 14% -> 18%
where the time goes in v2:
time: 192 us
  waiting for transfers between devices  81.6 us (42%)
  starting transfers between devices  53.8 us (28%)
  Pallas kernels  35.3 us (18%)
  local copies, waits for them, and re-layouts  11.5 us (6%)
  other arithmetic  5.39 us (3%)
  between operations  4.21 us (2%)
    ppermute x16, waiting for transfers between devices, shift(): return lax.ppermute(value, 'ctx', pairs)  30 us
    ppermute x16, starting transfers between devices, shift(): return lax.ppermute(value, 'ctx', pairs)  29.9 us
    all_to_all x3, waiting for transfers between devices, exchange(): lax.all_to_all(value.reshape(count, slots // count, width), ('ctx', 'rec'...  27.5 us
    pallas_call x2, Pallas kernels, attention(): pl.pallas_call(lambda *refs: attention_kernel(len(parts) - 1, pairs, *ref...  24.2 us
    ppermute x3, waiting for transfers between devices, halve(): lax.ppermute(sent, 'rec', [(i, i ^ 1 << bit) for i in range(rec_count)])  18.6 us
    all_to_all x3, starting transfers between devices, exchange(): lax.all_to_all(value.reshape(count, slots // count, width), ('ctx', 'rec'...  15.8 us
    unnamed x54, local copies, waits for them, and re-layouts  8.13 us
    ppermute x3, waiting for transfers between devices, sum_blocks(): total = total + lax.ppermute(sent, 'ctx', pairs).astype(jnp.float32)  5.42 us
  transfers between devices with their start and end apart: 25, of which 8 were waited for; matrix products, arithmetic and copies ran while one was open for 2% of the time, Pallas kernels for 18%

profile of v2, /device:TPU:0, one launch (start us, length us, event | category | flops | bytes accessed | tf_op | source)
XLA Modules:
  0.0 191.8 jit_solution(8095836925618005485)
XLA Ops:
  2.0 5.1 %collective-permute-start.1 = (bf16[256,640]{1,0:T(8,128)(2,1)S(1)}, bf16[256,640]{1,0:T(8,128)(2,1)S(1)}, u32[]{:S(2)}, u32[]{:S(2)}) collective-permute-start(bf16[256,640]{1,0:T(8,128)(2,1)S(1)} %pad_maximum_fusion.1.refs_6_), channel_id=1, source_target_pairs={{0,24},{8,0},{16,8},{24,16},{1,25},{9,1},{17,9},{25,17},{2,26},{10... | collective-permute-start | bytes 983048 | tf_op jit(solution)/shard_map/ppermute | solution.py:330
  7.8 2.3 %route_prep.1 = (bf16[512,1408]{1,0:T(8,128)(2,1)}, s32[1,512]{1,0:T(1,128)S(1)}) custom-call(s32[1]{0:T(128)S(6)} %copy.17.refs_0_, s32[1,512]{1,0:T(1,128)S(1)} %bitcast.48, s32[1,512]{1,0:T(1,128)S(1)} %bitcast.49, bf16[512,1280]{1,0:T(8,128)(2,1)S(1)} %copy-done.6), custom_call_target="tpu_custom_call" | custom-call | flops 671088640 | bytes 2621440 | tf_op jit(solution)/shard_map/route_prep/pallas_call | solution.py:64
  10.1 6.1 %all-to-all-start = ((bf16[32,16,1408]{2,1,0:T(8,128)(2,1)}), bf16[32,16,1408]{2,1,0:T(8,128)(2,1)S(1)}, u32[]{:S(2)}, u32[]{:S(2)}) async-start(bf16[32,16,1408]{2,1,0:T(8,128)(2,1)} %bitcast.3), calls=%async_computation | async-start | bytes 2883584 | tf_op jit(solution)/shard_map/all_to_all | solution.py:442
  16.2 6.9 %collective-permute-done.ahead_ref.refs_7_ = bf16[256,640]{1,0:T(8,128)(2,1)S(1)} collective-permute-done((bf16[256,640]{1,0:T(8,128)(2,1)S(1)}, bf16[256,640]{1,0:T(8,128)(2,1)S(1)}, u32[]{:S(2)}, u32[]{:S(2)}) %collective-permute-start) | collective-permute-done | bytes 327712 | tf_op jit(solution)/shard_map/ppermute | solution.py:330
  25.5 2.2 %collective-permute-start.3 = (bf16[128,640]{1,0:T(8,128)(2,1)S(1)}, bf16[128,640]{1,0:T(8,128)(2,1)S(1)}, u32[]{:S(2)}, u32[]{:S(2)}) collective-permute-start(bf16[128,640]{1,0:T(8,128)(2,1)S(1)} %get-tuple-element.53), channel_id=1, source_target_pairs={{0,24},{8,0},{16,8},{24,16},{1,25},{9,1},{17,9},{25,17},{2,26},{10... | collective-permute-start | bytes 491528 | tf_op jit(solution)/shard_map/ppermute | solution.py:330
  29.1 27.5 %all-to-all-done = bf16[32,16,1408]{2,1,0:T(8,128)(2,1)S(1)} async-done(((bf16[32,16,1408]{2,1,0:T(8,128)(2,1)}), bf16[32,16,1408]{2,1,0:T(8,128)(2,1)S(1)}, u32[]{:S(2)}, u32[]{:S(2)}) %all-to-all-start) | async-done | bytes 1441824 | tf_op jit(solution)/shard_map/all_to_all | solution.py:442
  56.6 3.0 %collective-permute-start.7 = (bf16[256,640]{1,0:T(8,128)(2,1)}, bf16[256,640]{1,0:T(8,128)(2,1)S(1)}, u32[]{:S(2)}, u32[]{:S(2)}) collective-permute-start(bf16[256,640]{1,0:T(8,128)(2,1)} %pad_maximum_fusion.refs_6_), channel_id=1, source_target_pairs={{0,24},{8,0},{16,8},{24,16},{1,25},{9,1},{17,9},{25,17},{2,26},{10... | collective-permute-start | bytes 983048 | tf_op jit(solution)/shard_map/ppermute | solution.py:330
  63.2 12.0 %attention.2 = (bf16[256,640]{1,0:T(8,128)(2,1)}, bf16[256,640]{1,0:T(8,128)(2,1)}, bf16[256,640]{1,0:T(8,128)(2,1)}, bf16[128,640]{1,0:T(8,128)(2,1)}, bf16[128...) custom-call(f32[1]{0:T(128)S(6)} %copy.16.refs_0_.gate_ref, ...), custom_call_target="tpu_custom_call" | custom-call | flops 12582912000 | bytes 4587520 | tf_op jit(solution)/shard_map/attention/pallas_call | solution.py:227
  76.5 3.8 %collective-permute-start.9 = (bf16[128,640]{1,0:T(8,128)(2,1)S(1)}, bf16[128,640]{1,0:T(8,128)(2,1)S(1)}, u32[]{:S(2)}, u32[]{:S(2)}) collective-permute-start(bf16[128,640]{1,0:T(8,128)(2,1)S(1)} %get-tuple-element.66), channel_id=1, source_target_pairs={{0,24},{8,0},{16,8},{24,16},{1,25},{9,1},{17,9},{25,17},{2,26},{10... | collective-permute-start | bytes 491528 | tf_op jit(solution)/shard_map/ppermute | solution.py:330
  80.3 4.3 %all-to-all-start.1 = ((bf16[32,16,640]{2,1,0:T(8,128)(2,1)}), bf16[32,16,640]{2,1,0:T(8,128)(2,1)}, u32[]{:S(2)}, u32[]{:S(2)}) async-start(bf16[32,16,640]{2,1,0:T(8,128)(2,1)} %bitcast.53), calls=%async_computation.1 | async-start | bytes 1310720 | tf_op jit(solution)/shard_map/all_to_all | solution.py:442
  84.6 3.6 %collective-permute-start.4 = (bf16[128,640]{1,0:T(8,128)(2,1)S(1)}, bf16[128,640]{1,0:T(8,128)(2,1)S(1)}, u32[]{:S(2)}, u32[]{:S(2)}) collective-permute-start(bf16[128,640]{1,0:T(8,128)(2,1)S(1)} %copy-done.22), channel_id=1, source_target_pairs={{0,24},{8,0},{16,8},{24,16},{1,25},{9,1},{17,9},{25,17},{2,26},{10... | collective-permute-start | bytes 491528 | tf_op jit(solution)/shard_map/ppermute | solution.py:330
  89.6 12.2 %attention.3 = (bf16[256,640]{1,0:T(8,128)(2,1)}, bf16[256,640]{1,0:T(8,128)(2,1)}, bf16[256,640]{1,0:T(8,128)(2,1)}, bf16[128,640]{1,0:T(8,128)(2,1)}, bf16[128...) custom-call(f32[1]{0:T(128)S(6)} %copy.16.refs_0_.gate_ref, ...), custom_call_target="tpu_custom_call" | custom-call | flops 12582912000 | bytes 4587520 | tf_op jit(solution)/shard_map/attention/pallas_call | solution.py:227
  101.8 5.1 %collective-permute-done.5.far_values_ref = bf16[128,640]{1,0:T(8,128)(2,1)S(1)} collective-permute-done((bf16[128,640]{1,0:T(8,128)(2,1)S(1)}, bf16[128,640]{1,0:T(8,128)(2,1)S(1)}, u32[]{:S(2)}, u32[]{:S(2)}) %collective-permute-start.5) | collective-permute-done | bytes 163872 | tf_op jit(solution)/shard_map/ppermute | solution.py:330
  110.6 2.0 %weight_term.1 = bf16[1280,1280]{1,0:T(8,128)(2,1)S(1)} custom-call(f32[1]{0:T(128)S(6)} %copy.16.refs_0_.gate_ref, bf16[1280,256]{1,0:T(8,128)(2,1)S(1)} %copy-done.2, bf16[640,256]{1,0:T(8,128)(2,1)S(1)} %copy-done.3, bf16[640,256]{1,0:T(8,128)(2,1)S(1)} %copy-done.4), custom_call_target="tpu_custom_call" | custom-call | flops 838860800 | bytes 4587520 | tf_op jit(solution)/shard_map/weight_term/pallas_call | solution.py:273
  114.0 5.5 %all-to-all-start.2 = ((bf16[32,16,768]{2,1,0:T(8,128)(2,1)}), bf16[32,16,768]{2,1,0:T(8,128)(2,1)}, u32[]{:S(2)}, u32[]{:S(2)}) async-start(bf16[32,16,768]{2,1,0:T(8,128)(2,1)} %bitcast.52), calls=%async_computation.2 | async-start | bytes 1572864 | tf_op jit(solution)/shard_map/all_to_all | solution.py:442
  119.5 3.6 %collective-permute-start.12 = (bf16[128,640]{1,0:T(8,128)(2,1)}, bf16[128,640]{1,0:T(8,128)(2,1)}, u32[]{:S(2)}, u32[]{:S(2)}) collective-permute-start(bf16[128,640]{1,0:T(8,128)(2,1)} %get-tuple-element.82), channel_id=1, source_target_pairs={{0,24},{8,0},{16,8},{24,16},{1,25},{9,1},{17,9},{25,17},{2,26},{10... | collective-permute-start | bytes 491528 | tf_op jit(solution)/shard_map/ppermute | solution.py:330
  126.6 3.9 %collective-permute-start.10 = (bf16[256,640]{1,0:T(8,128)(2,1)S(1)}, bf16[256,640]{1,0:T(8,128)(2,1)S(1)}, u32[]{:S(2)}, u32[]{:S(2)}) collective-permute-start(bf16[256,640]{1,0:T(8,128)(2,1)S(1)} %get-tuple-element.77), channel_id=1, source_target_pairs={{0,24},{8,0},{16,8},{24,16},{1,25},{9,1},{17,9},{25,17},{2,26},{10... | collective-permute-start | bytes 983048 | tf_op jit(solution)/shard_map/ppermute | solution.py:330
  130.5 18.6 %collective-permute-done.15 = bf16[4,2,40,1280]{3,2,1,0:T(8,128)(2,1)S(1)} collective-permute-done((bf16[4,2,40,1280]{3,2,1,0:T(8,128)(2,1)S(1)}, bf16[4,2,40,1280]{3,2,1,0:T(8,128)(2,1)S(1)}, u32[]{:S(2)}, u32[]{:S(2)}) %collective-permute-start.15) | collective-permute-done | bytes 819232 | tf_op jit(solution)/shard_map/ppermute | solution.py:426
  150.7 7.2 %collective-permute-done.11 = bf16[256,640]{1,0:T(8,128)(2,1)S(1)} collective-permute-done((bf16[256,640]{1,0:T(8,128)(2,1)S(1)}, bf16[256,640]{1,0:T(8,128)(2,1)S(1)}, u32[]{:S(2)}, u32[]{:S(2)}) %collective-permute-start.11) | collective-permute-done | bytes 327712 | tf_op jit(solution)/shard_map/ppermute | solution.py:330
  158.1 3.7 %pick_rows.1 = (bf16[512,1280]{1,0:T(8,128)(2,1)}, f32[1,1]{1,0:T(1,128)}) custom-call(s32[1,512]{1,0:T(1,128)S(1)} %get-tuple-element.48.refs_0_, bf16[512,640]{1,0:T(8,128)(2,1)} %bitcast.8.refs_1_, bf16[512,768]{1,0:T(8,128)(2,1)} %bitcast.10.refs_2_), custom_call_target="tpu_custom_call" | custom-call | flops 671088640 | bytes 2621440 | tf_op jit(solution)/shard_map/pick_rows/pallas_call | solution.py:309
  162.6 3.8 %collective-permute-start.19 = (bf16[40,1280]{1,0:T(8,128)(2,1)S(1)}, bf16[40,1280]{1,0:T(8,128)(2,1)S(1)}, u32[]{:S(2)}, u32[]{:S(2)}) collective-permute-start(bf16[40,1280]{1,0:T(8,128)(2,1)S(1)} %get-tuple-element.91), channel_id=1, source_target_pairs={{0,8},{8,0},{16,24},{24,16},{1,9},{9,1},{17,25},{25,17},{2,10},{10... | collective-permute-start | bytes 307208 | tf_op jit(solution)/shard_map/ppermute | solution.py:436
  169.1 2.4 %collective-permute-start.17 = (bf16[256,640]{1,0:T(8,128)(2,1)S(1)}, bf16[256,640]{1,0:T(8,128)(2,1)S(1)}, u32[]{:S(2)}, u32[]{:S(2)}) collective-permute-start(bf16[256,640]{1,0:T(8,128)(2,1)S(1)} %get-tuple-element.87), channel_id=1, source_target_pairs={{0,24},{8,0},{16,8},{24,16},{1,25},{9,1},{17,9},{25,17},{2,26},{10... | collective-permute-start | bytes 983048 | tf_op jit(solution)/shard_map/ppermute | solution.py:330
  174.0 3.4 %collective-permute-done.20 = bf16[40,1280]{1,0:T(8,128)(2,1)S(1)} collective-permute-done((bf16[40,1280]{1,0:T(8,128)(2,1)S(1)}, bf16[40,1280]{1,0:T(8,128)(2,1)S(1)}, u32[]{:S(2)}, u32[]{:S(2)}) %collective-permute-start.20) | collective-permute-done | bytes 102432 | tf_op jit(solution)/shard_map/ppermute | solution.py:436
  178.2 10.8 %collective-permute-done.17 = bf16[256,640]{1,0:T(8,128)(2,1)S(1)} collective-permute-done((bf16[256,640]{1,0:T(8,128)(2,1)S(1)}, bf16[256,640]{1,0:T(8,128)(2,1)S(1)}, u32[]{:S(2)}, u32[]{:S(2)}) %collective-permute-start.17) | collective-permute-done | bytes 327712 | tf_op jit(solution)/shard_map/ppermute | solution.py:330
  (108 shorter events, 28.7 us)
Async XLA Ops:
  2.0 14.1 %collective-permute-start.1 = (bf16[256,640]{1,0:T(8,128)(2,1)S(1)}, bf16[256,640]{1,0:T(8,128)(2,1)S(1)}, u32[]{:S(2)}, u32[]{:S(2)}) collective-permute-start(bf16[256,640]{1,0:T(8,128)(2,1)S(1)} %pad_maximum_fusion.1.refs_6_), channel_id=1, source_target_pairs={{0,24},{8,0},{16,8},{24,16},{1,25},{9,1},{17,9},{25,17},{2,26},{10... | collective-permute-start | bytes 983048 | tf_op jit(solution)/shard_map/ppermute | solution.py:330
  7.1 16.0 %collective-permute-start = (bf16[256,640]{1,0:T(8,128)(2,1)S(1)}, bf16[256,640]{1,0:T(8,128)(2,1)S(1)}, u32[]{:S(2)}, u32[]{:S(2)}) collective-permute-start(bf16[256,640]{1,0:T(8,128)(2,1)S(1)} %pad_maximum_fusion.1.refs_6_), channel_id=1, source_target_pairs={{0,8},{8,16},{16,24},{24,0},{1,9},{9,17},{17,25},{25,1},{2,10},{10... | collective-permute-start | bytes 983048 | tf_op jit(solution)/shard_map/ppermute | solution.py:330
  10.1 46.5 %all-to-all-start = ((bf16[32,16,1408]{2,1,0:T(8,128)(2,1)}), bf16[32,16,1408]{2,1,0:T(8,128)(2,1)S(1)}, u32[]{:S(2)}, u32[]{:S(2)}) async-start(bf16[32,16,1408]{2,1,0:T(8,128)(2,1)} %bitcast.3), calls=%async_computation | async-start | bytes 2883584 | tf_op jit(solution)/shard_map/all_to_all | solution.py:442
  23.8 38.1 %collective-permute-start.2 = (bf16[128,640]{1,0:T(8,128)(2,1)S(1)}, bf16[128,640]{1,0:T(8,128)(2,1)S(1)}, u32[]{:S(2)}, u32[]{:S(2)}) collective-permute-start(bf16[128,640]{1,0:T(8,128)(2,1)S(1)} %get-tuple-element.52), channel_id=1, source_target_pairs={{0,8},{8,16},{16,24},{24,0},{1,9},{9,17},{17,25},{25,1},{2,10},{10... | collective-permute-start | bytes 491528 | tf_op jit(solution)/shard_map/ppermute | solution.py:330
  25.5 36.5 %collective-permute-start.3 = (bf16[128,640]{1,0:T(8,128)(2,1)S(1)}, bf16[128,640]{1,0:T(8,128)(2,1)S(1)}, u32[]{:S(2)}, u32[]{:S(2)}) collective-permute-start(bf16[128,640]{1,0:T(8,128)(2,1)S(1)} %get-tuple-element.53), channel_id=1, source_target_pairs={{0,24},{8,0},{16,8},{24,16},{1,25},{9,1},{17,9},{25,17},{2,26},{10... | collective-permute-start | bytes 491528 | tf_op jit(solution)/shard_map/ppermute | solution.py:330
  56.6 18.5 %collective-permute-start.7 = (bf16[256,640]{1,0:T(8,128)(2,1)}, bf16[256,640]{1,0:T(8,128)(2,1)S(1)}, u32[]{:S(2)}, u32[]{:S(2)}) collective-permute-start(bf16[256,640]{1,0:T(8,128)(2,1)} %pad_maximum_fusion.refs_6_), channel_id=1, source_target_pairs={{0,24},{8,0},{16,8},{24,16},{1,25},{9,1},{17,9},{25,17},{2,26},{10... | collective-permute-start | bytes 983048 | tf_op jit(solution)/shard_map/ppermute | solution.py:330
  59.6 15.6 %collective-permute-start.6 = (bf16[256,640]{1,0:T(8,128)(2,1)}, bf16[256,640]{1,0:T(8,128)(2,1)}, u32[]{:S(2)}, u32[]{:S(2)}) collective-permute-start(bf16[256,640]{1,0:T(8,128)(2,1)} %pad_maximum_fusion.refs_6_), channel_id=1, source_target_pairs={{0,8},{8,16},{16,24},{24,0},{1,9},{9,17},{17,25},{25,1},{2,10},{10... | collective-permute-start | bytes 983048 | tf_op jit(solution)/shard_map/ppermute | solution.py:330
  76.4 11.8 %collective-permute-start.8 = (bf16[128,640]{1,0:T(8,128)(2,1)S(1)}, bf16[128,640]{1,0:T(8,128)(2,1)S(1)}, u32[]{:S(2)}, u32[]{:S(2)}) collective-permute-start(bf16[128,640]{1,0:T(8,128)(2,1)S(1)} %get-tuple-element.65), channel_id=1, source_target_pairs={{0,8},{8,16},{16,24},{24,0},{1,9},{9,17},{17,25},{25,1},{2,10},{10... | collective-permute-start | bytes 491528 | tf_op jit(solution)/shard_map/ppermute | solution.py:330
  76.5 11.8 %collective-permute-start.9 = (bf16[128,640]{1,0:T(8,128)(2,1)S(1)}, bf16[128,640]{1,0:T(8,128)(2,1)S(1)}, u32[]{:S(2)}, u32[]{:S(2)}) collective-permute-start(bf16[128,640]{1,0:T(8,128)(2,1)S(1)} %get-tuple-element.66), channel_id=1, source_target_pairs={{0,24},{8,0},{16,8},{24,16},{1,25},{9,1},{17,9},{25,17},{2,26},{10... | collective-permute-start | bytes 491528 | tf_op jit(solution)/shard_map/ppermute | solution.py:330
  80.3 32.3 %all-to-all-start.1 = ((bf16[32,16,640]{2,1,0:T(8,128)(2,1)}), bf16[32,16,640]{2,1,0:T(8,128)(2,1)}, u32[]{:S(2)}, u32[]{:S(2)}) async-start(bf16[32,16,640]{2,1,0:T(8,128)(2,1)} %bitcast.53), calls=%async_computation.1 | async-start | bytes 1310720 | tf_op jit(solution)/shard_map/all_to_all | solution.py:442
  84.6 17.2 %collective-permute-start.4 = (bf16[128,640]{1,0:T(8,128)(2,1)S(1)}, bf16[128,640]{1,0:T(8,128)(2,1)S(1)}, u32[]{:S(2)}, u32[]{:S(2)}) collective-permute-start(bf16[128,640]{1,0:T(8,128)(2,1)S(1)} %copy-done.22), channel_id=1, source_target_pairs={{0,24},{8,0},{16,8},{24,16},{1,25},{9,1},{17,9},{25,17},{2,26},{10... | collective-permute-start | bytes 491528 | tf_op jit(solution)/shard_map/ppermute | solution.py:330
  88.2 18.6 %collective-permute-start.5 = (bf16[128,640]{1,0:T(8,128)(2,1)S(1)}, bf16[128,640]{1,0:T(8,128)(2,1)S(1)}, u32[]{:S(2)}, u32[]{:S(2)}) collective-permute-start(bf16[128,640]{1,0:T(8,128)(2,1)S(1)} %copy-done.21), channel_id=1, source_target_pairs={{0,8},{8,16},{16,24},{24,0},{1,9},{9,17},{17,25},{25,1},{2,10},{10... | collective-permute-start | bytes 491528 | tf_op jit(solution)/shard_map/ppermute | solution.py:330
  113.9 9.1 %collective-permute-start.14 = (bf16[4,4,40,1280]{3,2,1,0:T(8,128)(2,1)}, bf16[4,4,40,1280]{3,2,1,0:T(8,128)(2,1)}, u32[]{:S(2)}, u32[]{:S(2)}) collective-permute-start(bf16[4,4,40,1280]{3,2,1,0:T(8,128)(2,1)} %dynamic-slice_bitcast_fusion), channel_id=1, source_target_pairs={{0,1},{1,0},{2,3},{3,2},{4,5},{5,4},{6,7},{7,6},{8,9},{9,8},{10,11... | collective-permute-start | bytes 4915208 | tf_op jit(solution)/shard_map/ppermute | solution.py:426
  114.0 44.1 %all-to-all-start.2 = ((bf16[32,16,768]{2,1,0:T(8,128)(2,1)}), bf16[32,16,768]{2,1,0:T(8,128)(2,1)}, u32[]{:S(2)}, u32[]{:S(2)}) async-start(bf16[32,16,768]{2,1,0:T(8,128)(2,1)} %bitcast.52), calls=%async_computation.2 | async-start | bytes 1572864 | tf_op jit(solution)/shard_map/all_to_all | solution.py:442
  119.5 43.1 %collective-permute-start.12 = (bf16[128,640]{1,0:T(8,128)(2,1)}, bf16[128,640]{1,0:T(8,128)(2,1)}, u32[]{:S(2)}, u32[]{:S(2)}) collective-permute-start(bf16[128,640]{1,0:T(8,128)(2,1)} %get-tuple-element.82), channel_id=1, source_target_pairs={{0,24},{8,0},{16,8},{24,16},{1,25},{9,1},{17,9},{25,17},{2,26},{10... | collective-permute-start | bytes 491528 | tf_op jit(solution)/shard_map/ppermute | solution.py:330
  123.1 39.5 %collective-permute-start.13 = (bf16[128,640]{1,0:T(8,128)(2,1)}, bf16[128,640]{1,0:T(8,128)(2,1)}, u32[]{:S(2)}, u32[]{:S(2)}) collective-permute-start(bf16[128,640]{1,0:T(8,128)(2,1)} %get-tuple-element.83), channel_id=1, source_target_pairs={{0,8},{8,16},{16,24},{24,0},{1,9},{9,17},{17,25},{25,1},{2,10},{10... | collective-permute-start | bytes 491528 | tf_op jit(solution)/shard_map/ppermute | solution.py:330
  125.0 24.1 %collective-permute-start.15 = (bf16[4,2,40,1280]{3,2,1,0:T(8,128)(2,1)S(1)}, bf16[4,2,40,1280]{3,2,1,0:T(8,128)(2,1)S(1)}, u32[]{:S(2)}, u32[]{:S(2)}) collective-permute-start(bf16[4,2,40,1280]{3,2,1,0:T(8,128)(2,1)S(1)} %dynamic-slice_bitcast_fusion.1), channel_id=1, source_target_pairs={{0,2},{1,3},{2,0},{3,1},{4,6},{5,7},{6,4},{7,5},{8,10},{9,11},{10,... | collective-permute-start | bytes 2457608 | tf_op jit(solution)/shard_map/ppermute | solution.py:426
  126.6 24.0 %collective-permute-start.10 = (bf16[256,640]{1,0:T(8,128)(2,1)S(1)}, bf16[256,640]{1,0:T(8,128)(2,1)S(1)}, u32[]{:S(2)}, u32[]{:S(2)}) collective-permute-start(bf16[256,640]{1,0:T(8,128)(2,1)S(1)} %get-tuple-element.77), channel_id=1, source_target_pairs={{0,24},{8,0},{16,8},{24,16},{1,25},{9,1},{17,9},{25,17},{2,26},{10... | collective-permute-start | bytes 983048 | tf_op jit(solution)/shard_map/ppermute | solution.py:330
  130.5 27.4 %collective-permute-start.11 = (bf16[256,640]{1,0:T(8,128)(2,1)S(1)}, bf16[256,640]{1,0:T(8,128)(2,1)S(1)}, u32[]{:S(2)}, u32[]{:S(2)}) collective-permute-start(bf16[256,640]{1,0:T(8,128)(2,1)S(1)} %get-tuple-element.78), channel_id=1, source_target_pairs={{0,8},{8,16},{16,24},{24,0},{1,9},{9,17},{17,25},{25,1},{2,10},{10... | collective-permute-start | bytes 983048 | tf_op jit(solution)/shard_map/ppermute | solution.py:330
  149.3 13.1 %collective-permute-start.16 = (bf16[4,1,40,1280]{3,2,1,0:T(8,128)(2,1)S(1)}, bf16[4,1,40,1280]{3,2,1,0:T(8,128)(2,1)S(1)}, u32[]{:S(2)}, u32[]{:S(2)}) collective-permute-start(bf16[4,1,40,1280]{3,2,1,0:T(8,128)(2,1)S(1)} %constant_dynamic-slice_fusion), channel_id=1, source_target_pairs={{0,4},{1,5},{2,6},{3,7},{4,0},{5,1},{6,2},{7,3},{8,12},{9,13},{10,... | collective-permute-start | bytes 1228808 | tf_op jit(solution)/shard_map/ppermute | solution.py:426
  162.6 9.4 %collective-permute-start.19 = (bf16[40,1280]{1,0:T(8,128)(2,1)S(1)}, bf16[40,1280]{1,0:T(8,128)(2,1)S(1)}, u32[]{:S(2)}, u32[]{:S(2)}) collective-permute-start(bf16[40,1280]{1,0:T(8,128)(2,1)S(1)} %get-tuple-element.91), channel_id=1, source_target_pairs={{0,8},{8,0},{16,24},{24,16},{1,9},{9,1},{17,25},{25,17},{2,10},{10... | collective-permute-start | bytes 307208 | tf_op jit(solution)/shard_map/ppermute | solution.py:436
  167.6 9.8 %collective-permute-start.20 = (bf16[40,1280]{1,0:T(8,128)(2,1)S(1)}, bf16[40,1280]{1,0:T(8,128)(2,1)S(1)}, u32[]{:S(2)}, u32[]{:S(2)}) collective-permute-start(bf16[40,1280]{1,0:T(8,128)(2,1)S(1)} %get-tuple-element.93), channel_id=1, source_target_pairs={{0,16},{8,24},{16,0},{24,8},{1,17},{9,25},{17,1},{25,9},{2,18},{10... | collective-permute-start | bytes 307208 | tf_op jit(solution)/shard_map/ppermute | solution.py:436
  169.1 19.9 %collective-permute-start.17 = (bf16[256,640]{1,0:T(8,128)(2,1)S(1)}, bf16[256,640]{1,0:T(8,128)(2,1)S(1)}, u32[]{:S(2)}, u32[]{:S(2)}) collective-permute-start(bf16[256,640]{1,0:T(8,128)(2,1)S(1)} %get-tuple-element.87), channel_id=1, source_target_pairs={{0,24},{8,0},{16,8},{24,16},{1,25},{9,1},{17,9},{25,17},{2,26},{10... | collective-permute-start | bytes 983048 | tf_op jit(solution)/shard_map/ppermute | solution.py:330
  171.4 17.5 %collective-permute-start.18 = (bf16[256,640]{1,0:T(8,128)(2,1)S(1)}, bf16[256,640]{1,0:T(8,128)(2,1)S(1)}, u32[]{:S(2)}, u32[]{:S(2)}) collective-permute-start(bf16[256,640]{1,0:T(8,128)(2,1)S(1)} %get-tuple-element.88), channel_id=1, source_target_pairs={{0,8},{8,16},{16,24},{24,0},{1,9},{9,17},{17,25},{25,1},{2,10},{10... | collective-permute-start | bytes 983048 | tf_op jit(solution)/shard_map/ppermute | solution.py:330
  (28 other events, 168.8 us)

commit v3 on v2

--- a/solution.py
+++ b/solution.py
@@ -12,6 +12,7 @@
 ATTENTION_COST = 150
 FAR_COST = 300000
 STEP_COST = 74000
+TOTAL_COST = 150000
 NT = (((1,), (1,)), ((), ()))
 NN = (((1,), (0,)), ((), ()))
 
@@ -121,8 +122,8 @@
     )(recv)
 
 
-def attend(gate_ref, query_ref, weight_ref, rows_ref, index_ref, keys, values,
-           attn_ref, back_ref, gate_out_ref):
+def attend(gate_ref, query_ref, weight_ref, rows_ref, rows_t_ref, index_ref, keys, values,
+           product_ref, back_ref, gate_out_ref):
     rows = query_ref.shape[0]
     slots = index_ref.shape[0]
     root = HEAD_DIM ** -0.5
@@ -138,6 +139,7 @@
     key_term = None
     value_term = None
     query_parts = []
+    attn_parts = []
     gate_sum = None
     for head in range(2):
         span = slice(head * HEAD_DIM, (head + 1) * HEAD_DIM)
@@ -150,7 +152,7 @@
         probs = shifted * inverse
         probs_low = probs.astype(jnp.bfloat16)
         attn_h = mm(values_tr[span, :], probs_low).astype(jnp.bfloat16)
-        attn_ref[span, :] = attn_h
+        attn_parts.append(attn_h)
         attn_wide = attn_h.astype(jnp.float32)
         delta = jnp.sum(grad_t[span, :].astype(jnp.float32) * attn_wide, axis=0, keepdims=True)
         gate_h = jnp.sum(upstream[span, :] * attn_wide, axis=0, keepdims=True)
@@ -163,6 +165,8 @@
         gate_sum = gate_h if head == 0 else gate_sum + gate_h
         query_parts.append(mm(keys_tr[span, :], dscore) * root)
     gate_out_ref[...] += gate_sum
+    product = mm(rows_t_ref[...], jnp.concatenate(attn_parts, axis=0), NT)
+    product_ref[...] = (gate * product).astype(jnp.bfloat16)
     query_grad = jnp.transpose(jnp.concatenate(query_parts, axis=0).astype(jnp.bfloat16))
     index = index_ref[...][:, :1].astype(jnp.float32)
     place = index == (iota((slots, rows), 1) + 1).astype(jnp.float32)
@@ -181,9 +185,9 @@
 
 
 def attention_kernel(blocks, pairs, gate_ref, before_ref, query_ref, weight_ref, rows_ref,
-                     index_ref, *refs):
+                     rows_t_ref, index_ref, *refs):
     parts, outs = refs[: blocks + 1], refs[blocks + 1 : 2 * blocks + 2]
-    attn_ref, back_ref, gate_out_ref = refs[2 * blocks + 2 :]
+    product_ref, back_ref, gate_out_ref = refs[2 * blocks + 2 :]
     step = pl.program_id(0)
 
     @pl.when(step == 0)
@@ -198,8 +202,8 @@
             [part[chunk:] for part in parts[:-2]] + [parts[-1][...]], axis=0
         )
         key_term, value_term = attend(
-            gate_ref, query_ref, weight_ref, rows_ref, index_ref, keys, values,
-            attn_ref, back_ref, gate_out_ref,
+            gate_ref, query_ref, weight_ref, rows_ref, rows_t_ref, index_ref, keys, values,
+            product_ref, back_ref, gate_out_ref,
         )
         for number, out in enumerate(outs[:-2]):
             span = slice(number * chunk, (number + 1) * chunk)
@@ -214,7 +218,8 @@
         back_ref[...] = gate_lanes(total, back_ref.shape)
 
 
-def attention(gate_logit, before, queries, out_weight, grad_rows, recv, parts, first_pair, extra):
+def attention(gate_logit, before, queries, out_weight, grad_rows, rows_t, recv, parts, first_pair,
+              extra):
     rows, width = queries.shape
     slots = recv.shape[0]
     span = parts[0].shape[1]
@@ -229,7 +234,7 @@
         grid=(pairs + extra,),
         out_shape=(
             *[jax.ShapeDtypeStruct(part.shape, jnp.bfloat16) for part in parts],
-            jax.ShapeDtypeStruct((span, rows), jnp.bfloat16),
+            jax.ShapeDtypeStruct((width, span), jnp.bfloat16),
             jax.ShapeDtypeStruct((slots, span + extra * LANES), jnp.bfloat16),
             jax.ShapeDtypeStruct((1, rows), jnp.float32),
         ),
@@ -239,12 +244,13 @@
             pl.BlockSpec((rows, LANES), lambda i: (0, at(i) + first_pair)),
             pl.BlockSpec((LANES, width), lambda i: (at(i) + first_pair, 0)),
             pl.BlockSpec((rows, width), whole),
+            pl.BlockSpec((width, rows), whole),
             pl.BlockSpec((slots, LANES), lambda i: (0, width // LANES)),
             *part_specs,
         ],
         out_specs=(
             *part_specs,
-            pl.BlockSpec((LANES, rows), lambda i: (at(i), 0)),
+            pl.BlockSpec((width, LANES), columns),
             pl.BlockSpec((slots, LANES), lambda i: (0, i)),
             pl.BlockSpec((1, rows), whole),
         ),
@@ -255,40 +261,8 @@
             bytes_accessed=8 * tokens * span + 12 * rows * span,
             transcendentals=rows * tokens * span // HEAD_DIM,
         ),
-    )(gate_logit, before, queries, out_weight, grad_rows, recv, *parts)
+    )(gate_logit, before, queries, out_weight, grad_rows, rows_t, recv, *parts)
     return outs[: len(parts)], *outs[len(parts) :]
-
-
-def weight_kernel(gate_ref, rows_t_ref, first_ref, second_ref, out_ref):
-    gate = jnp.tanh(jnp.full((1, LANES), gate_ref[0], jnp.float32))[:, :1]
-    half = first_ref.shape[0]
-    for number, attn_ref in enumerate((first_ref, second_ref)):
-        block = mm(rows_t_ref[...], attn_ref[...], NT)
-        out_ref[:, number * half : (number + 1) * half] = (gate * block).astype(jnp.bfloat16)
-
-
-def weight_term(gate_logit, rows_t, first_attn, second_attn):
-    width, rows = rows_t.shape
-    steps = 5
-    return pl.pallas_call(
-        weight_kernel,
-        grid=(steps,),
-        out_shape=jax.ShapeDtypeStruct((width, width), jnp.bfloat16),
-        in_specs=[
-            pl.BlockSpec(memory_space=pltpu.SMEM),
-            pl.BlockSpec((width // steps, rows), lambda i: (i, 0)),
-            pl.BlockSpec((width // 2, rows), lambda i: (0, 0)),
-            pl.BlockSpec((width // 2, rows), lambda i: (0, 0)),
-        ],
-        out_specs=pl.BlockSpec((width // steps, width), lambda i: (i, 0)),
-        compiler_params=params(),
-        name="weight_term",
-        cost_estimate=pl.CostEstimate(
-            flops=2 * rows * width * width,
-            bytes_accessed=2 * width * width + 4 * rows * width,
-            transcendentals=0,
-        ),
-    )(gate_logit, rows_t, first_attn, second_attn)
 
 
 def pick_kernel(pair_cap, target_ref, first_ref, second_ref, out_ref, gate_ref):
@@ -375,55 +349,98 @@
     return shift(parts[-2], -1), shift(parts[-1], 1)
 
 
-def step_kernel(back_ref, forth_ref, far_keys_ref, far_values_ref, back_out_ref, forth_out_ref):
-    half = far_keys_ref.shape[0]
-    back_out_ref[:half] = add(back_ref[:half], far_keys_ref[...])
-    back_out_ref[half:] = back_ref[half:]
-    forth_out_ref[:half] = forth_ref[:half]
-    forth_out_ref[half:] = add(forth_ref[half:], far_values_ref[...])
-
-
-def step_sums(back, forth, far_keys, far_values):
+def step_kernel(*refs):
+    back_ref, forth_ref = refs[-2:]
+    rows = refs[0].shape[0]
+    half = rows // 2
+    for number in range(2):
+        back, forth, far_keys, far_values = refs[4 * number : 4 * number + 4]
+        first = number * rows
+        middle = first + half
+        back_ref[first:middle] = add(back[:half], far_keys[...])
+        back_ref[middle : first + rows] = back[half:]
+        forth_ref[first:middle] = forth[:half]
+        forth_ref[middle : first + rows] = add(forth[half:], far_values[...])
+
+
+def step_sums(halves):
     vmem = pl.BlockSpec(memory_space=pltpu.VMEM)
+    back = halves[0][0]
+    shape = jax.ShapeDtypeStruct((2 * back.shape[0], back.shape[1]), back.dtype)
     return pl.pallas_call(
         step_kernel,
-        out_shape=(jax.ShapeDtypeStruct(back.shape, back.dtype),) * 2,
+        out_shape=(shape, shape),
+        in_specs=[vmem] * 8,
+        out_specs=(vmem, vmem),
+        compiler_params=params(),
+        name="step_sums",
+        cost_estimate=pl.CostEstimate(
+            flops=STEP_COST * back.size, bytes_accessed=16 * back.size, transcendentals=0
+        ),
+    )(*halves[0], *halves[1])
+
+
+def total_kernel(first_ref, second_ref, back_ref, forth_ref, key_ref, value_ref):
+    rows, span = first_ref.shape
+    half = rows // 2
+    for number, own_ref in enumerate((first_ref, second_ref)):
+        moved = slice(number * rows, (number + 1) * rows)
+        total = own_ref[...].astype(jnp.float32) + back_ref[moved].astype(jnp.float32)
+        total = (total + forth_ref[moved].astype(jnp.float32)).astype(jnp.bfloat16)
+        columns = slice(number * span, (number + 1) * span)
+        key_ref[:, columns] = total[:half]
+        value_ref[:, columns] = total[half:]
+
+
+def total_sums(first, second, back, forth):
+    vmem = pl.BlockSpec(memory_space=pltpu.VMEM)
+    shape = jax.ShapeDtypeStruct((first.shape[0] // 2, 2 * first.shape[1]), first.dtype)
+    return pl.pallas_call(
+        total_kernel,
+        out_shape=(shape, shape),
         in_specs=[vmem] * 4,
         out_specs=(vmem, vmem),
         compiler_params=params(),
-        name="step_sums",
-        cost_estimate=pl.CostEstimate(
-            flops=STEP_COST * back.size,
-            bytes_accessed=8 * back.size,
-            transcendentals=0,
-        ),
-    )(back, forth, far_keys, far_values)
-
-
-def finish_sums(parts, far_keys, far_values):
-    half = far_keys.shape[0]
+        name="total_sums",
+        cost_estimate=pl.CostEstimate(
+            flops=TOTAL_COST * first.size, bytes_accessed=16 * first.size, transcendentals=0
+        ),
+    )(first, second, back, forth)
+
+
+def ring_sums(first_terms, second_terms, first_far, second_far):
     steps = lax.axis_size("ctx") // 2 - 1
-    back, forth = step_sums(parts[2 * steps - 1], parts[2 * steps], far_keys, far_values)
+    far = 2 * steps - 1
+    back, forth = step_sums(
+        [
+            (terms[far], terms[far + 1], *moved)
+            for terms, moved in ((first_terms, first_far), (second_terms, second_far))
+        ]
+    )
     for step in range(steps, 0, -1):
         if step < steps:
-            back = add(parts[2 * step - 1], back)
-            forth = add(parts[2 * step], forth)
+            near = 2 * step - 1
+            back, forth = (
+                add(jnp.concatenate([first_terms[at], second_terms[at]], axis=0), moved)
+                for at, moved in ((near, back), (near + 1, forth))
+            )
         back = shift(back, -1)
         forth = shift(forth, 1)
-    own = parts[0].astype(jnp.float32)
-    total = own + back.astype(jnp.float32) + forth.astype(jnp.float32)
-    total = total.astype(jnp.bfloat16)
-    return total[:half], total[half:]
-
-
-def halve(term, bit):
+    return total_sums(first_terms[0], second_terms[0], back, forth)
+
+
+def halve(term, bit, lowest):
     rec_count = lax.axis_size("rec")
     ctx_count, left, rows, width = term.shape
-    term = term.reshape(ctx_count, left // 2, 2, rows, width)
+    pair = (left // 2, 2) if lowest else (2, left // 2)
+    term = term.reshape(ctx_count, *pair, rows, width)
     mine = (lax.axis_index("rec") >> bit) & 1
-    sent = lax.dynamic_index_in_dim(term, 1 - mine, 2, keepdims=False)
-    kept = lax.dynamic_index_in_dim(term, mine, 2, keepdims=False)
-    return add(kept, lax.ppermute(sent, "rec", [(i, i ^ (1 << bit)) for i in range(rec_count)]))
+
+    def half(which):
+        return lax.dynamic_index_in_dim(term, which, 2 if lowest else 1, keepdims=False)
+
+    got = lax.ppermute(half(1 - mine), "rec", [(i, i ^ (1 << bit)) for i in range(rec_count)])
+    return add(half(mine), got)
 
 
 def sum_blocks(term):
@@ -474,38 +491,40 @@
     recv, second = tie((recv, second))
     second_parts = gather_near(second)
     grad_rows, rows_t = unpack_rows(recv, rows)
-    common = (queries[0], out_weight, grad_rows, recv)
-    first_terms, first_attn, first_back, gate_part = attention(
+    common = (queries[0], out_weight, grad_rows, rows_t, recv)
+    first_terms, first_product, first_back, gate_part = attention(
         gate_logit, jnp.zeros((1, rows), jnp.float32), *common, first_parts, 0, 0
     )
     first_far = start_sums(first_terms)
     first_returned = exchange(first_back, count)
     second_parts, gate_part = tie((second_parts, gate_part))
+    blocks, devices = lax.axis_size("ctx"), lax.axis_size("rec")
+    shape = (blocks, devices, width // count, half)
+    first_product = halve(first_product.reshape(shape), 0, True)
     second_parts = gather_far(second_parts, 1)
-    second_terms, second_attn, second_back, _ = attention(
+    second_terms, second_product, second_back, _ = attention(
         gate_logit, gate_part, *common, second_parts, half // LANES, 1
     )
     second_far = start_sums(second_terms)
-    first_far, second_attn = tie((first_far, second_attn))
-    product = weight_term(gate_logit, rows_t, first_attn, second_attn)
-    first_returned, product = tie((first_returned, product))
-    blocks, devices = lax.axis_size("ctx"), lax.axis_size("rec")
-    product = halve(product.reshape(blocks, devices, width // count, width), 0)
+    first_far, second_product, first_returned, first_product = tie(
+        (first_far, second_product, first_returned, first_product)
+    )
+    second_product = halve(second_product.reshape(shape), 0, True)
     second_returned = exchange(second_back, count)
-    first_sum = finish_sums(first_terms, *first_far)
     bit = 1
-    while product.shape[1] > 1:
-        product = halve(product, bit)
+    while first_product.shape[1] > 1:
+        opposite = devices.bit_length() - 1 - bit
+        first_product = halve(first_product, bit, True)
+        second_product = halve(second_product, opposite, False)
         bit += 1
-    second_far, weight_chips = tie((second_far, product[:, 0]))
-    second_sum = finish_sums(second_terms, *second_far)
+    weight_chips = jnp.concatenate([first_product[:, 0], second_product[:, 0]], axis=2)
+    key_sum, value_sum = ring_sums(first_terms, second_terms, first_far, second_far)
     weight_grad = sum_blocks(weight_chips)
     query_grads, gate_total = pick_rows(
         target, first_returned, second_returned, row_grads.shape[0] // count
     )
     gate_value = jnp.tanh(gate_logit[0])
     gate_grad = (1.0 - gate_value * gate_value) * gate_total[0, 0]
-    key_sum, value_sum = (jnp.concatenate(pair, axis=1) for pair in zip(first_sum, second_sum))
     return query_grads, key_sum[None], value_sum[None], weight_grad, gate_grad.reshape(1)
 
 

time: 192 us -> 178 us (0.927)
  waiting for transfers between devices: 81.6 us -> 74.2 us
  starting transfers between devices: 53.8 us -> 47.4 us
    ppermute x16 -> x14, waiting for transfers between devices: 30 us -> 21 us  [shift(): return lax.ppermute(value, 'ctx', pairs)]
    ppermute x16 -> x14, starting transfers between devices: 29.9 us -> 24.2 us  [shift(): return lax.ppermute(value, 'ctx', pairs)]
    unnamed x54 -> x46, local copies, waits for them, and re-layouts: 8.13 us -> 3.84 us
    all_to_all x3, waiting for transfers between devices: 27.5 us -> 31.7 us  [exchange(): lax.all_to_all(value.reshape(count, slots // count, width), ('ctx', 'rec'...]
    squeeze x4 -> x6, local copies, waits for them, and re-layouts: 1.46 us -> 5.37 us  [half(): lax.dynamic_index_in_dim(term, which, 2 if lowest else 1, keepdims=False)]
    ppermute x3 -> x6, waiting for transfers between devices: 18.6 us -> 15.3 us  [halve(): lax.ppermute(half(1 - mine), 'rec', [(i, i ^ 1 << bit) for i in range(rec...]
    ppermute x3 -> x6, starting transfers between devices: 2.86 us -> 5.9 us  [halve(): lax.ppermute(half(1 - mine), 'rec', [(i, i ^ 1 << bit) for i in range(rec...]
    all_to_all x3, starting transfers between devices: 15.8 us -> 12.8 us  [exchange(): lax.all_to_all(value.reshape(count, slots // count, width), ('ctx', 'rec'...]
  transfers between devices with their start and end apart: 25 -> 26, of which waited for: 8 -> 9; matrix products, arithmetic and copies ran while one was open for 2% -> 5% of each run, Pallas kernels for 18% -> 19%
where the time goes in v3:
time: 178 us; the launch traced here: 177 us
  waiting for transfers between devices  74.2 us (42%)
  starting transfers between devices  47.4 us (27%)
  Pallas kernels  33.9 us (19%)
  local copies, waits for them, and re-layouts  11.2 us (6%)
  other arithmetic  6.03 us (3%)
  between operations  4.2 us (2%)
    all_to_all x3, waiting for transfers between devices, exchange(): lax.all_to_all(value.reshape(count, slots // count, width), ('ctx', 'rec'...  31.7 us
    pallas_call x2, Pallas kernels, attention(): pl.pallas_call(lambda *refs: attention_kernel(len(parts) - 1, pairs, *ref...  26.3 us
    ppermute x14, starting transfers between devices, shift(): return lax.ppermute(value, 'ctx', pairs)  24.2 us
    ppermute x14, waiting for transfers between devices, shift(): return lax.ppermute(value, 'ctx', pairs)  21 us
    ppermute x6, waiting for transfers between devices, halve(): lax.ppermute(half(1 - mine), 'rec', [(i, i ^ 1 << bit) for i in range(rec...  15.3 us
    all_to_all x3, starting transfers between devices, exchange(): lax.all_to_all(value.reshape(count, slots // count, width), ('ctx', 'rec'...  12.8 us
    ppermute x3, waiting for transfers between devices, sum_blocks(): total = total + lax.ppermute(sent, 'ctx', pairs).astype(jnp.float32)  6.13 us
    ppermute x6, starting transfers between devices, halve(): lax.ppermute(half(1 - mine), 'rec', [(i, i ^ 1 << bit) for i in range(rec...  5.9 us
  transfers between devices with their start and end apart: 26, of which 9 were waited for; matrix products, arithmetic and copies ran while one was open for 5% of the time, Pallas kernels for 19%

profile of v3, /device:TPU:0, one launch (start us, length us, event | category | flops | bytes accessed | tf_op | source)
XLA Modules:
  0.0 176.9 jit_solution(17834654731334188140)
XLA Ops:
  2.0 3.1 %collective-permute-start = (bf16[256,640]{1,0:T(8,128)(2,1)S(1)}, bf16[256,640]{1,0:T(8,128)(2,1)S(1)}, u32[]{:S(2)}, u32[]{:S(2)}) collective-permute-start(bf16[256,640]{1,0:T(8,128)(2,1)S(1)} %pad_maximum_fusion.1.refs_7_), channel_id=1, source_target_pairs={{0,8},{8,16},{16,24},{24,0},{1,9},{9,17},{17,25},{25,1},{2,10},{10... | collective-permute-start | bytes 983048 | tf_op jit(solution)/shard_map/ppermute | solution.py:304
  5.1 2.1 %collective-permute-start.1 = (bf16[256,640]{1,0:T(8,128)(2,1)S(1)}, bf16[256,640]{1,0:T(8,128)(2,1)S(1)}, u32[]{:S(2)}, u32[]{:S(2)}) collective-permute-start(bf16[256,640]{1,0:T(8,128)(2,1)S(1)} %pad_maximum_fusion.1.refs_7_), channel_id=1, source_target_pairs={{0,24},{8,0},{16,8},{24,16},{1,25},{9,1},{17,9},{25,17},{2,26},{10... | collective-permute-start | bytes 983048 | tf_op jit(solution)/shard_map/ppermute | solution.py:304
  7.9 2.3 %route_prep.1 = (bf16[512,1408]{1,0:T(8,128)(2,1)}, s32[1,512]{1,0:T(1,128)S(1)}) custom-call(s32[1]{0:T(128)S(6)} %copy.19.refs_0_, s32[1,512]{1,0:T(1,128)S(1)} %bitcast.62, s32[1,512]{1,0:T(1,128)S(1)} %bitcast.63, bf16[512,1280]{1,0:T(8,128)(2,1)S(1)} %copy-done.2), custom_call_target="tpu_custom_call" | custom-call | flops 671088640 | bytes 2621440 | tf_op jit(solution)/shard_map/route_prep/pallas_call | solution.py:65
  10.1 4.2 %all-to-all-start = ((bf16[32,16,1408]{2,1,0:T(8,128)(2,1)}), bf16[32,16,1408]{2,1,0:T(8,128)(2,1)S(1)}, u32[]{:S(2)}, u32[]{:S(2)}) async-start(bf16[32,16,1408]{2,1,0:T(8,128)(2,1)} %bitcast.3), calls=%async_computation | async-start | bytes 2883584 | tf_op jit(solution)/shard_map/all_to_all | solution.py:459
  15.7 6.3 %collective-permute-done.1.behind_ref.refs_9_ = bf16[256,640]{1,0:T(8,128)(2,1)S(1)} collective-permute-done((bf16[256,640]{1,0:T(8,128)(2,1)S(1)}, bf16[256,640]{1,0:T(8,128)(2,1)S(1)}, u32[]{:S(2)}, u32[]{:S(2)}) %collective-permute-start.1) | collective-permute-done | bytes 327712 | tf_op jit(solution)/shard_map/ppermute | solution.py:304
  23.2 3.3 %collective-permute-start.3 = (bf16[128,640]{1,0:T(8,128)(2,1)S(1)}, bf16[128,640]{1,0:T(8,128)(2,1)S(1)}, u32[]{:S(2)}, u32[]{:S(2)}) collective-permute-start(bf16[128,640]{1,0:T(8,128)(2,1)S(1)} %get-tuple-element.51), channel_id=1, source_target_pairs={{0,24},{8,0},{16,8},{24,16},{1,25},{9,1},{17,9},{25,17},{2,26},{10... | collective-permute-start | bytes 491528 | tf_op jit(solution)/shard_map/ppermute | solution.py:304
  28.0 28.5 %all-to-all-done = bf16[32,16,1408]{2,1,0:T(8,128)(2,1)S(1)} async-done(((bf16[32,16,1408]{2,1,0:T(8,128)(2,1)}), bf16[32,16,1408]{2,1,0:T(8,128)(2,1)S(1)}, u32[]{:S(2)}, u32[]{:S(2)}) %all-to-all-start) | async-done | bytes 1441824 | tf_op jit(solution)/shard_map/all_to_all | solution.py:459
  56.7 3.6 %collective-permute-start.7 = (bf16[256,640]{1,0:T(8,128)(2,1)}, bf16[256,640]{1,0:T(8,128)(2,1)}, u32[]{:S(2)}, u32[]{:S(2)}) collective-permute-start(bf16[256,640]{1,0:T(8,128)(2,1)} %pad_maximum_fusion.refs_7_), channel_id=1, source_target_pairs={{0,24},{8,0},{16,8},{24,16},{1,25},{9,1},{17,9},{25,17},{2,26},{10... | collective-permute-start | bytes 983048 | tf_op jit(solution)/shard_map/ppermute | solution.py:304
  64.0 13.0 %attention.2 = (bf16[256,640]{1,0:T(8,128)(2,1)}, bf16[256,640]{1,0:T(8,128)(2,1)}, bf16[256,640]{1,0:T(8,128)(2,1)}, bf16[128,640]{1,0:T(8,128)(2,1)}, bf16[128...) custom-call(f32[1]{0:T(128)S(6)} %copy.18.refs_0_, ...), custom_call_target="tpu_custom_call" | custom-call | flops 12582912000 | bytes 4587520 | tf_op jit(solution)/shard_map/attention/pallas_call | solution.py:232
  78.3 3.8 %collective-permute-start.9 = (bf16[128,640]{1,0:T(8,128)(2,1)S(1)}, bf16[128,640]{1,0:T(8,128)(2,1)}, u32[]{:S(2)}, u32[]{:S(2)}) collective-permute-start(bf16[128,640]{1,0:T(8,128)(2,1)S(1)} %get-tuple-element.61), channel_id=1, source_target_pairs={{0,24},{8,0},{16,8},{24,16},{1,25},{9,1},{17,9},{25,17},{2,26},{10... | collective-permute-start | bytes 491528 | tf_op jit(solution)/shard_map/ppermute | solution.py:304
  82.1 2.1 %dynamic-slice_bitcast_fusion.1 = bf16[4,4,40,640]{3,2,1,0:T(8,128)(2,1)} fusion(bf16[4,4,2,40,640]{4,3,2,1,0:T(8,128)(2,1)} %bitcast.70, s32[]{:T(128)S(6)} %select_n.43), kind=kLoop, calls=%fused_computation.9 | loop fusion | bytes 1638404 | tf_op jit(solution)/shard_map/jit(dynamic_index_in_dim)/squeeze | solution.py:440
  86.2 4.0 %all-to-all-start.1 = ((bf16[32,16,640]{2,1,0:T(8,128)(2,1)}), bf16[32,16,640]{2,1,0:T(8,128)(2,1)S(1)}, u32[]{:S(2)}, u32[]{:S(2)}) async-start(bf16[32,16,640]{2,1,0:T(8,128)(2,1)} %bitcast.7), calls=%async_computation.1 | async-start | bytes 1310720 | tf_op jit(solution)/shard_map/all_to_all | solution.py:459
  90.9 13.3 %attention.3 = (bf16[256,640]{1,0:T(8,128)(2,1)}, bf16[256,640]{1,0:T(8,128)(2,1)}, bf16[256,640]{1,0:T(8,128)(2,1)}, bf16[128,640]{1,0:T(8,128)(2,1)}, bf16[128...) custom-call(f32[1]{0:T(128)S(6)} %copy.18.refs_0_, ...), custom_call_target="tpu_custom_call" | custom-call | flops 12582912000 | bytes 4587520 | tf_op jit(solution)/shard_map/attention/pallas_call | solution.py:232
  104.2 2.5 %fusion.1 = bf16[4,4,40,640]{3,2,1,0:T(8,128)(2,1)} fusion(bf16[4,4,40,640]{3,2,1,0:T(8,128)(2,1)} %collective-permute-done.10, bf16[4,4,2,40,640]{4,3,2,1,0:T(8,128)(2,1)} %bitcast.71, s32[]{:T(128)S(6)} %select_n.42), kind=kLoop, calls=%fused_computation.3 | loop fusion | flops 1638400 | bytes 2457604 | tf_op jit(solution)/shard_map/convert_element_type | solution.py:345
  106.8 3.2 %all-to-all-done.1 = bf16[32,16,640]{2,1,0:T(8,128)(2,1)S(1)} async-done(((bf16[32,16,640]{2,1,0:T(8,128)(2,1)}), bf16[32,16,640]{2,1,0:T(8,128)(2,1)S(1)}, u32[]{:S(2)}, u32[]{:S(2)}) %all-to-all-start.1) | async-done | bytes 655392 | tf_op jit(solution)/shard_map/all_to_all | solution.py:459
  110.0 2.1 %dynamic-slice_bitcast_fusion = bf16[4,4,40,640]{3,2,1,0:T(8,128)(2,1)} fusion(bf16[4,4,2,40,640]{4,3,2,1,0:T(8,128)(2,1)} %bitcast.68, s32[]{:T(128)S(6)} %select_n.43), kind=kLoop, calls=%fused_computation.8 | loop fusion | bytes 1638404 | tf_op jit(solution)/shard_map/jit(dynamic_index_in_dim)/squeeze | solution.py:440
  114.3 4.6 %all-to-all-start.2 = ((bf16[32,16,768]{2,1,0:T(8,128)(2,1)}), bf16[32,16,768]{2,1,0:T(8,128)(2,1)S(1)}, u32[]{:S(2)}, u32[]{:S(2)}) async-start(bf16[32,16,768]{2,1,0:T(8,128)(2,1)} %bitcast.72), calls=%async_computation.2 | async-start | bytes 1572864 | tf_op jit(solution)/shard_map/all_to_all | solution.py:459
  125.3 3.4 %collective-permute-start.13 = (bf16[512,640]{1,0:T(8,128)(2,1)S(1)}, bf16[512,640]{1,0:T(8,128)(2,1)S(1)}, u32[]{:S(2)}, u32[]{:S(2)}) collective-permute-start(bf16[512,640]{1,0:T(8,128)(2,1)S(1)} %get-tuple-element.78), channel_id=1, source_target_pairs={{0,24},{8,0},{16,8},{24,16},{1,25},{9,1},{17,9},{25,17},{2,26},{10... | collective-permute-start | bytes 1966088 | tf_op jit(solution)/shard_map/ppermute | solution.py:304
  128.8 10.0 %collective-permute-done.15 = bf16[4,2,40,640]{3,2,1,0:T(8,128)(2,1)S(1)} collective-permute-done((bf16[4,2,40,640]{3,2,1,0:T(8,128)(2,1)S(1)}, bf16[4,2,40,640]{3,2,1,0:T(8,128)(2,1)S(1)}, u32[]{:S(2)}, u32[]{:S(2)}) %collective-permute-start.15) | collective-permute-done | bytes 409632 | tf_op jit(solution)/shard_map/ppermute | solution.py:442
  141.6 3.8 %collective-permute-done.16 = bf16[4,1,40,640]{3,2,1,0:T(8,128)(2,1)S(1)} collective-permute-done((bf16[4,1,40,640]{3,2,1,0:T(8,128)(2,1)S(1)}, bf16[4,1,40,640]{3,2,1,0:T(8,128)(2,1)S(1)}, u32[]{:S(2)}, u32[]{:S(2)}) %collective-permute-start.16) | collective-permute-done | bytes 204832 | tf_op jit(solution)/shard_map/ppermute | solution.py:442
  148.4 2.3 %collective-permute-start.21 = (bf16[40,1280]{1,0:T(8,128)(2,1)S(1)}, bf16[40,1280]{1,0:T(8,128)(2,1)S(1)}, u32[]{:S(2)}, u32[]{:S(2)}) collective-permute-start(bf16[40,1280]{1,0:T(8,128)(2,1)S(1)} %get-tuple-element.86), channel_id=1, source_target_pairs={{0,16},{8,24},{16,0},{24,8},{1,17},{9,25},{17,1},{25,9},{2,18},{10... | collective-permute-start | bytes 307208 | tf_op jit(solution)/shard_map/ppermute | solution.py:453
  151.5 13.3 %collective-permute-done.14.forth_ref = bf16[512,640]{1,0:T(8,128)(2,1)S(1)} collective-permute-done((bf16[512,640]{1,0:T(8,128)(2,1)S(1)}, bf16[512,640]{1,0:T(8,128)(2,1)S(1)}, u32[]{:S(2)}, u32[]{:S(2)}) %collective-permute-start.14) | collective-permute-done | bytes 655392 | tf_op jit(solution)/shard_map/ppermute | solution.py:304
  165.9 2.3 %pick_rows.1 = (bf16[512,1280]{1,0:T(8,128)(2,1)}, f32[1,1]{1,0:T(1,128)}) custom-call(s32[1,512]{1,0:T(1,128)S(1)} %get-tuple-element.45.refs_0_, bf16[512,640]{1,0:T(8,128)(2,1)S(1)} %bitcast.61, bf16[512,768]{1,0:T(8,128)(2,1)S(1)} %bitcast.60), custom_call_target="tpu_custom_call" | custom-call | flops 671088640 | bytes 2621440 | tf_op jit(solution)/shard_map/pick_rows/pallas_call | solution.py:283
  168.9 6.1 %collective-permute-done.21 = bf16[40,1280]{1,0:T(8,128)(2,1)S(1)} collective-permute-done((bf16[40,1280]{1,0:T(8,128)(2,1)S(1)}, bf16[40,1280]{1,0:T(8,128)(2,1)S(1)}, u32[]{:S(2)}, u32[]{:S(2)}) %collective-permute-start.21) | collective-permute-done | bytes 102432 | tf_op jit(solution)/shard_map/ppermute | solution.py:453
  (102 shorter events, 29.4 us)
Async XLA Ops:
  2.0 13.7 %collective-permute-start = (bf16[256,640]{1,0:T(8,128)(2,1)S(1)}, bf16[256,640]{1,0:T(8,128)(2,1)S(1)}, u32[]{:S(2)}, u32[]{:S(2)}) collective-permute-start(bf16[256,640]{1,0:T(8,128)(2,1)S(1)} %pad_maximum_fusion.1.refs_7_), channel_id=1, source_target_pairs={{0,8},{8,16},{16,24},{24,0},{1,9},{9,17},{17,25},{25,1},{2,10},{10... | collective-permute-start | bytes 983048 | tf_op jit(solution)/shard_map/ppermute | solution.py:304
  5.1 16.9 %collective-permute-start.1 = (bf16[256,640]{1,0:T(8,128)(2,1)S(1)}, bf16[256,640]{1,0:T(8,128)(2,1)S(1)}, u32[]{:S(2)}, u32[]{:S(2)}) collective-permute-start(bf16[256,640]{1,0:T(8,128)(2,1)S(1)} %pad_maximum_fusion.1.refs_7_), channel_id=1, source_target_pairs={{0,24},{8,0},{16,8},{24,16},{1,25},{9,1},{17,9},{25,17},{2,26},{10... | collective-permute-start | bytes 983048 | tf_op jit(solution)/shard_map/ppermute | solution.py:304
  10.1 46.3 %all-to-all-start = ((bf16[32,16,1408]{2,1,0:T(8,128)(2,1)}), bf16[32,16,1408]{2,1,0:T(8,128)(2,1)S(1)}, u32[]{:S(2)}, u32[]{:S(2)}) async-start(bf16[32,16,1408]{2,1,0:T(8,128)(2,1)} %bitcast.3), calls=%async_computation | async-start | bytes 2883584 | tf_op jit(solution)/shard_map/all_to_all | solution.py:459
  22.7 39.9 %collective-permute-start.2 = (bf16[128,640]{1,0:T(8,128)(2,1)S(1)}, bf16[128,640]{1,0:T(8,128)(2,1)S(1)}, u32[]{:S(2)}, u32[]{:S(2)}) collective-permute-start(bf16[128,640]{1,0:T(8,128)(2,1)S(1)} %get-tuple-element.50), channel_id=1, source_target_pairs={{0,8},{8,16},{16,24},{24,0},{1,9},{9,17},{17,25},{25,1},{2,10},{10... | collective-permute-start | bytes 491528 | tf_op jit(solution)/shard_map/ppermute | solution.py:304
  23.2 39.4 %collective-permute-start.3 = (bf16[128,640]{1,0:T(8,128)(2,1)S(1)}, bf16[128,640]{1,0:T(8,128)(2,1)S(1)}, u32[]{:S(2)}, u32[]{:S(2)}) collective-permute-start(bf16[128,640]{1,0:T(8,128)(2,1)S(1)} %get-tuple-element.51), channel_id=1, source_target_pairs={{0,24},{8,0},{16,8},{24,16},{1,25},{9,1},{17,9},{25,17},{2,26},{10... | collective-permute-start | bytes 491528 | tf_op jit(solution)/shard_map/ppermute | solution.py:304
  56.5 20.5 %collective-permute-start.6 = (bf16[256,640]{1,0:T(8,128)(2,1)}, bf16[256,640]{1,0:T(8,128)(2,1)S(1)}, u32[]{:S(2)}, u32[]{:S(2)}) collective-permute-start(bf16[256,640]{1,0:T(8,128)(2,1)} %pad_maximum_fusion.refs_7_), channel_id=1, source_target_pairs={{0,8},{8,16},{16,24},{24,0},{1,9},{9,17},{17,25},{25,1},{2,10},{10... | collective-permute-start | bytes 983048 | tf_op jit(solution)/shard_map/ppermute | solution.py:304
  56.7 20.3 %collective-permute-start.7 = (bf16[256,640]{1,0:T(8,128)(2,1)}, bf16[256,640]{1,0:T(8,128)(2,1)}, u32[]{:S(2)}, u32[]{:S(2)}) collective-permute-start(bf16[256,640]{1,0:T(8,128)(2,1)} %pad_maximum_fusion.refs_7_), channel_id=1, source_target_pairs={{0,24},{8,0},{16,8},{24,16},{1,25},{9,1},{17,9},{25,17},{2,26},{10... | collective-permute-start | bytes 983048 | tf_op jit(solution)/shard_map/ppermute | solution.py:304
  78.2 12.0 %collective-permute-start.8 = (bf16[128,640]{1,0:T(8,128)(2,1)S(1)}, bf16[128,640]{1,0:T(8,128)(2,1)S(1)}, u32[]{:S(2)}, u32[]{:S(2)}) collective-permute-start(bf16[128,640]{1,0:T(8,128)(2,1)S(1)} %get-tuple-element.60), channel_id=1, source_target_pairs={{0,8},{8,16},{16,24},{24,0},{1,9},{9,17},{17,25},{25,1},{2,10},{10... | collective-permute-start | bytes 491528 | tf_op jit(solution)/shard_map/ppermute | solution.py:304
  78.3 12.6 %collective-permute-start.9 = (bf16[128,640]{1,0:T(8,128)(2,1)S(1)}, bf16[128,640]{1,0:T(8,128)(2,1)}, u32[]{:S(2)}, u32[]{:S(2)}) collective-permute-start(bf16[128,640]{1,0:T(8,128)(2,1)S(1)} %get-tuple-element.61), channel_id=1, source_target_pairs={{0,24},{8,0},{16,8},{24,16},{1,25},{9,1},{17,9},{25,17},{2,26},{10... | collective-permute-start | bytes 491528 | tf_op jit(solution)/shard_map/ppermute | solution.py:304
  84.2 20.0 %collective-permute-start.10 = (bf16[4,4,40,640]{3,2,1,0:T(8,128)(2,1)}, bf16[4,4,40,640]{3,2,1,0:T(8,128)(2,1)}, u32[]{:S(2)}, u32[]{:S(2)}) collective-permute-start(bf16[4,4,40,640]{3,2,1,0:T(8,128)(2,1)} %dynamic-slice_bitcast_fusion.1), channel_id=1, source_target_pairs={{0,1},{1,0},{2,3},{3,2},{4,5},{5,4},{6,7},{7,6},{8,9},{9,8},{10,11... | collective-permute-start | bytes 2457608 | tf_op jit(solution)/shard_map/ppermute | solution.py:442
  84.2 22.6 %collective-permute-start.4 = (bf16[128,640]{1,0:T(8,128)(2,1)}, bf16[128,640]{1,0:T(8,128)(2,1)S(1)}, u32[]{:S(2)}, u32[]{:S(2)}) collective-permute-start(bf16[128,640]{1,0:T(8,128)(2,1)} %get-tuple-element.52), channel_id=1, source_target_pairs={{0,24},{8,0},{16,8},{24,16},{1,25},{9,1},{17,9},{25,17},{2,26},{10... | collective-permute-start | bytes 491528 | tf_op jit(solution)/shard_map/ppermute | solution.py:304
  84.2 22.6 %collective-permute-start.5 = (bf16[128,640]{1,0:T(8,128)(2,1)S(1)}, bf16[128,640]{1,0:T(8,128)(2,1)S(1)}, u32[]{:S(2)}, u32[]{:S(2)}) collective-permute-start(bf16[128,640]{1,0:T(8,128)(2,1)S(1)} %copy-done.19), channel_id=1, source_target_pairs={{0,8},{8,16},{16,24},{24,0},{1,9},{9,17},{17,25},{25,1},{2,10},{10... | collective-permute-start | bytes 491528 | tf_op jit(solution)/shard_map/ppermute | solution.py:304
  86.2 23.8 %all-to-all-start.1 = ((bf16[32,16,640]{2,1,0:T(8,128)(2,1)}), bf16[32,16,640]{2,1,0:T(8,128)(2,1)S(1)}, u32[]{:S(2)}, u32[]{:S(2)}) async-start(bf16[32,16,640]{2,1,0:T(8,128)(2,1)} %bitcast.7), calls=%async_computation.1 | async-start | bytes 1310720 | tf_op jit(solution)/shard_map/all_to_all | solution.py:459
  112.1 9.7 %collective-permute-start.17 = (bf16[4,4,40,640]{3,2,1,0:T(8,128)(2,1)}, bf16[4,4,40,640]{3,2,1,0:T(8,128)(2,1)}, u32[]{:S(2)}, u32[]{:S(2)}) collective-permute-start(bf16[4,4,40,640]{3,2,1,0:T(8,128)(2,1)} %dynamic-slice_bitcast_fusion), channel_id=1, source_target_pairs={{0,1},{1,0},{2,3},{3,2},{4,5},{5,4},{6,7},{7,6},{8,9},{9,8},{10,11... | collective-permute-start | bytes 2457608 | tf_op jit(solution)/shard_map/ppermute | solution.py:442
  112.2 12.9 %collective-permute-start.11 = (bf16[128,640]{1,0:T(8,128)(2,1)S(1)}, bf16[128,640]{1,0:T(8,128)(2,1)S(1)}, u32[]{:S(2)}, u32[]{:S(2)}) collective-permute-start(bf16[128,640]{1,0:T(8,128)(2,1)S(1)} %copy-done.18), channel_id=1, source_target_pairs={{0,24},{8,0},{16,8},{24,16},{1,25},{9,1},{17,9},{25,17},{2,26},{10... | collective-permute-start | bytes 491528 | tf_op jit(solution)/shard_map/ppermute | solution.py:304
  112.9 12.2 %collective-permute-start.12 = (bf16[128,640]{1,0:T(8,128)(2,1)S(1)}, bf16[128,640]{1,0:T(8,128)(2,1)S(1)}, u32[]{:S(2)}, u32[]{:S(2)}) collective-permute-start(bf16[128,640]{1,0:T(8,128)(2,1)S(1)} %copy-done.17), channel_id=1, source_target_pairs={{0,8},{8,16},{16,24},{24,0},{1,9},{9,17},{17,25},{25,1},{2,10},{10... | collective-permute-start | bytes 491528 | tf_op jit(solution)/shard_map/ppermute | solution.py:304
  114.3 51.6 %all-to-all-start.2 = ((bf16[32,16,768]{2,1,0:T(8,128)(2,1)}), bf16[32,16,768]{2,1,0:T(8,128)(2,1)S(1)}, u32[]{:S(2)}, u32[]{:S(2)}) async-start(bf16[32,16,768]{2,1,0:T(8,128)(2,1)} %bitcast.72), calls=%async_computation.2 | async-start | bytes 1572864 | tf_op jit(solution)/shard_map/all_to_all | solution.py:459
  120.0 18.7 %collective-permute-start.15 = (bf16[4,2,40,640]{3,2,1,0:T(8,128)(2,1)S(1)}, bf16[4,2,40,640]{3,2,1,0:T(8,128)(2,1)S(1)}, u32[]{:S(2)}, u32[]{:S(2)}) collective-permute-start(bf16[4,2,40,640]{3,2,1,0:T(8,128)(2,1)S(1)} %dynamic-slice_bitcast_fusion.3), channel_id=1, source_target_pairs={{0,2},{1,3},{2,0},{3,1},{4,6},{5,7},{6,4},{7,5},{8,10},{9,11},{10,... | collective-permute-start | bytes 1228808 | tf_op jit(solution)/shard_map/ppermute | solution.py:442
  123.6 17.1 %collective-permute-start.18 = (bf16[4,2,40,640]{3,2,0,1:T(8,128)(2,1)S(1)}, bf16[4,2,40,640]{3,2,0,1:T(8,128)(2,1)S(1)}, u32[]{:S(2)}, u32[]{:S(2)}) collective-permute-start(bf16[4,2,40,640]{3,2,0,1:T(8,128)(2,1)S(1)} %dynamic-slice_bitcast_fusion.2), channel_id=1, source_target_pairs={{0,4},{1,5},{2,6},{3,7},{4,0},{5,1},{6,2},{7,3},{8,12},{9,13},{10,... | collective-permute-start | bytes 1228808 | tf_op jit(solution)/shard_map/ppermute | solution.py:442
  125.3 26.2 %collective-permute-start.13 = (bf16[512,640]{1,0:T(8,128)(2,1)S(1)}, bf16[512,640]{1,0:T(8,128)(2,1)S(1)}, u32[]{:S(2)}, u32[]{:S(2)}) collective-permute-start(bf16[512,640]{1,0:T(8,128)(2,1)S(1)} %get-tuple-element.78), channel_id=1, source_target_pairs={{0,24},{8,0},{16,8},{24,16},{1,25},{9,1},{17,9},{25,17},{2,26},{10... | collective-permute-start | bytes 1966088 | tf_op jit(solution)/shard_map/ppermute | solution.py:304
  128.8 36.1 %collective-permute-start.14 = (bf16[512,640]{1,0:T(8,128)(2,1)S(1)}, bf16[512,640]{1,0:T(8,128)(2,1)S(1)}, u32[]{:S(2)}, u32[]{:S(2)}) collective-permute-start(bf16[512,640]{1,0:T(8,128)(2,1)S(1)} %get-tuple-element.79), channel_id=1, source_target_pairs={{0,8},{8,16},{16,24},{24,0},{1,9},{9,17},{17,25},{25,1},{2,10},{10... | collective-permute-start | bytes 1966088 | tf_op jit(solution)/shard_map/ppermute | solution.py:304
  147.1 21.8 %collective-permute-start.20 = (bf16[40,1280]{1,0:T(8,128)(2,1)S(1)}, bf16[40,1280]{1,0:T(8,128)(2,1)S(1)}, u32[]{:S(2)}, u32[]{:S(2)}) collective-permute-start(bf16[40,1280]{1,0:T(8,128)(2,1)S(1)} %get-tuple-element.85), channel_id=1, source_target_pairs={{0,8},{8,0},{16,24},{24,16},{1,9},{9,1},{17,25},{25,17},{2,10},{10... | collective-permute-start | bytes 307208 | tf_op jit(solution)/shard_map/ppermute | solution.py:453
  148.4 26.6 %collective-permute-start.21 = (bf16[40,1280]{1,0:T(8,128)(2,1)S(1)}, bf16[40,1280]{1,0:T(8,128)(2,1)S(1)}, u32[]{:S(2)}, u32[]{:S(2)}) collective-permute-start(bf16[40,1280]{1,0:T(8,128)(2,1)S(1)} %get-tuple-element.86), channel_id=1, source_target_pairs={{0,16},{8,24},{16,0},{24,8},{1,17},{9,25},{17,1},{25,9},{2,18},{10... | collective-permute-start | bytes 307208 | tf_op jit(solution)/shard_map/ppermute | solution.py:453
  150.7 24.4 %collective-permute-start.22 = (bf16[40,1280]{1,0:T(8,128)(2,1)S(1)}, bf16[40,1280]{1,0:T(8,128)(2,1)S(1)}, u32[]{:S(2)}, u32[]{:S(2)}) collective-permute-start(bf16[40,1280]{1,0:T(8,128)(2,1)S(1)} %get-tuple-element.87), channel_id=1, source_target_pairs={{0,24},{8,16},{16,8},{24,0},{1,25},{9,17},{17,9},{25,1},{2,26},{10... | collective-permute-start | bytes 307208 | tf_op jit(solution)/shard_map/ppermute | solution.py:453
  (25 other events, 166.9 us)

commit v4 on v3

--- a/solution.py
+++ b/solution.py
@@ -12,7 +12,8 @@
 ATTENTION_COST = 150
 FAR_COST = 300000
 STEP_COST = 74000
-TOTAL_COST = 150000
+FIRST_COST = 300000
+SECOND_COST = 1000
 NT = (((1,), (1,)), ((), ()))
 NN = (((1,), (0,)), ((), ()))
 
@@ -136,34 +137,31 @@
     grad = jnp.transpose(grad_t)
     lane_masks = head_masks((rows, LANES), 1)
     row_masks = head_masks((LANES, rows), 0)
-    key_term = None
-    value_term = None
-    query_parts = []
-    attn_parts = []
+    spans = [slice(head * HEAD_DIM, (head + 1) * HEAD_DIM) for head in range(2)]
+    query_h = [keep(mask, query) for mask in lane_masks]
+    grad_h = [keep(mask, grad) for mask in lane_masks]
+    scores = [mm(keys, part, NT) for part in query_h]
+    dprobs = [mm(values, keep(mask, grad_t)) for mask in row_masks]
+    probs, low = [], []
+    for head in range(2):
+        peak = jnp.max(scores[head], axis=0, keepdims=True)
+        shifted = jnp.exp(scores[head] - peak)
+        inverse = 1.0 / jnp.sum(shifted, axis=0, keepdims=True)
+        probs.append(shifted * inverse)
+        low.append(probs[head].astype(jnp.bfloat16))
+    attn_parts = [mm(values_tr[spans[h], :], low[h]).astype(jnp.bfloat16) for h in range(2)]
+    dscores = []
     gate_sum = None
     for head in range(2):
-        span = slice(head * HEAD_DIM, (head + 1) * HEAD_DIM)
-        query_h = keep(lane_masks[head], query)
-        grad_h = keep(lane_masks[head], grad)
-        scores = mm(keys, query_h, NT)
-        peak = jnp.max(scores, axis=0, keepdims=True)
-        shifted = jnp.exp(scores - peak)
-        inverse = 1.0 / jnp.sum(shifted, axis=0, keepdims=True)
-        probs = shifted * inverse
-        probs_low = probs.astype(jnp.bfloat16)
-        attn_h = mm(values_tr[span, :], probs_low).astype(jnp.bfloat16)
-        attn_parts.append(attn_h)
-        attn_wide = attn_h.astype(jnp.float32)
+        attn_wide = attn_parts[head].astype(jnp.float32)
+        span = spans[head]
         delta = jnp.sum(grad_t[span, :].astype(jnp.float32) * attn_wide, axis=0, keepdims=True)
         gate_h = jnp.sum(upstream[span, :] * attn_wide, axis=0, keepdims=True)
-        dprob = mm(values, keep(row_masks[head], grad_t))
-        dscore = (probs * (dprob - delta)).astype(jnp.bfloat16)
-        value_part = mm(probs_low, grad_h)
-        key_part = mm(dscore, query_h)
-        value_term = value_part if head == 0 else value_term + value_part
-        key_term = key_part if head == 0 else key_term + key_part
         gate_sum = gate_h if head == 0 else gate_sum + gate_h
-        query_parts.append(mm(keys_tr[span, :], dscore) * root)
+        dscores.append((probs[head] * (dprobs[head] - delta)).astype(jnp.bfloat16))
+    value_term = mm(low[0], grad_h[0]) + mm(low[1], grad_h[1])
+    key_term = mm(dscores[0], query_h[0]) + mm(dscores[1], query_h[1])
+    query_parts = [mm(keys_tr[spans[h], :], dscores[h]) * root for h in range(2)]
     gate_out_ref[...] += gate_sum
     product = mm(rows_t_ref[...], jnp.concatenate(attn_parts, axis=0), NT)
     product_ref[...] = (gate * product).astype(jnp.bfloat16)
@@ -349,84 +347,70 @@
     return shift(parts[-2], -1), shift(parts[-1], 1)
 
 
-def step_kernel(*refs):
-    back_ref, forth_ref = refs[-2:]
-    rows = refs[0].shape[0]
-    half = rows // 2
-    for number in range(2):
-        back, forth, far_keys, far_values = refs[4 * number : 4 * number + 4]
-        first = number * rows
-        middle = first + half
-        back_ref[first:middle] = add(back[:half], far_keys[...])
-        back_ref[middle : first + rows] = back[half:]
-        forth_ref[first:middle] = forth[:half]
-        forth_ref[middle : first + rows] = add(forth[half:], far_values[...])
-
-
-def step_sums(halves):
+def step_kernel(back_ref, forth_ref, far_keys_ref, far_values_ref, back_out_ref, forth_out_ref):
+    half = far_keys_ref.shape[0]
+    back_out_ref[:half] = add(back_ref[:half], far_keys_ref[...])
+    back_out_ref[half:] = back_ref[half:]
+    forth_out_ref[:half] = forth_ref[:half]
+    forth_out_ref[half:] = add(forth_ref[half:], far_values_ref[...])
+
+
+def step_sums(back, forth, far_keys, far_values):
     vmem = pl.BlockSpec(memory_space=pltpu.VMEM)
-    back = halves[0][0]
-    shape = jax.ShapeDtypeStruct((2 * back.shape[0], back.shape[1]), back.dtype)
     return pl.pallas_call(
         step_kernel,
-        out_shape=(shape, shape),
-        in_specs=[vmem] * 8,
+        out_shape=(jax.ShapeDtypeStruct(back.shape, back.dtype),) * 2,
+        in_specs=[vmem] * 4,
         out_specs=(vmem, vmem),
         compiler_params=params(),
         name="step_sums",
         cost_estimate=pl.CostEstimate(
-            flops=STEP_COST * back.size, bytes_accessed=16 * back.size, transcendentals=0
-        ),
-    )(*halves[0], *halves[1])
-
-
-def total_kernel(first_ref, second_ref, back_ref, forth_ref, key_ref, value_ref):
-    rows, span = first_ref.shape
-    half = rows // 2
-    for number, own_ref in enumerate((first_ref, second_ref)):
-        moved = slice(number * rows, (number + 1) * rows)
-        total = own_ref[...].astype(jnp.float32) + back_ref[moved].astype(jnp.float32)
-        total = (total + forth_ref[moved].astype(jnp.float32)).astype(jnp.bfloat16)
-        columns = slice(number * span, (number + 1) * span)
-        key_ref[:, columns] = total[:half]
-        value_ref[:, columns] = total[half:]
-
-
-def total_sums(first, second, back, forth):
+            flops=STEP_COST * back.size,
+            bytes_accessed=8 * back.size,
+            transcendentals=0,
+        ),
+    )(back, forth, far_keys, far_values)
+
+
+def send_sums(parts, far_keys, far_values):
+    steps = lax.axis_size("ctx") // 2 - 1
+    back, forth = step_sums(parts[2 * steps - 1], parts[2 * steps], far_keys, far_values)
+    for step in range(steps, 0, -1):
+        if step < steps:
+            back = add(parts[2 * step - 1], back)
+            forth = add(parts[2 * step], forth)
+        back = shift(back, -1)
+        forth = shift(forth, 1)
+    return parts[0], back, forth
+
+
+def total_kernel(own_ref, back_ref, forth_ref, *refs):
+    total = own_ref[...].astype(jnp.float32) + back_ref[...].astype(jnp.float32)
+    total = (total + forth_ref[...].astype(jnp.float32)).astype(jnp.bfloat16)
+    outs = refs[-2:]
+    half = outs[0].shape[0]
+    span = total.shape[1]
+    for before, out, value in zip(refs[:-2] or (None, None), outs, (total[:half], total[half:])):
+        if before is not None:
+            out[:, :-span] = before[...]
+        out[:, -span:] = value
+
+
+def total_sums(own, back, forth, before, cost):
     vmem = pl.BlockSpec(memory_space=pltpu.VMEM)
-    shape = jax.ShapeDtypeStruct((first.shape[0] // 2, 2 * first.shape[1]), first.dtype)
+    span = own.shape[1] + (before[0].shape[1] if before else 0)
+    shape = jax.ShapeDtypeStruct((own.shape[0] // 2, span), own.dtype)
     return pl.pallas_call(
         total_kernel,
         out_shape=(shape, shape),
-        in_specs=[vmem] * 4,
+        in_specs=[vmem] * (3 + len(before)),
         out_specs=(vmem, vmem),
         compiler_params=params(),
         name="total_sums",
         cost_estimate=pl.CostEstimate(
-            flops=TOTAL_COST * first.size, bytes_accessed=16 * first.size, transcendentals=0
-        ),
-    )(first, second, back, forth)
-
-
-def ring_sums(first_terms, second_terms, first_far, second_far):
-    steps = lax.axis_size("ctx") // 2 - 1
-    far = 2 * steps - 1
-    back, forth = step_sums(
-        [
-            (terms[far], terms[far + 1], *moved)
-            for terms, moved in ((first_terms, first_far), (second_terms, second_far))
-        ]
-    )
-    for step in range(steps, 0, -1):
-        if step < steps:
-            near = 2 * step - 1
-            back, forth = (
-                add(jnp.concatenate([first_terms[at], second_terms[at]], axis=0), moved)
-                for at, moved in ((near, back), (near + 1, forth))
-            )
-        back = shift(back, -1)
-        forth = shift(forth, 1)
-    return total_sums(first_terms[0], second_terms[0], back, forth)
+            flops=cost * own.size, bytes_accessed=8 * own.size, transcendentals=0
+        ),
+    )(own, back, forth, *before)
 
 
 def halve(term, bit, lowest):
@@ -518,7 +502,10 @@
         second_product = halve(second_product, opposite, False)
         bit += 1
     weight_chips = jnp.concatenate([first_product[:, 0], second_product[:, 0]], axis=2)
-    key_sum, value_sum = ring_sums(first_terms, second_terms, first_far, second_far)
+    first_sum = total_sums(*send_sums(first_terms, *first_far), (), FIRST_COST)
+    key_sum, value_sum = total_sums(
+        *send_sums(second_terms, *second_far), first_sum, SECOND_COST
+    )
     weight_grad = sum_blocks(weight_chips)
     query_grads, gate_total = pick_rows(
         target, first_returned, second_returned, row_grads.shape[0] // count

time: 178 us -> 174 us (0.978)
  starting transfers between devices: 47.4 us -> 65.8 us
  waiting for transfers between devices: 74.2 us -> 56.3 us
  Pallas kernels: 33.9 us -> 31.7 us
    ppermute x14 -> x16, waiting for transfers between devices: 21 us -> 10.1 us  [shift(): return lax.ppermute(value, 'ctx', pairs)]
    ppermute x3, starting transfers between devices: 4.45 us -> 15.1 us  [sum_blocks(): total = total + lax.ppermute(sent, 'ctx', pairs).astype(jnp.float32)]
    ppermute x14 -> x16, starting transfers between devices: 24.2 us -> 30.8 us  [shift(): return lax.ppermute(value, 'ctx', pairs)]
    ppermute x3, waiting for transfers between devices: 6.13 us -> 0.01 us  [sum_blocks(): total = total + lax.ppermute(sent, 'ctx', pairs).astype(jnp.float32)]
    all_to_all x3, waiting for transfers between devices: 31.7 us -> 28.7 us  [exchange(): lax.all_to_all(value.reshape(count, slots // count, width), ('ctx', 'rec'...]
    pallas_call x2, Pallas kernels: 26.3 us -> 24.1 us  [attention(): pl.pallas_call(lambda *refs: attention_kernel(len(parts) - 1, pairs, *ref...]
    ppermute x6, waiting for transfers between devices: 15.3 us -> 17.4 us  [halve(): lax.ppermute(half(1 - mine), 'rec', [(i, i ^ 1 << bit) for i in range(rec...]
    squeeze x6, local copies, waits for them, and re-layouts: 5.37 us -> 3.48 us  [half(): lax.dynamic_index_in_dim(term, which, 2 if lowest else 1, keepdims=False)]
  transfers between devices with their start and end apart: 26 -> 28, of which waited for: 9 -> 8; matrix products, arithmetic and copies ran while one was open for 5% -> 5% of each run, Pallas kernels for 19% -> 18%
where the time goes in v4:
time: 174 us; the launch traced here: 173 us
  starting transfers between devices  65.8 us (38%)
  waiting for transfers between devices  56.3 us (32%)
  Pallas kernels  31.7 us (18%)
  local copies, waits for them, and re-layouts  10.8 us (6%)
  other arithmetic  4.62 us (3%)
  between operations  4.23 us (2%)
    ppermute x16, starting transfers between devices, shift(): return lax.ppermute(value, 'ctx', pairs)  30.8 us
    all_to_all x3, waiting for transfers between devices, exchange(): lax.all_to_all(value.reshape(count, slots // count, width), ('ctx', 'rec'...  28.7 us
    pallas_call x2, Pallas kernels, attention(): pl.pallas_call(lambda *refs: attention_kernel(len(parts) - 1, pairs, *ref...  24.1 us
    ppermute x6, waiting for transfers between devices, halve(): lax.ppermute(half(1 - mine), 'rec', [(i, i ^ 1 << bit) for i in range(rec...  17.4 us
    ppermute x3, starting transfers between devices, sum_blocks(): total = total + lax.ppermute(sent, 'ctx', pairs).astype(jnp.float32)  15.1 us
    all_to_all x3, starting transfers between devices, exchange(): lax.all_to_all(value.reshape(count, slots // count, width), ('ctx', 'rec'...  14 us
    ppermute x16, waiting for transfers between devices, shift(): return lax.ppermute(value, 'ctx', pairs)  10.1 us
    ppermute x6, starting transfers between devices, halve(): lax.ppermute(half(1 - mine), 'rec', [(i, i ^ 1 << bit) for i in range(rec...  5.84 us
  transfers between devices with their start and end apart: 28, of which 8 were waited for; matrix products, arithmetic and copies ran while one was open for 5% of the time, Pallas kernels for 18%

profile of v4, /device:TPU:0, one launch (start us, length us, event | category | flops | bytes accessed | tf_op | source)
XLA Modules:
  0.0 173.4 jit_solution(16191483534091550399)
XLA Ops:
  2.0 3.1 %collective-permute-start = (bf16[256,640]{1,0:T(8,128)(2,1)S(1)}, bf16[256,640]{1,0:T(8,128)(2,1)S(1)}, u32[]{:S(2)}, u32[]{:S(2)}) collective-permute-start(bf16[256,640]{1,0:T(8,128)(2,1)S(1)} %pad_maximum_fusion.1.refs_7_), channel_id=1, source_target_pairs={{0,8},{8,16},{16,24},{24,0},{1,9},{9,17},{17,25},{25,1},{2,10},{10... | collective-permute-start | bytes 983048 | tf_op jit(solution)/shard_map/ppermute | solution.py:302
  7.9 2.3 %route_prep.1 = (bf16[512,1408]{1,0:T(8,128)(2,1)}, s32[1,512]{1,0:T(1,128)S(1)}) custom-call(s32[1]{0:T(128)S(6)} %copy.19.refs_0_, s32[1,512]{1,0:T(1,128)S(1)} %bitcast.62, s32[1,512]{1,0:T(1,128)S(1)} %bitcast.63, bf16[512,1280]{1,0:T(8,128)(2,1)S(1)} %copy-done.3), custom_call_target="tpu_custom_call" | custom-call | flops 671088640 | bytes 2621440 | tf_op jit(solution)/shard_map/route_prep/pallas_call | solution.py:66
  10.2 4.2 %all-to-all-start = ((bf16[32,16,1408]{2,1,0:T(8,128)(2,1)}), bf16[32,16,1408]{2,1,0:T(8,128)(2,1)S(1)}, u32[]{:S(2)}, u32[]{:S(2)}) async-start(bf16[32,16,1408]{2,1,0:T(8,128)(2,1)} %bitcast.3), calls=%async_computation | async-start | bytes 2883584 | tf_op jit(solution)/shard_map/all_to_all | solution.py:443
  15.7 6.3 %collective-permute-done.1.behind_ref.refs_9_ = bf16[256,640]{1,0:T(8,128)(2,1)S(1)} collective-permute-done((bf16[256,640]{1,0:T(8,128)(2,1)S(1)}, bf16[256,640]{1,0:T(8,128)(2,1)S(1)}, u32[]{:S(2)}, u32[]{:S(2)}) %collective-permute-start.1) | collective-permute-done | bytes 327712 | tf_op jit(solution)/shard_map/ppermute | solution.py:302
  23.2 3.3 %collective-permute-start.3 = (bf16[128,640]{1,0:T(8,128)(2,1)S(1)}, bf16[128,640]{1,0:T(8,128)(2,1)S(1)}, u32[]{:S(2)}, u32[]{:S(2)}) collective-permute-start(bf16[128,640]{1,0:T(8,128)(2,1)S(1)} %get-tuple-element.55), channel_id=1, source_target_pairs={{0,24},{8,0},{16,8},{24,16},{1,25},{9,1},{17,9},{25,17},{2,26},{10... | collective-permute-start | bytes 491528 | tf_op jit(solution)/shard_map/ppermute | solution.py:302
  28.0 28.5 %all-to-all-done = bf16[32,16,1408]{2,1,0:T(8,128)(2,1)S(1)} async-done(((bf16[32,16,1408]{2,1,0:T(8,128)(2,1)}), bf16[32,16,1408]{2,1,0:T(8,128)(2,1)S(1)}, u32[]{:S(2)}, u32[]{:S(2)}) %all-to-all-start) | async-done | bytes 1441824 | tf_op jit(solution)/shard_map/all_to_all | solution.py:443
  56.7 3.6 %collective-permute-start.7 = (bf16[256,640]{1,0:T(8,128)(2,1)}, bf16[256,640]{1,0:T(8,128)(2,1)}, u32[]{:S(2)}, u32[]{:S(2)}) collective-permute-start(bf16[256,640]{1,0:T(8,128)(2,1)} %pad_maximum_fusion.refs_7_), channel_id=1, source_target_pairs={{0,24},{8,0},{16,8},{24,16},{1,25},{9,1},{17,9},{25,17},{2,26},{10... | collective-permute-start | bytes 983048 | tf_op jit(solution)/shard_map/ppermute | solution.py:302
  64.0 11.9 %attention.2 = (bf16[256,640]{1,0:T(8,128)(2,1)}, bf16[256,640]{1,0:T(8,128)(2,1)}, bf16[256,640]{1,0:T(8,128)(2,1)}, bf16[128,640]{1,0:T(8,128)(2,1)}, bf16[128...) custom-call(f32[1]{0:T(128)S(6)} %copy.18.refs_0_, ...), custom_call_target="tpu_custom_call" | custom-call | flops 12582912000 | bytes 4587520 | tf_op jit(solution)/shard_map/attention/pallas_call | solution.py:230
  77.2 3.8 %collective-permute-start.9 = (bf16[128,640]{1,0:T(8,128)(2,1)S(1)}, bf16[128,640]{1,0:T(8,128)(2,1)S(1)}, u32[]{:S(2)}, u32[]{:S(2)}) collective-permute-start(bf16[128,640]{1,0:T(8,128)(2,1)S(1)} %get-tuple-element.65), channel_id=1, source_target_pairs={{0,24},{8,0},{16,8},{24,16},{1,25},{9,1},{17,9},{25,17},{2,26},{10... | collective-permute-start | bytes 491528 | tf_op jit(solution)/shard_map/ppermute | solution.py:302
  81.0 2.1 %dynamic-slice_bitcast_fusion.1 = bf16[4,4,40,640]{3,2,1,0:T(8,128)(2,1)} fusion(bf16[4,4,2,40,640]{4,3,2,1,0:T(8,128)(2,1)} %bitcast.68, s32[]{:T(128)S(6)} %select_n.43), kind=kLoop, calls=%fused_computation.9 | loop fusion | bytes 1638404 | tf_op jit(solution)/shard_map/jit(dynamic_index_in_dim)/squeeze | solution.py:424
  85.2 4.0 %all-to-all-start.1 = ((bf16[32,16,640]{2,1,0:T(8,128)(2,1)}), bf16[32,16,640]{2,1,0:T(8,128)(2,1)S(1)}, u32[]{:S(2)}, u32[]{:S(2)}) async-start(bf16[32,16,640]{2,1,0:T(8,128)(2,1)} %bitcast.7), calls=%async_computation.1 | async-start | bytes 1310720 | tf_op jit(solution)/shard_map/all_to_all | solution.py:443
  90.6 12.2 %attention.3 = (bf16[256,640]{1,0:T(8,128)(2,1)}, bf16[256,640]{1,0:T(8,128)(2,1)}, bf16[256,640]{1,0:T(8,128)(2,1)}, bf16[128,640]{1,0:T(8,128)(2,1)}, bf16[128...) custom-call(f32[1]{0:T(128)S(6)} %copy.18.refs_0_, ...), custom_call_target="tpu_custom_call" | custom-call | flops 12582912000 | bytes 4587520 | tf_op jit(solution)/shard_map/attention/pallas_call | solution.py:230
  102.7 3.7 %collective-permute-start.11 = (bf16[128,640]{1,0:T(8,128)(2,1)}, bf16[128,640]{1,0:T(8,128)(2,1)S(1)}, u32[]{:S(2)}, u32[]{:S(2)}) collective-permute-start(bf16[128,640]{1,0:T(8,128)(2,1)} %get-tuple-element.75), channel_id=1, source_target_pairs={{0,24},{8,0},{16,8},{24,16},{1,25},{9,1},{17,9},{25,17},{2,26},{10... | collective-permute-start | bytes 491528 | tf_op jit(solution)/shard_map/ppermute | solution.py:302
  106.4 2.5 %fusion.1 = bf16[4,4,40,640]{3,2,1,0:T(8,128)(2,1)} fusion(bf16[4,4,40,640]{3,2,1,0:T(8,128)(2,1)} %collective-permute-done.10, bf16[4,4,2,40,640]{4,3,2,1,0:T(8,128)(2,1)} %bitcast.69, s32[]{:T(128)S(6)} %select_n.42), kind=kLoop, calls=%fused_computation.3 | loop fusion | flops 1638400 | bytes 2457604 | tf_op jit(solution)/shard_map/convert_element_type | solution.py:343
  109.2 5.8 %all-to-all-start.2 = ((bf16[32,16,768]{2,1,0:T(8,128)(2,1)}), bf16[32,16,768]{2,1,0:T(8,128)(2,1)S(1)}, u32[]{:S(2)}, u32[]{:S(2)}) async-start(bf16[32,16,768]{2,1,0:T(8,128)(2,1)} %bitcast.72), calls=%async_computation.2 | async-start | bytes 1572864 | tf_op jit(solution)/shard_map/all_to_all | solution.py:443
  116.7 3.6 %collective-permute-start.13 = (bf16[256,640]{1,0:T(8,128)(2,1)S(1)}, bf16[256,640]{1,0:T(8,128)(2,1)S(1)}, u32[]{:S(2)}, u32[]{:S(2)}) collective-permute-start(bf16[256,640]{1,0:T(8,128)(2,1)S(1)} %get-tuple-element.77), channel_id=1, source_target_pairs={{0,24},{8,0},{16,8},{24,16},{1,25},{9,1},{17,9},{25,17},{2,26},{10... | collective-permute-start | bytes 983048 | tf_op jit(solution)/shard_map/ppermute | solution.py:302
  123.9 3.9 %collective-permute-start.15 = (bf16[256,640]{1,0:T(8,128)(2,1)S(1)}, bf16[256,640]{1,0:T(8,128)(2,1)S(1)}, u32[]{:S(2)}, u32[]{:S(2)}) collective-permute-start(bf16[256,640]{1,0:T(8,128)(2,1)S(1)} %get-tuple-element.84), channel_id=1, source_target_pairs={{0,24},{8,0},{16,8},{24,16},{1,25},{9,1},{17,9},{25,17},{2,26},{10... | collective-permute-start | bytes 983048 | tf_op jit(solution)/shard_map/ppermute | solution.py:302
  127.8 8.2 %collective-permute-done.17 = bf16[4,2,40,640]{3,2,1,0:T(8,128)(2,1)S(1)} collective-permute-done((bf16[4,2,40,640]{3,2,1,0:T(8,128)(2,1)S(1)}, bf16[4,2,40,640]{3,2,1,0:T(8,128)(2,1)S(1)}, u32[]{:S(2)}, u32[]{:S(2)}) %collective-permute-start.17) | collective-permute-done | bytes 409632 | tf_op jit(solution)/shard_map/ppermute | solution.py:426
  138.7 4.5 %collective-permute-done.18 = bf16[4,1,40,640]{3,2,1,0:T(8,128)(2,1)S(1)} collective-permute-done((bf16[4,1,40,640]{3,2,1,0:T(8,128)(2,1)S(1)}, bf16[4,1,40,640]{3,2,1,0:T(8,128)(2,1)S(1)}, u32[]{:S(2)}, u32[]{:S(2)}) %collective-permute-start.18) | collective-permute-done | bytes 204832 | tf_op jit(solution)/shard_map/ppermute | solution.py:426
  144.2 4.8 %collective-permute-done.21 = bf16[4,1,40,640]{3,2,0,1:T(8,128)(2,1)S(1)} collective-permute-done((bf16[4,1,40,640]{3,2,0,1:T(8,128)(2,1)S(1)}, bf16[4,1,40,640]{3,2,0,1:T(8,128)(2,1)S(1)}, u32[]{:S(2)}, u32[]{:S(2)}) %collective-permute-start.21) | collective-permute-done | bytes 204832 | tf_op jit(solution)/shard_map/ppermute | solution.py:426
  149.6 2.5 %collective-permute-done.15.back_ref = bf16[256,640]{1,0:T(8,128)(2,1)S(1)} collective-permute-done((bf16[256,640]{1,0:T(8,128)(2,1)S(1)}, bf16[256,640]{1,0:T(8,128)(2,1)S(1)}, u32[]{:S(2)}, u32[]{:S(2)}) %collective-permute-start.15) | collective-permute-done | bytes 327712 | tf_op jit(solution)/shard_map/ppermute | solution.py:302
  152.0 11.2 %collective-permute-start.23 = (bf16[40,1280]{1,0:T(8,128)(2,1)S(1)}, bf16[40,1280]{1,0:T(8,128)(2,1)S(1)}, u32[]{:S(2)}, u32[]{:S(2)}) collective-permute-start(bf16[40,1280]{1,0:T(8,128)(2,1)S(1)} %get-tuple-element.94), channel_id=1, source_target_pairs={{0,16},{8,24},{16,0},{24,8},{1,17},{9,25},{17,1},{25,9},{2,18},{10... | collective-permute-start | bytes 307208 | tf_op jit(solution)/shard_map/ppermute | solution.py:437
  163.2 3.4 %collective-permute-start.24 = (bf16[40,1280]{1,0:T(8,128)(2,1)S(1)}, bf16[40,1280]{1,0:T(8,128)(2,1)S(1)}, u32[]{:S(2)}, u32[]{:S(2)}) collective-permute-start(bf16[40,1280]{1,0:T(8,128)(2,1)S(1)} %get-tuple-element.95), channel_id=1, source_target_pairs={{0,24},{8,16},{16,8},{24,0},{1,25},{9,17},{17,9},{25,1},{2,26},{10... | collective-permute-start | bytes 307208 | tf_op jit(solution)/shard_map/ppermute | solution.py:437
  168.5 2.3 %pick_rows.1 = (bf16[512,1280]{1,0:T(8,128)(2,1)}, f32[1,1]{1,0:T(1,128)}) custom-call(s32[1,512]{1,0:T(1,128)S(1)} %get-tuple-element.49.refs_0_, bf16[512,640]{1,0:T(8,128)(2,1)S(1)} %bitcast.61, bf16[512,768]{1,0:T(8,128)(2,1)S(1)} %bitcast.60), custom_call_target="tpu_custom_call" | custom-call | flops 671088640 | bytes 2621440 | tf_op jit(solution)/shard_map/pick_rows/pallas_call | solution.py:281
  (110 shorter events, 27.7 us)
Async XLA Ops:
  2.0 13.7 %collective-permute-start = (bf16[256,640]{1,0:T(8,128)(2,1)S(1)}, bf16[256,640]{1,0:T(8,128)(2,1)S(1)}, u32[]{:S(2)}, u32[]{:S(2)}) collective-permute-start(bf16[256,640]{1,0:T(8,128)(2,1)S(1)} %pad_maximum_fusion.1.refs_7_), channel_id=1, source_target_pairs={{0,8},{8,16},{16,24},{24,0},{1,9},{9,17},{17,25},{25,1},{2,10},{10... | collective-permute-start | bytes 983048 | tf_op jit(solution)/shard_map/ppermute | solution.py:302
  5.1 16.9 %collective-permute-start.1 = (bf16[256,640]{1,0:T(8,128)(2,1)S(1)}, bf16[256,640]{1,0:T(8,128)(2,1)S(1)}, u32[]{:S(2)}, u32[]{:S(2)}) collective-permute-start(bf16[256,640]{1,0:T(8,128)(2,1)S(1)} %pad_maximum_fusion.1.refs_7_), channel_id=1, source_target_pairs={{0,24},{8,0},{16,8},{24,16},{1,25},{9,1},{17,9},{25,17},{2,26},{10... | collective-permute-start | bytes 983048 | tf_op jit(solution)/shard_map/ppermute | solution.py:302
  10.2 46.3 %all-to-all-start = ((bf16[32,16,1408]{2,1,0:T(8,128)(2,1)}), bf16[32,16,1408]{2,1,0:T(8,128)(2,1)S(1)}, u32[]{:S(2)}, u32[]{:S(2)}) async-start(bf16[32,16,1408]{2,1,0:T(8,128)(2,1)} %bitcast.3), calls=%async_computation | async-start | bytes 2883584 | tf_op jit(solution)/shard_map/all_to_all | solution.py:443
  22.7 39.9 %collective-permute-start.2 = (bf16[128,640]{1,0:T(8,128)(2,1)S(1)}, bf16[128,640]{1,0:T(8,128)(2,1)S(1)}, u32[]{:S(2)}, u32[]{:S(2)}) collective-permute-start(bf16[128,640]{1,0:T(8,128)(2,1)S(1)} %get-tuple-element.54), channel_id=1, source_target_pairs={{0,8},{8,16},{16,24},{24,0},{1,9},{9,17},{17,25},{25,1},{2,10},{10... | collective-permute-start | bytes 491528 | tf_op jit(solution)/shard_map/ppermute | solution.py:302
  23.2 39.4 %collective-permute-start.3 = (bf16[128,640]{1,0:T(8,128)(2,1)S(1)}, bf16[128,640]{1,0:T(8,128)(2,1)S(1)}, u32[]{:S(2)}, u32[]{:S(2)}) collective-permute-start(bf16[128,640]{1,0:T(8,128)(2,1)S(1)} %get-tuple-element.55), channel_id=1, source_target_pairs={{0,24},{8,0},{16,8},{24,16},{1,25},{9,1},{17,9},{25,17},{2,26},{10... | collective-permute-start | bytes 491528 | tf_op jit(solution)/shard_map/ppermute | solution.py:302
  56.5 19.4 %collective-permute-start.6 = (bf16[256,640]{1,0:T(8,128)(2,1)}, bf16[256,640]{1,0:T(8,128)(2,1)S(1)}, u32[]{:S(2)}, u32[]{:S(2)}) collective-permute-start(bf16[256,640]{1,0:T(8,128)(2,1)} %pad_maximum_fusion.refs_7_), channel_id=1, source_target_pairs={{0,8},{8,16},{16,24},{24,0},{1,9},{9,17},{17,25},{25,1},{2,10},{10... | collective-permute-start | bytes 983048 | tf_op jit(solution)/shard_map/ppermute | solution.py:302
  56.7 19.2 %collective-permute-start.7 = (bf16[256,640]{1,0:T(8,128)(2,1)}, bf16[256,640]{1,0:T(8,128)(2,1)}, u32[]{:S(2)}, u32[]{:S(2)}) collective-permute-start(bf16[256,640]{1,0:T(8,128)(2,1)} %pad_maximum_fusion.refs_7_), channel_id=1, source_target_pairs={{0,24},{8,0},{16,8},{24,16},{1,25},{9,1},{17,9},{25,17},{2,26},{10... | collective-permute-start | bytes 983048 | tf_op jit(solution)/shard_map/ppermute | solution.py:302
  77.1 12.1 %collective-permute-start.8 = (bf16[128,640]{1,0:T(8,128)(2,1)S(1)}, bf16[128,640]{1,0:T(8,128)(2,1)S(1)}, u32[]{:S(2)}, u32[]{:S(2)}) collective-permute-start(bf16[128,640]{1,0:T(8,128)(2,1)S(1)} %get-tuple-element.64), channel_id=1, source_target_pairs={{0,8},{8,16},{16,24},{24,0},{1,9},{9,17},{17,25},{25,1},{2,10},{10... | collective-permute-start | bytes 491528 | tf_op jit(solution)/shard_map/ppermute | solution.py:302
  77.2 12.1 %collective-permute-start.9 = (bf16[128,640]{1,0:T(8,128)(2,1)S(1)}, bf16[128,640]{1,0:T(8,128)(2,1)S(1)}, u32[]{:S(2)}, u32[]{:S(2)}) collective-permute-start(bf16[128,640]{1,0:T(8,128)(2,1)S(1)} %get-tuple-element.65), channel_id=1, source_target_pairs={{0,24},{8,0},{16,8},{24,16},{1,25},{9,1},{17,9},{25,17},{2,26},{10... | collective-permute-start | bytes 491528 | tf_op jit(solution)/shard_map/ppermute | solution.py:302
  83.2 23.3 %collective-permute-start.10 = (bf16[4,4,40,640]{3,2,1,0:T(8,128)(2,1)}, bf16[4,4,40,640]{3,2,1,0:T(8,128)(2,1)}, u32[]{:S(2)}, u32[]{:S(2)}) collective-permute-start(bf16[4,4,40,640]{3,2,1,0:T(8,128)(2,1)} %dynamic-slice_bitcast_fusion.1), channel_id=1, source_target_pairs={{0,1},{1,0},{2,3},{3,2},{4,5},{5,4},{6,7},{7,6},{8,9},{9,8},{10,11... | collective-permute-start | bytes 2457608 | tf_op jit(solution)/shard_map/ppermute | solution.py:426
  83.2 31.8 %collective-permute-start.4 = (bf16[128,640]{1,0:T(8,128)(2,1)S(1)}, bf16[128,640]{1,0:T(8,128)(2,1)S(1)}, u32[]{:S(2)}, u32[]{:S(2)}) collective-permute-start(bf16[128,640]{1,0:T(8,128)(2,1)S(1)} %copy-done.19), channel_id=1, source_target_pairs={{0,24},{8,0},{16,8},{24,16},{1,25},{9,1},{17,9},{25,17},{2,26},{10... | collective-permute-start | bytes 491528 | tf_op jit(solution)/shard_map/ppermute | solution.py:302
  83.2 31.8 %collective-permute-start.5 = (bf16[128,640]{1,0:T(8,128)(2,1)S(1)}, bf16[128,640]{1,0:T(8,128)(2,1)S(1)}, u32[]{:S(2)}, u32[]{:S(2)}) collective-permute-start(bf16[128,640]{1,0:T(8,128)(2,1)S(1)} %copy-done.18), channel_id=1, source_target_pairs={{0,8},{8,16},{16,24},{24,0},{1,9},{9,17},{17,25},{25,1},{2,10},{10... | collective-permute-start | bytes 491528 | tf_op jit(solution)/shard_map/ppermute | solution.py:302
  85.2 24.0 %all-to-all-start.1 = ((bf16[32,16,640]{2,1,0:T(8,128)(2,1)}), bf16[32,16,640]{2,1,0:T(8,128)(2,1)S(1)}, u32[]{:S(2)}, u32[]{:S(2)}) async-start(bf16[32,16,640]{2,1,0:T(8,128)(2,1)} %bitcast.7), calls=%async_computation.1 | async-start | bytes 1310720 | tf_op jit(solution)/shard_map/all_to_all | solution.py:443
  102.7 13.8 %collective-permute-start.11 = (bf16[128,640]{1,0:T(8,128)(2,1)}, bf16[128,640]{1,0:T(8,128)(2,1)S(1)}, u32[]{:S(2)}, u32[]{:S(2)}) collective-permute-start(bf16[128,640]{1,0:T(8,128)(2,1)} %get-tuple-element.75), channel_id=1, source_target_pairs={{0,24},{8,0},{16,8},{24,16},{1,25},{9,1},{17,9},{25,17},{2,26},{10... | collective-permute-start | bytes 491528 | tf_op jit(solution)/shard_map/ppermute | solution.py:302
  106.4 10.1 %collective-permute-start.12 = (bf16[128,640]{1,0:T(8,128)(2,1)}, bf16[128,640]{1,0:T(8,128)(2,1)S(1)}, u32[]{:S(2)}, u32[]{:S(2)}) collective-permute-start(bf16[128,640]{1,0:T(8,128)(2,1)} %get-tuple-element.76), channel_id=1, source_target_pairs={{0,8},{8,16},{16,24},{24,0},{1,9},{9,17},{17,25},{25,1},{2,10},{10... | collective-permute-start | bytes 491528 | tf_op jit(solution)/shard_map/ppermute | solution.py:302
  109.2 59.3 %all-to-all-start.2 = ((bf16[32,16,768]{2,1,0:T(8,128)(2,1)}), bf16[32,16,768]{2,1,0:T(8,128)(2,1)S(1)}, u32[]{:S(2)}, u32[]{:S(2)}) async-start(bf16[32,16,768]{2,1,0:T(8,128)(2,1)} %bitcast.72), calls=%async_computation.2 | async-start | bytes 1572864 | tf_op jit(solution)/shard_map/all_to_all | solution.py:443
  116.7 50.1 %collective-permute-start.13 = (bf16[256,640]{1,0:T(8,128)(2,1)S(1)}, bf16[256,640]{1,0:T(8,128)(2,1)S(1)}, u32[]{:S(2)}, u32[]{:S(2)}) collective-permute-start(bf16[256,640]{1,0:T(8,128)(2,1)S(1)} %get-tuple-element.77), channel_id=1, source_target_pairs={{0,24},{8,0},{16,8},{24,16},{1,25},{9,1},{17,9},{25,17},{2,26},{10... | collective-permute-start | bytes 983048 | tf_op jit(solution)/shard_map/ppermute | solution.py:302
  120.3 46.5 %collective-permute-start.14 = (bf16[256,640]{1,0:T(8,128)(2,1)S(1)}, bf16[256,640]{1,0:T(8,128)(2,1)S(1)}, u32[]{:S(2)}, u32[]{:S(2)}) collective-permute-start(bf16[256,640]{1,0:T(8,128)(2,1)S(1)} %get-tuple-element.78), channel_id=1, source_target_pairs={{0,8},{8,16},{16,24},{24,0},{1,9},{9,17},{17,25},{25,1},{2,10},{10... | collective-permute-start | bytes 983048 | tf_op jit(solution)/shard_map/ppermute | solution.py:302
  120.3 15.6 %collective-permute-start.17 = (bf16[4,2,40,640]{3,2,1,0:T(8,128)(2,1)S(1)}, bf16[4,2,40,640]{3,2,1,0:T(8,128)(2,1)S(1)}, u32[]{:S(2)}, u32[]{:S(2)}) collective-permute-start(bf16[4,2,40,640]{3,2,1,0:T(8,128)(2,1)S(1)} %dynamic-slice_bitcast_fusion.3), channel_id=1, source_target_pairs={{0,2},{1,3},{2,0},{3,1},{4,6},{5,7},{6,4},{7,5},{8,10},{9,11},{10,... | collective-permute-start | bytes 1228808 | tf_op jit(solution)/shard_map/ppermute | solution.py:426
  122.2 14.8 %collective-permute-start.20 = (bf16[4,2,40,640]{3,2,0,1:T(8,128)(2,1)S(1)}, bf16[4,2,40,640]{3,2,0,1:T(8,128)(2,1)S(1)}, u32[]{:S(2)}, u32[]{:S(2)}) collective-permute-start(bf16[4,2,40,640]{3,2,0,1:T(8,128)(2,1)S(1)} %dynamic-slice_bitcast_fusion.2), channel_id=1, source_target_pairs={{0,4},{1,5},{2,6},{3,7},{4,0},{5,1},{6,2},{7,3},{8,12},{9,13},{10,... | collective-permute-start | bytes 1228808 | tf_op jit(solution)/shard_map/ppermute | solution.py:426
  123.9 28.1 %collective-permute-start.15 = (bf16[256,640]{1,0:T(8,128)(2,1)S(1)}, bf16[256,640]{1,0:T(8,128)(2,1)S(1)}, u32[]{:S(2)}, u32[]{:S(2)}) collective-permute-start(bf16[256,640]{1,0:T(8,128)(2,1)S(1)} %get-tuple-element.84), channel_id=1, source_target_pairs={{0,24},{8,0},{16,8},{24,16},{1,25},{9,1},{17,9},{25,17},{2,26},{10... | collective-permute-start | bytes 983048 | tf_op jit(solution)/shard_map/ppermute | solution.py:302
  135.9 27.3 %collective-permute-start.16 = (bf16[256,640]{1,0:T(8,128)(2,1)S(1)}, bf16[256,640]{1,0:T(8,128)(2,1)S(1)}, u32[]{:S(2)}, u32[]{:S(2)}) collective-permute-start(bf16[256,640]{1,0:T(8,128)(2,1)S(1)} %get-tuple-element.85), channel_id=1, source_target_pairs={{0,8},{8,16},{16,24},{24,0},{1,9},{9,17},{17,25},{25,1},{2,10},{10... | collective-permute-start | bytes 983048 | tf_op jit(solution)/shard_map/ppermute | solution.py:302
  149.0 22.4 %collective-permute-start.22 = (bf16[40,1280]{1,0:T(8,128)(2,1)S(1)}, bf16[40,1280]{1,0:T(8,128)(2,1)S(1)}, u32[]{:S(2)}, u32[]{:S(2)}) collective-permute-start(bf16[40,1280]{1,0:T(8,128)(2,1)S(1)} %get-tuple-element.93), channel_id=1, source_target_pairs={{0,8},{8,0},{16,24},{24,16},{1,9},{9,1},{17,25},{25,17},{2,10},{10... | collective-permute-start | bytes 307208 | tf_op jit(solution)/shard_map/ppermute | solution.py:437
  152.0 19.5 %collective-permute-start.23 = (bf16[40,1280]{1,0:T(8,128)(2,1)S(1)}, bf16[40,1280]{1,0:T(8,128)(2,1)S(1)}, u32[]{:S(2)}, u32[]{:S(2)}) collective-permute-start(bf16[40,1280]{1,0:T(8,128)(2,1)S(1)} %get-tuple-element.94), channel_id=1, source_target_pairs={{0,16},{8,24},{16,0},{24,8},{1,17},{9,25},{17,1},{25,9},{2,18},{10... | collective-permute-start | bytes 307208 | tf_op jit(solution)/shard_map/ppermute | solution.py:437
  (28 other events, 157.3 us)

commit v5 on v4

--- a/solution.py
+++ b/solution.py
@@ -263,13 +263,21 @@
     return outs[: len(parts)], *outs[len(parts) :]
 
 
-def pick_kernel(pair_cap, target_ref, first_ref, second_ref, out_ref, gate_ref):
-    slots, half = first_ref.shape
+def picked(target_ref, returned):
+    slots = returned.shape[0]
     target = as_column(target_ref[...].astype(jnp.float32))
     place = target == iota((slots, slots), 1).astype(jnp.float32)
     place = jnp.where(place, 1.0, 0.0).astype(jnp.bfloat16)
-    out_ref[:, :half] = mm(place, first_ref[...]).astype(jnp.bfloat16)
-    out_ref[:, half:] = mm(place, second_ref[:, :half]).astype(jnp.bfloat16)
+    return mm(place, returned).astype(jnp.bfloat16)
+
+
+def pick_first_kernel(target_ref, first_ref, out_ref):
+    out_ref[...] = picked(target_ref, first_ref[...])
+
+
+def pick_second_kernel(pair_cap, target_ref, second_ref, _, out_ref, gate_ref):
+    half = out_ref.shape[1]
+    out_ref[...] = picked(target_ref, second_ref[:, :half])
     shares = second_ref[:, half:].astype(jnp.float32)
     shares = jnp.where(iota(shares.shape, 0) % pair_cap == 0, shares, 0.0)
     gate_ref[...] = jnp.sum(jnp.sum(shares, axis=0, keepdims=True), axis=1, keepdims=True)
@@ -277,23 +285,36 @@
 
 def pick_rows(target, first, second, pair_cap):
     slots, half = first.shape
-    vmem = pl.BlockSpec(memory_space=pltpu.VMEM)
+    whole = lambda i: (0, 0)
+    shape = jax.ShapeDtypeStruct((slots, 2 * half), jnp.bfloat16)
+    cost = pl.CostEstimate(
+        flops=2 * slots * slots * half, bytes_accessed=4 * slots * half, transcendentals=0
+    )
+    left = pl.pallas_call(
+        pick_first_kernel,
+        grid=(1,),
+        out_shape=shape,
+        in_specs=[pl.BlockSpec((1, slots), whole), pl.BlockSpec((slots, half), whole)],
+        out_specs=pl.BlockSpec((slots, half), whole),
+        compiler_params=params(),
+        name="pick_first",
+        cost_estimate=cost,
+    )(target, first)
     return pl.pallas_call(
-        lambda *refs: pick_kernel(pair_cap, *refs),
-        out_shape=(
-            jax.ShapeDtypeStruct((slots, 2 * half), jnp.bfloat16),
-            jax.ShapeDtypeStruct((1, 1), jnp.float32),
-        ),
-        in_specs=[vmem, vmem, vmem],
-        out_specs=(vmem, vmem),
-        compiler_params=params(),
-        name="pick_rows",
-        cost_estimate=pl.CostEstimate(
-            flops=4 * slots * slots * half,
-            bytes_accessed=8 * slots * half,
-            transcendentals=0,
-        ),
-    )(target, first, second)
+        lambda *refs: pick_second_kernel(pair_cap, *refs),
+        grid=(1,),
+        out_shape=(shape, jax.ShapeDtypeStruct((1, 1), jnp.float32)),
+        in_specs=[
+            pl.BlockSpec((1, slots), whole),
+            pl.BlockSpec(second.shape, whole),
+            pl.BlockSpec(memory_space=pl.ANY),
+        ],
+        out_specs=(pl.BlockSpec((slots, half), lambda i: (0, 1)), pl.BlockSpec((1, 1), whole)),
+        input_output_aliases={2: 0},
+        compiler_params=params(),
+        name="pick_second",
+        cost_estimate=cost,
+    )(target, second, left)
 
 
 def shift(value, step):

time: 174 us -> 174 us (level)
    unnamed x48 -> x52, local copies, waits for them, and re-layouts: 5.3 us -> 5.32 us
  transfers between devices with their start and end apart: 28 -> 28, of which waited for: 8 -> 9; matrix products, arithmetic and copies ran while one was open for 5% -> 5% of each run, Pallas kernels for 18% -> 18%
where the time goes in v5:
time: 174 us; the launch traced here: 173 us
  starting transfers between devices  65.8 us (38%)
  waiting for transfers between devices  54.9 us (32%)
  Pallas kernels  32.8 us (19%)
  local copies, waits for them, and re-layouts  10.8 us (6%)
  other arithmetic  4.61 us (3%)
  between operations  4.24 us (2%)
    ppermute x16, starting transfers between devices, shift(): return lax.ppermute(value, 'ctx', pairs)  30.8 us
    all_to_all x3, waiting for transfers between devices, exchange(): lax.all_to_all(value.reshape(count, slots // count, width), ('ctx', 'rec'...  28.7 us
    pallas_call x2, Pallas kernels, attention(): pl.pallas_call(lambda *refs: attention_kernel(len(parts) - 1, pairs, *ref...  24 us
    ppermute x6, waiting for transfers between devices, halve(): lax.ppermute(half(1 - mine), 'rec', [(i, i ^ 1 << bit) for i in range(rec...  15.7 us
    ppermute x3, starting transfers between devices, sum_blocks(): total = total + lax.ppermute(sent, 'ctx', pairs).astype(jnp.float32)  15 us
    all_to_all x3, starting transfers between devices, exchange(): lax.all_to_all(value.reshape(count, slots // count, width), ('ctx', 'rec'...  14 us
    ppermute x16, waiting for transfers between devices, shift(): return lax.ppermute(value, 'ctx', pairs)  10.1 us
    ppermute x6, starting transfers between devices, halve(): lax.ppermute(half(1 - mine), 'rec', [(i, i ^ 1 << bit) for i in range(rec...  5.87 us
  transfers between devices with their start and end apart: 28, of which 9 were waited for; matrix products, arithmetic and copies ran while one was open for 5% of the time, Pallas kernels for 18%

profile of v5, /device:TPU:0, one launch (start us, length us, event | category | flops | bytes accessed | tf_op | source)
XLA Modules:
  0.0 173.1 jit_solution(1825623275221741365)
XLA Ops:
  2.0 3.1 %collective-permute-start.2 = (bf16[256,640]{1,0:T(8,128)(2,1)S(1)}, bf16[256,640]{1,0:T(8,128)(2,1)S(1)}, u32[]{:S(2)}, u32[]{:S(2)}) collective-permute-start(bf16[256,640]{1,0:T(8,128)(2,1)S(1)} %pad_maximum_fusion.1.refs_7_), channel_id=1, source_target_pairs={{0,8},{8,16},{16,24},{24,0},{1,9},{9,17},{17,25},{25,1},{2,10},{10... | collective-permute-start | bytes 983048 | tf_op jit(solution)/shard_map/ppermute | solution.py:323
  5.1 2.1 %collective-permute-start.3 = (bf16[256,640]{1,0:T(8,128)(2,1)S(1)}, bf16[256,640]{1,0:T(8,128)(2,1)S(1)}, u32[]{:S(2)}, u32[]{:S(2)}) collective-permute-start(bf16[256,640]{1,0:T(8,128)(2,1)S(1)} %pad_maximum_fusion.1.refs_7_), channel_id=1, source_target_pairs={{0,24},{8,0},{16,8},{24,16},{1,25},{9,1},{17,9},{25,17},{2,26},{10... | collective-permute-start | bytes 983048 | tf_op jit(solution)/shard_map/ppermute | solution.py:323
  7.9 2.3 %route_prep.1 = (bf16[512,1408]{1,0:T(8,128)(2,1)}, s32[1,512]{1,0:T(1,128)S(1)}) custom-call(s32[1]{0:T(128)S(6)} %copy.21.refs_0_, s32[1,512]{1,0:T(1,128)S(1)} %bitcast.62, s32[1,512]{1,0:T(1,128)S(1)} %bitcast.63, bf16[512,1280]{1,0:T(8,128)(2,1)S(1)} %copy-done.3), custom_call_target="tpu_custom_call" | custom-call | flops 671088640 | bytes 2621440 | tf_op jit(solution)/shard_map/route_prep/pallas_call | solution.py:66
  10.2 4.2 %all-to-all-start = ((bf16[32,16,1408]{2,1,0:T(8,128)(2,1)}), bf16[32,16,1408]{2,1,0:T(8,128)(2,1)S(1)}, u32[]{:S(2)}, u32[]{:S(2)}) async-start(bf16[32,16,1408]{2,1,0:T(8,128)(2,1)} %bitcast.2), calls=%async_computation | async-start | bytes 2883584 | tf_op jit(solution)/shard_map/all_to_all | solution.py:464
  15.7 6.3 %collective-permute-done.3.behind_ref.refs_9_ = bf16[256,640]{1,0:T(8,128)(2,1)S(1)} collective-permute-done((bf16[256,640]{1,0:T(8,128)(2,1)S(1)}, bf16[256,640]{1,0:T(8,128)(2,1)S(1)}, u32[]{:S(2)}, u32[]{:S(2)}) %collective-permute-start.3) | collective-permute-done | bytes 327712 | tf_op jit(solution)/shard_map/ppermute | solution.py:323
  23.2 3.3 %collective-permute-start.5 = (bf16[128,640]{1,0:T(8,128)(2,1)S(1)}, bf16[128,640]{1,0:T(8,128)(2,1)S(1)}, u32[]{:S(2)}, u32[]{:S(2)}) collective-permute-start(bf16[128,640]{1,0:T(8,128)(2,1)S(1)} %get-tuple-element.56), channel_id=1, source_target_pairs={{0,24},{8,0},{16,8},{24,16},{1,25},{9,1},{17,9},{25,17},{2,26},{10... | collective-permute-start | bytes 491528 | tf_op jit(solution)/shard_map/ppermute | solution.py:323
  28.0 28.5 %all-to-all-done = bf16[32,16,1408]{2,1,0:T(8,128)(2,1)S(1)} async-done(((bf16[32,16,1408]{2,1,0:T(8,128)(2,1)}), bf16[32,16,1408]{2,1,0:T(8,128)(2,1)S(1)}, u32[]{:S(2)}, u32[]{:S(2)}) %all-to-all-start) | async-done | bytes 1441824 | tf_op jit(solution)/shard_map/all_to_all | solution.py:464
  56.7 3.6 %collective-permute-start.1 = (bf16[256,640]{1,0:T(8,128)(2,1)}, bf16[256,640]{1,0:T(8,128)(2,1)}, u32[]{:S(2)}, u32[]{:S(2)}) collective-permute-start(bf16[256,640]{1,0:T(8,128)(2,1)} %pad_maximum_fusion.refs_7_), channel_id=1, source_target_pairs={{0,24},{8,0},{16,8},{24,16},{1,25},{9,1},{17,9},{25,17},{2,26},{10... | collective-permute-start | bytes 983048 | tf_op jit(solution)/shard_map/ppermute | solution.py:323
  63.9 11.9 %attention.2 = (bf16[256,640]{1,0:T(8,128)(2,1)}, bf16[256,640]{1,0:T(8,128)(2,1)}, bf16[256,640]{1,0:T(8,128)(2,1)}, bf16[128,640]{1,0:T(8,128)(2,1)}, bf16[128...) custom-call(f32[1]{0:T(128)S(6)} %copy.20.refs_0_, ...), custom_call_target="tpu_custom_call" | custom-call | flops 12582912000 | bytes 4587520 | tf_op jit(solution)/shard_map/attention/pallas_call | solution.py:230
  77.1 3.8 %collective-permute-start.7 = (bf16[128,640]{1,0:T(8,128)(2,1)S(1)}, bf16[128,640]{1,0:T(8,128)(2,1)S(1)}, u32[]{:S(2)}, u32[]{:S(2)}) collective-permute-start(bf16[128,640]{1,0:T(8,128)(2,1)S(1)} %get-tuple-element.63), channel_id=1, source_target_pairs={{0,24},{8,0},{16,8},{24,16},{1,25},{9,1},{17,9},{25,17},{2,26},{10... | collective-permute-start | bytes 491528 | tf_op jit(solution)/shard_map/ppermute | solution.py:323
  81.0 2.1 %dynamic-slice_bitcast_fusion.1 = bf16[4,4,40,640]{3,2,1,0:T(8,128)(2,1)} fusion(bf16[4,4,2,40,640]{4,3,2,1,0:T(8,128)(2,1)} %bitcast.68, s32[]{:T(128)S(6)} %select_n.43), kind=kLoop, calls=%fused_computation.9 | loop fusion | bytes 1638404 | tf_op jit(solution)/shard_map/jit(dynamic_index_in_dim)/squeeze | solution.py:445
  85.1 4.0 %all-to-all-start.2 = ((bf16[32,16,640]{2,1,0:T(8,128)(2,1)}), bf16[32,16,640]{2,1,0:T(8,128)(2,1)S(1)}, u32[]{:S(2)}, u32[]{:S(2)}) async-start(bf16[32,16,640]{2,1,0:T(8,128)(2,1)} %bitcast.9), calls=%async_computation.2 | async-start | bytes 1310720 | tf_op jit(solution)/shard_map/all_to_all | solution.py:464
  90.5 12.2 %attention.3 = (bf16[256,640]{1,0:T(8,128)(2,1)}, bf16[256,640]{1,0:T(8,128)(2,1)}, bf16[256,640]{1,0:T(8,128)(2,1)}, bf16[128,640]{1,0:T(8,128)(2,1)}, bf16[128...) custom-call(f32[1]{0:T(128)S(6)} %copy.20.refs_0_, ...), custom_call_target="tpu_custom_call" | custom-call | flops 12582912000 | bytes 4587520 | tf_op jit(solution)/shard_map/attention/pallas_call | solution.py:230
  102.7 3.7 %collective-permute-start.11 = (bf16[128,640]{1,0:T(8,128)(2,1)}, bf16[128,640]{1,0:T(8,128)(2,1)S(1)}, u32[]{:S(2)}, u32[]{:S(2)}) collective-permute-start(bf16[128,640]{1,0:T(8,128)(2,1)} %get-tuple-element.75), channel_id=1, source_target_pairs={{0,24},{8,0},{16,8},{24,16},{1,25},{9,1},{17,9},{25,17},{2,26},{10... | collective-permute-start | bytes 491528 | tf_op jit(solution)/shard_map/ppermute | solution.py:323
  106.4 2.5 %fusion.1 = bf16[4,4,40,640]{3,2,1,0:T(8,128)(2,1)} fusion(bf16[4,4,40,640]{3,2,1,0:T(8,128)(2,1)} %collective-permute-done.10, bf16[4,4,2,40,640]{4,3,2,1,0:T(8,128)(2,1)} %bitcast.69, s32[]{:T(128)S(6)} %select_n.42), kind=kLoop, calls=%fused_computation.3 | loop fusion | flops 1638400 | bytes 2457604 | tf_op jit(solution)/shard_map/convert_element_type | solution.py:364
  109.1 5.8 %all-to-all-start.1 = ((bf16[32,16,768]{2,1,0:T(8,128)(2,1)}), bf16[32,16,768]{2,1,0:T(8,128)(2,1)S(1)}, u32[]{:S(2)}, u32[]{:S(2)}) async-start(bf16[32,16,768]{2,1,0:T(8,128)(2,1)} %bitcast.72), calls=%async_computation.1 | async-start | bytes 1572864 | tf_op jit(solution)/shard_map/all_to_all | solution.py:464
  116.7 3.6 %collective-permute-start.13 = (bf16[256,640]{1,0:T(8,128)(2,1)S(1)}, bf16[256,640]{1,0:T(8,128)(2,1)S(1)}, u32[]{:S(2)}, u32[]{:S(2)}) collective-permute-start(bf16[256,640]{1,0:T(8,128)(2,1)S(1)} %get-tuple-element.77), channel_id=1, source_target_pairs={{0,24},{8,0},{16,8},{24,16},{1,25},{9,1},{17,9},{25,17},{2,26},{10... | collective-permute-start | bytes 983048 | tf_op jit(solution)/shard_map/ppermute | solution.py:323
  123.9 3.9 %collective-permute-start.15 = (bf16[256,640]{1,0:T(8,128)(2,1)S(1)}, bf16[256,640]{1,0:T(8,128)(2,1)S(1)}, u32[]{:S(2)}, u32[]{:S(2)}) collective-permute-start(bf16[256,640]{1,0:T(8,128)(2,1)S(1)} %get-tuple-element.84), channel_id=1, source_target_pairs={{0,24},{8,0},{16,8},{24,16},{1,25},{9,1},{17,9},{25,17},{2,26},{10... | collective-permute-start | bytes 983048 | tf_op jit(solution)/shard_map/ppermute | solution.py:323
  129.5 6.4 %collective-permute-done.17 = bf16[4,2,40,640]{3,2,1,0:T(8,128)(2,1)S(1)} collective-permute-done((bf16[4,2,40,640]{3,2,1,0:T(8,128)(2,1)S(1)}, bf16[4,2,40,640]{3,2,1,0:T(8,128)(2,1)S(1)}, u32[]{:S(2)}, u32[]{:S(2)}) %collective-permute-start.17) | collective-permute-done | bytes 409632 | tf_op jit(solution)/shard_map/ppermute | solution.py:447
  138.7 4.5 %collective-permute-done.18 = bf16[4,1,40,640]{3,2,1,0:T(8,128)(2,1)S(1)} collective-permute-done((bf16[4,1,40,640]{3,2,1,0:T(8,128)(2,1)S(1)}, bf16[4,1,40,640]{3,2,1,0:T(8,128)(2,1)S(1)}, u32[]{:S(2)}, u32[]{:S(2)}) %collective-permute-start.18) | collective-permute-done | bytes 204832 | tf_op jit(solution)/shard_map/ppermute | solution.py:447
  144.3 4.8 %collective-permute-done.21 = bf16[4,1,40,640]{3,2,0,1:T(8,128)(2,1)S(1)} collective-permute-done((bf16[4,1,40,640]{3,2,0,1:T(8,128)(2,1)S(1)}, bf16[4,1,40,640]{3,2,0,1:T(8,128)(2,1)S(1)}, u32[]{:S(2)}, u32[]{:S(2)}) %collective-permute-start.21) | collective-permute-done | bytes 204832 | tf_op jit(solution)/shard_map/ppermute | solution.py:447
  149.6 2.4 %collective-permute-done.15.back_ref = bf16[256,640]{1,0:T(8,128)(2,1)S(1)} collective-permute-done((bf16[256,640]{1,0:T(8,128)(2,1)S(1)}, bf16[256,640]{1,0:T(8,128)(2,1)S(1)}, u32[]{:S(2)}, u32[]{:S(2)}) %collective-permute-start.15) | collective-permute-done | bytes 327712 | tf_op jit(solution)/shard_map/ppermute | solution.py:323
  152.0 11.2 %collective-permute-start.23 = (bf16[40,1280]{1,0:T(8,128)(2,1)S(1)}, bf16[40,1280]{1,0:T(8,128)(2,1)S(1)}, u32[]{:S(2)}, u32[]{:S(2)}) collective-permute-start(bf16[40,1280]{1,0:T(8,128)(2,1)S(1)} %get-tuple-element.94), channel_id=1, source_target_pairs={{0,16},{8,24},{16,0},{24,8},{1,17},{9,25},{17,1},{25,9},{2,18},{10... | collective-permute-start | bytes 307208 | tf_op jit(solution)/shard_map/ppermute | solution.py:458
  163.2 3.4 %collective-permute-start.24 = (bf16[40,1280]{1,0:T(8,128)(2,1)S(1)}, bf16[40,1280]{1,0:T(8,128)(2,1)S(1)}, u32[]{:S(2)}, u32[]{:S(2)}) collective-permute-start(bf16[40,1280]{1,0:T(8,128)(2,1)S(1)} %get-tuple-element.95), channel_id=1, source_target_pairs={{0,24},{8,16},{16,8},{24,0},{1,25},{9,17},{17,9},{25,1},{2,26},{10... | collective-permute-start | bytes 307208 | tf_op jit(solution)/shard_map/ppermute | solution.py:458
  (115 shorter events, 29.5 us)
Async XLA Ops:
  2.0 13.7 %collective-permute-start.2 = (bf16[256,640]{1,0:T(8,128)(2,1)S(1)}, bf16[256,640]{1,0:T(8,128)(2,1)S(1)}, u32[]{:S(2)}, u32[]{:S(2)}) collective-permute-start(bf16[256,640]{1,0:T(8,128)(2,1)S(1)} %pad_maximum_fusion.1.refs_7_), channel_id=1, source_target_pairs={{0,8},{8,16},{16,24},{24,0},{1,9},{9,17},{17,25},{25,1},{2,10},{10... | collective-permute-start | bytes 983048 | tf_op jit(solution)/shard_map/ppermute | solution.py:323
  5.1 16.9 %collective-permute-start.3 = (bf16[256,640]{1,0:T(8,128)(2,1)S(1)}, bf16[256,640]{1,0:T(8,128)(2,1)S(1)}, u32[]{:S(2)}, u32[]{:S(2)}) collective-permute-start(bf16[256,640]{1,0:T(8,128)(2,1)S(1)} %pad_maximum_fusion.1.refs_7_), channel_id=1, source_target_pairs={{0,24},{8,0},{16,8},{24,16},{1,25},{9,1},{17,9},{25,17},{2,26},{10... | collective-permute-start | bytes 983048 | tf_op jit(solution)/shard_map/ppermute | solution.py:323
  10.2 46.3 %all-to-all-start = ((bf16[32,16,1408]{2,1,0:T(8,128)(2,1)}), bf16[32,16,1408]{2,1,0:T(8,128)(2,1)S(1)}, u32[]{:S(2)}, u32[]{:S(2)}) async-start(bf16[32,16,1408]{2,1,0:T(8,128)(2,1)} %bitcast.2), calls=%async_computation | async-start | bytes 2883584 | tf_op jit(solution)/shard_map/all_to_all | solution.py:464
  22.7 39.9 %collective-permute-start.4 = (bf16[128,640]{1,0:T(8,128)(2,1)S(1)}, bf16[128,640]{1,0:T(8,128)(2,1)S(1)}, u32[]{:S(2)}, u32[]{:S(2)}) collective-permute-start(bf16[128,640]{1,0:T(8,128)(2,1)S(1)} %get-tuple-element.55), channel_id=1, source_target_pairs={{0,8},{8,16},{16,24},{24,0},{1,9},{9,17},{17,25},{25,1},{2,10},{10... | collective-permute-start | bytes 491528 | tf_op jit(solution)/shard_map/ppermute | solution.py:323
  23.2 39.4 %collective-permute-start.5 = (bf16[128,640]{1,0:T(8,128)(2,1)S(1)}, bf16[128,640]{1,0:T(8,128)(2,1)S(1)}, u32[]{:S(2)}, u32[]{:S(2)}) collective-permute-start(bf16[128,640]{1,0:T(8,128)(2,1)S(1)} %get-tuple-element.56), channel_id=1, source_target_pairs={{0,24},{8,0},{16,8},{24,16},{1,25},{9,1},{17,9},{25,17},{2,26},{10... | collective-permute-start | bytes 491528 | tf_op jit(solution)/shard_map/ppermute | solution.py:323
  56.5 19.4 %collective-permute-start = (bf16[256,640]{1,0:T(8,128)(2,1)}, bf16[256,640]{1,0:T(8,128)(2,1)S(1)}, u32[]{:S(2)}, u32[]{:S(2)}) collective-permute-start(bf16[256,640]{1,0:T(8,128)(2,1)} %pad_maximum_fusion.refs_7_), channel_id=1, source_target_pairs={{0,8},{8,16},{16,24},{24,0},{1,9},{9,17},{17,25},{25,1},{2,10},{10... | collective-permute-start | bytes 983048 | tf_op jit(solution)/shard_map/ppermute | solution.py:323
  56.7 19.2 %collective-permute-start.1 = (bf16[256,640]{1,0:T(8,128)(2,1)}, bf16[256,640]{1,0:T(8,128)(2,1)}, u32[]{:S(2)}, u32[]{:S(2)}) collective-permute-start(bf16[256,640]{1,0:T(8,128)(2,1)} %pad_maximum_fusion.refs_7_), channel_id=1, source_target_pairs={{0,24},{8,0},{16,8},{24,16},{1,25},{9,1},{17,9},{25,17},{2,26},{10... | collective-permute-start | bytes 983048 | tf_op jit(solution)/shard_map/ppermute | solution.py:323
  77.1 12.1 %collective-permute-start.6 = (bf16[128,640]{1,0:T(8,128)(2,1)S(1)}, bf16[128,640]{1,0:T(8,128)(2,1)S(1)}, u32[]{:S(2)}, u32[]{:S(2)}) collective-permute-start(bf16[128,640]{1,0:T(8,128)(2,1)S(1)} %get-tuple-element.62), channel_id=1, source_target_pairs={{0,8},{8,16},{16,24},{24,0},{1,9},{9,17},{17,25},{25,1},{2,10},{10... | collective-permute-start | bytes 491528 | tf_op jit(solution)/shard_map/ppermute | solution.py:323
  77.1 12.1 %collective-permute-start.7 = (bf16[128,640]{1,0:T(8,128)(2,1)S(1)}, bf16[128,640]{1,0:T(8,128)(2,1)S(1)}, u32[]{:S(2)}, u32[]{:S(2)}) collective-permute-start(bf16[128,640]{1,0:T(8,128)(2,1)S(1)} %get-tuple-element.63), channel_id=1, source_target_pairs={{0,24},{8,0},{16,8},{24,16},{1,25},{9,1},{17,9},{25,17},{2,26},{10... | collective-permute-start | bytes 491528 | tf_op jit(solution)/shard_map/ppermute | solution.py:323
  83.1 23.3 %collective-permute-start.10 = (bf16[4,4,40,640]{3,2,1,0:T(8,128)(2,1)}, bf16[4,4,40,640]{3,2,1,0:T(8,128)(2,1)}, u32[]{:S(2)}, u32[]{:S(2)}) collective-permute-start(bf16[4,4,40,640]{3,2,1,0:T(8,128)(2,1)} %dynamic-slice_bitcast_fusion.1), channel_id=1, source_target_pairs={{0,1},{1,0},{2,3},{3,2},{4,5},{5,4},{6,7},{7,6},{8,9},{9,8},{10,11... | collective-permute-start | bytes 2457608 | tf_op jit(solution)/shard_map/ppermute | solution.py:447
  83.1 31.8 %collective-permute-start.8 = (bf16[128,640]{1,0:T(8,128)(2,1)S(1)}, bf16[128,640]{1,0:T(8,128)(2,1)S(1)}, u32[]{:S(2)}, u32[]{:S(2)}) collective-permute-start(bf16[128,640]{1,0:T(8,128)(2,1)S(1)} %copy-done.21), channel_id=1, source_target_pairs={{0,24},{8,0},{16,8},{24,16},{1,25},{9,1},{17,9},{25,17},{2,26},{10... | collective-permute-start | bytes 491528 | tf_op jit(solution)/shard_map/ppermute | solution.py:323
  83.1 31.8 %collective-permute-start.9 = (bf16[128,640]{1,0:T(8,128)(2,1)S(1)}, bf16[128,640]{1,0:T(8,128)(2,1)S(1)}, u32[]{:S(2)}, u32[]{:S(2)}) collective-permute-start(bf16[128,640]{1,0:T(8,128)(2,1)S(1)} %copy-done.20), channel_id=1, source_target_pairs={{0,8},{8,16},{16,24},{24,0},{1,9},{9,17},{17,25},{25,1},{2,10},{10... | collective-permute-start | bytes 491528 | tf_op jit(solution)/shard_map/ppermute | solution.py:323
  85.1 23.9 %all-to-all-start.2 = ((bf16[32,16,640]{2,1,0:T(8,128)(2,1)}), bf16[32,16,640]{2,1,0:T(8,128)(2,1)S(1)}, u32[]{:S(2)}, u32[]{:S(2)}) async-start(bf16[32,16,640]{2,1,0:T(8,128)(2,1)} %bitcast.9), calls=%async_computation.2 | async-start | bytes 1310720 | tf_op jit(solution)/shard_map/all_to_all | solution.py:464
  102.7 13.9 %collective-permute-start.11 = (bf16[128,640]{1,0:T(8,128)(2,1)}, bf16[128,640]{1,0:T(8,128)(2,1)S(1)}, u32[]{:S(2)}, u32[]{:S(2)}) collective-permute-start(bf16[128,640]{1,0:T(8,128)(2,1)} %get-tuple-element.75), channel_id=1, source_target_pairs={{0,24},{8,0},{16,8},{24,16},{1,25},{9,1},{17,9},{25,17},{2,26},{10... | collective-permute-start | bytes 491528 | tf_op jit(solution)/shard_map/ppermute | solution.py:323
  106.4 10.2 %collective-permute-start.12 = (bf16[128,640]{1,0:T(8,128)(2,1)}, bf16[128,640]{1,0:T(8,128)(2,1)S(1)}, u32[]{:S(2)}, u32[]{:S(2)}) collective-permute-start(bf16[128,640]{1,0:T(8,128)(2,1)} %get-tuple-element.76), channel_id=1, source_target_pairs={{0,8},{8,16},{16,24},{24,0},{1,9},{9,17},{17,25},{25,1},{2,10},{10... | collective-permute-start | bytes 491528 | tf_op jit(solution)/shard_map/ppermute | solution.py:323
  109.1 59.3 %all-to-all-start.1 = ((bf16[32,16,768]{2,1,0:T(8,128)(2,1)}), bf16[32,16,768]{2,1,0:T(8,128)(2,1)S(1)}, u32[]{:S(2)}, u32[]{:S(2)}) async-start(bf16[32,16,768]{2,1,0:T(8,128)(2,1)} %bitcast.72), calls=%async_computation.1 | async-start | bytes 1572864 | tf_op jit(solution)/shard_map/all_to_all | solution.py:464
  116.7 50.0 %collective-permute-start.13 = (bf16[256,640]{1,0:T(8,128)(2,1)S(1)}, bf16[256,640]{1,0:T(8,128)(2,1)S(1)}, u32[]{:S(2)}, u32[]{:S(2)}) collective-permute-start(bf16[256,640]{1,0:T(8,128)(2,1)S(1)} %get-tuple-element.77), channel_id=1, source_target_pairs={{0,24},{8,0},{16,8},{24,16},{1,25},{9,1},{17,9},{25,17},{2,26},{10... | collective-permute-start | bytes 983048 | tf_op jit(solution)/shard_map/ppermute | solution.py:323
  120.3 46.4 %collective-permute-start.14 = (bf16[256,640]{1,0:T(8,128)(2,1)S(1)}, bf16[256,640]{1,0:T(8,128)(2,1)S(1)}, u32[]{:S(2)}, u32[]{:S(2)}) collective-permute-start(bf16[256,640]{1,0:T(8,128)(2,1)S(1)} %get-tuple-element.78), channel_id=1, source_target_pairs={{0,8},{8,16},{16,24},{24,0},{1,9},{9,17},{17,25},{25,1},{2,10},{10... | collective-permute-start | bytes 983048 | tf_op jit(solution)/shard_map/ppermute | solution.py:323
  120.3 15.5 %collective-permute-start.17 = (bf16[4,2,40,640]{3,2,1,0:T(8,128)(2,1)S(1)}, bf16[4,2,40,640]{3,2,1,0:T(8,128)(2,1)S(1)}, u32[]{:S(2)}, u32[]{:S(2)}) collective-permute-start(bf16[4,2,40,640]{3,2,1,0:T(8,128)(2,1)S(1)} %dynamic-slice_bitcast_fusion.3), channel_id=1, source_target_pairs={{0,2},{1,3},{2,0},{3,1},{4,6},{5,7},{6,4},{7,5},{8,10},{9,11},{10,... | collective-permute-start | bytes 1228808 | tf_op jit(solution)/shard_map/ppermute | solution.py:447
  122.3 14.8 %collective-permute-start.20 = (bf16[4,2,40,640]{3,2,0,1:T(8,128)(2,1)S(1)}, bf16[4,2,40,640]{3,2,0,1:T(8,128)(2,1)S(1)}, u32[]{:S(2)}, u32[]{:S(2)}) collective-permute-start(bf16[4,2,40,640]{3,2,0,1:T(8,128)(2,1)S(1)} %dynamic-slice_bitcast_fusion.2), channel_id=1, source_target_pairs={{0,4},{1,5},{2,6},{3,7},{4,0},{5,1},{6,2},{7,3},{8,12},{9,13},{10,... | collective-permute-start | bytes 1228808 | tf_op jit(solution)/shard_map/ppermute | solution.py:447
  123.9 28.0 %collective-permute-start.15 = (bf16[256,640]{1,0:T(8,128)(2,1)S(1)}, bf16[256,640]{1,0:T(8,128)(2,1)S(1)}, u32[]{:S(2)}, u32[]{:S(2)}) collective-permute-start(bf16[256,640]{1,0:T(8,128)(2,1)S(1)} %get-tuple-element.84), channel_id=1, source_target_pairs={{0,24},{8,0},{16,8},{24,16},{1,25},{9,1},{17,9},{25,17},{2,26},{10... | collective-permute-start | bytes 983048 | tf_op jit(solution)/shard_map/ppermute | solution.py:323
  135.9 27.3 %collective-permute-start.16 = (bf16[256,640]{1,0:T(8,128)(2,1)S(1)}, bf16[256,640]{1,0:T(8,128)(2,1)S(1)}, u32[]{:S(2)}, u32[]{:S(2)}) collective-permute-start(bf16[256,640]{1,0:T(8,128)(2,1)S(1)} %get-tuple-element.85), channel_id=1, source_target_pairs={{0,8},{8,16},{16,24},{24,0},{1,9},{9,17},{17,25},{25,1},{2,10},{10... | collective-permute-start | bytes 983048 | tf_op jit(solution)/shard_map/ppermute | solution.py:323
  149.1 21.7 %collective-permute-start.22 = (bf16[40,1280]{1,0:T(8,128)(2,1)S(1)}, bf16[40,1280]{1,0:T(8,128)(2,1)S(1)}, u32[]{:S(2)}, u32[]{:S(2)}) collective-permute-start(bf16[40,1280]{1,0:T(8,128)(2,1)S(1)} %get-tuple-element.93), channel_id=1, source_target_pairs={{0,8},{8,0},{16,24},{24,16},{1,9},{9,1},{17,25},{25,17},{2,10},{10... | collective-permute-start | bytes 307208 | tf_op jit(solution)/shard_map/ppermute | solution.py:458
  152.0 18.8 %collective-permute-start.23 = (bf16[40,1280]{1,0:T(8,128)(2,1)S(1)}, bf16[40,1280]{1,0:T(8,128)(2,1)S(1)}, u32[]{:S(2)}, u32[]{:S(2)}) collective-permute-start(bf16[40,1280]{1,0:T(8,128)(2,1)S(1)} %get-tuple-element.94), channel_id=1, source_target_pairs={{0,16},{8,24},{16,0},{24,8},{1,17},{9,25},{17,1},{25,9},{2,18},{10... | collective-permute-start | bytes 307208 | tf_op jit(solution)/shard_map/ppermute | solution.py:458
  (30 other events, 160.7 us)
